TPU v7x, 32 devices: a whole 2x2x4 slice. The times are simulated.
32 devices in a mesh: dp: 4 (over y, x), shard: 8 (over z, core).
Axes of the slice: x: 2, y: 2, z: 4, core: 2. Of those that a mesh axis runs over, the one named last changes fastest.
Arguments:
- layer_input: bfloat16 [384, 46240], P('shard', 'dp'), may hold values from -6 to 6
- cotangent: bfloat16 [32768, 512], P('dp'), may hold values from -0.032958984 to 0.032958984
- momentum: float32 [10368, 512], P('shard'), may hold values from -6 to 6
Outputs:
- momentum_new: float32 [10368, 512], P('shard')
- direction: float32 [10368, 512], P('shard')
All inputs are finite; a program needn't handle non-finite values.
Results may differ from a plain program's by a relative error of at most 0.0003.
Values sent between devices are 32-bit elements; how exact they have to be, the bound alone decides.
No kernel may reach another device: no remote copies, remote signals or barrier semaphores. Data moves between devices by JAX's collectives and lax.ppermute only.
A program may use at most 320 MiB of HBM per device.

v0:
```python
import jax
import jax.numpy as jnp
from jax import lax
from jax.sharding import PartitionSpec as P

HW = 32
ITERS = 2
ROWS = 10368


HIGH = lax.Precision.HIGHEST


def gram_sum(block):
    local = lax.dot_general(block, block, (((0,), (0,)), ((), ())), precision=HIGH)
    return lax.psum(local, "shard")


def body(layer_input, cotangent, momentum):
    chans = layer_input.shape[0]
    voxels = cotangent.shape[0]
    depth = voxels // (HW * HW)
    volume = layer_input.reshape(chans, depth + 2, HW + 2, HW + 2)
    slabs = []
    for kd in range(3):
        for kh in range(3):
            for kw in range(3):
                slabs.append(volume[:, kd : kd + depth, kh : kh + HW, kw : kw + HW])
    patches = jnp.stack(slabs, axis=1).reshape(chans * 27, voxels)
    partial_grad = jnp.dot(patches, cotangent, preferred_element_type=jnp.float32)
    grad = lax.psum(partial_grad, "dp")
    momentum_new = 0.95 * momentum + grad
    squared = lax.psum(jnp.sum(momentum_new * momentum_new), "shard")
    iterate = momentum_new / (jnp.sqrt(squared) + 1e-07)
    gram = gram_sum(iterate)
    for step in range(ITERS):
        if step > 0:
            gram = gram_sum(iterate)
        poly = -4.775 * gram + 2.0315 * jnp.dot(gram, gram, precision=HIGH)
        iterate = 3.4445 * iterate + jnp.dot(iterate, poly, precision=HIGH)
    direction = iterate * jnp.sqrt(jnp.float32(ROWS))
    return (momentum_new, direction)


def solution(mesh):
    return jax.shard_map(
        body,
        mesh=mesh,
        in_specs=(P("shard", "dp"), P("dp", None), P("shard", None)),
        out_specs=(P("shard", None), P("shard", None)),
        check_vma=False,
    )
```

profile of v0, /device:TPU:0, one launch (start us, length us, event | category | flops | bytes accessed | tf_op | source)
XLA Modules:
  0.0 548.9 jit_solution(15928005073139925350)
XLA Ops:
  7.2 0.0 all-reduce.4.cloned.1.call-start
  7.2 8.6 %reshape.10 = bf16[48,10,34,34]{3,2,1,0:T(8,128)(2,1)} reshape(bf16[48,11560]{1,0:T(8,128)(2,1)} %param.3) | data formatting | bytes 2219520 | tf_op jit(solution)/shard_map/reshape | solution.py:23
  15.8 0.0 copy-start
  15.8 4.7 fusion.27
  20.5 0.0 copy-done
  20.5 2.6 fusion.26
  23.1 2.6 fusion.25
  25.7 3.5 fusion.24
  29.2 3.9 fusion.23
  33.1 3.9 fusion.22
  37.0 3.5 fusion.21
  40.5 4.1 fusion.20
  44.6 4.0 fusion.19
  48.6 2.6 fusion.18
  51.2 2.5 fusion.17
  53.7 2.6 fusion.16
  56.4 3.5 fusion.15
  59.9 3.9 fusion.14
  63.8 4.4 fusion.13
  68.1 3.5 fusion.12
  71.6 3.8 fusion.11
  75.5 3.9 fusion.10
  79.3 2.6 fusion.9
  81.9 2.5 fusion.8
  84.4 2.6 fusion.7
  86.9 3.5 fusion.6
  90.5 4.1 fusion.5
  94.6 3.8 fusion.4
  98.4 3.5 fusion.3
  101.9 4.0 fusion.2
  106.0 3.9 fusion.1
  109.8 56.4 %copy.5 = bf16[48,27,8,32,32]{4,3,2,1,0:T(8,128)(2,1)} copy(bf16[48,27,8,32,32]{4,3,2,0,1:T(8,128)(2,1)} %fusion.1) | data formatting | bytes 42467328 | tf_op jit(solution)/shard_map/stack | solution.py:29
  166.2 102.6 %reshape.11 = bf16[1296,8192]{1,0:T(8,128)(2,1)} reshape(bf16[48,27,8,32,32]{4,3,2,1,0:T(8,128)(2,1)} %copy.5) | data formatting | bytes 42467328 | tf_op jit(solution)/shard_map/reshape | solution.py:29
  268.8 0.0 copy-start.1
  268.8 19.1 %fusion.31 = f32[1296,512]{1,0:T(8,128)} fusion(bf16[1296,8192]{1,0:T(8,128)(2,1)} %reshape.11, bf16[8192,512]{1,0:T(8,128)(2,1)} %param.4), kind=kOutput, calls=%fused_computation.65 | convolution fusion | flops 10871635968 | bytes 32276480 | tf_op jit(solution)/shard_map/dot_general | solution.py:30
  287.9 0.0 all-reduce.4.cloned.1.call-update
  287.9 0.0 all-reduce.6.cloned.1.call-start
  288.0 81.9 %all-reduce.4.cloned.1.call-done = f32[1296,512]{1,0:T(8,128)} async-done(((f32[1296,512]{1,0:T(8,128)}), f32[1296,512]{1,0:T(8,128)}) %all-reduce.4.cloned.1.call-update) | async-done | bytes 2654224 | tf_op jit(solution)/shard_map/psum | solution.py:31
  369.9 0.0 copy-done.1
  369.9 4.5 multiply_reduce_fusion
  374.4 17.0 %psum.29 = f32[]{:T(128)} all-reduce(f32[]{:T(128)} %get-tuple-element.2), channel_id=1, replica_groups=mesh['dp'=4,'shard'=8] {'shard'}, use_global_device_ids=true, to_apply=%region_2.0 | all-reduce | flops 1 | bytes 8 | tf_op jit(solution)/shard_map/psum | solution.py:33
  392.0 8.8 %fusion.30 = f32[512,512]{1,0:T(8,128)} fusion(f32[1296,512]{1,0:T(8,128)} %get-tuple-element.3, f32[]{:T(128)S(6)} %add.27), kind=kOutput, calls=%fused_computation.64 | convolution fusion | flops 4077527040 | bytes 3702788 | tf_op jit(solution)/shard_map/dot_general | solution.py:15
  400.8 0.0 all-reduce.6.cloned.1.call-update
  400.8 0.4 all-reduce.8.cloned.1.call-start
  401.3 55.8 %all-reduce.6.cloned.1.call-done = f32[512,512]{1,0:T(8,128)} async-done(((f32[512,512]{1,0:T(8,128)}), f32[512,512]{1,0:T(8,128)}) %all-reduce.6.cloned.1.call-update) | async-done | bytes 1048592 | tf_op jit(solution)/shard_map/psum | solution.py:16
  457.1 3.9 fusion.29
  461.0 6.9 %convolution_add_fusion.1 = f32[1296,512]{1,0:T(8,128)S(1)} fusion(f32[512,512]{1,0:T(8,128)S(1)} %fusion.29, f32[1296,512]{1,0:T(8,128)} %get-tuple-element.3, f32[]{:T(128)S(6)} %add.27), kind=kOutput, calls=%fused_computation.1 | convolution fusion | flops 4079517696 | bytes 6356996 | tf_op jit(solution)/shard_map/dot_general | solution.py:40
  467.9 6.1 %fusion.32 = f32[512,512]{1,0:T(8,128)} fusion(f32[1296,512]{1,0:T(8,128)S(1)} %convolution_add_fusion.1), kind=kOutput, calls=%fused_computation.66 | convolution fusion | flops 4076863488 | bytes 3702784 | tf_op jit(solution)/shard_map/dot_general | solution.py:15
  474.0 0.0 all-reduce.8.cloned.1.call-update
  474.1 57.9 %all-reduce.8.cloned.1.call-done = f32[512,512]{1,0:T(8,128)} async-done(((f32[512,512]{1,0:T(8,128)}), f32[512,512]{1,0:T(8,128)}) %all-reduce.8.cloned.1.call-update) | async-done | bytes 1048592 | tf_op jit(solution)/shard_map/psum | solution.py:16
  532.0 4.1 fusion.28
  536.1 6.1 %fusion = f32[1296,512]{1,0:T(8,128)} fusion(f32[1296,512]{1,0:T(8,128)S(1)} %convolution_add_fusion.1, f32[512,512]{1,0:T(8,128)S(1)} %fusion.28), kind=kOutput, calls=%fused_computation.2 | convolution fusion | flops 4078854144 | bytes 6356992 | tf_op jit(solution)/shard_map/dot_general | solution.py:40
Async XLA Ops:
  7.2 362.7 %all-reduce.4.cloned.1.call-start = ((), (), s32[]{:S(2)}) async-start(), calls=%async_computation | async-start | bytes 5308416 | tf_op jit(solution)/shard_map/psum | solution.py:31
  15.8 4.7 copy-start
  268.8 101.1 %copy-start.1 = (f32[1296,512]{1,0:T(8,128)S(1)}, f32[1296,512]{1,0:T(8,128)}, u32[]{:S(2)}) copy-start(f32[1296,512]{1,0:T(8,128)} %param.5) | copy-start | bytes 7962628
  287.9 169.1 %all-reduce.6.cloned.1.call-start = ((), (), s32[]{:S(2)}) async-start(), calls=%async_computation.1 | async-start | bytes 2097152 | tf_op jit(solution)/shard_map/psum | solution.py:16
  400.8 131.2 %all-reduce.8.cloned.1.call-start = ((), (), s32[]{:S(2)}) async-start(), calls=%async_computation.2 | async-start | bytes 2097152 | tf_op jit(solution)/shard_map/psum | solution.py:16
Sparse Core Ops, SparseCore 0:
  288.1 81.7 all-reduce.3
  400.9 56.0 all-reduce.5
  474.2 57.7 all-reduce.7
where the time goes:
time: 554 us; the launch traced here: 549 us
  local copies, waits for them, and re-layouts  262 us (47%)
  waiting for transfers between devices  196 us (35%)
  matrix products  55 us (10%)
  blocking collectives  17 us (3%)
  between operations  14.7 us (3%)
    psum x2, waiting for transfers between devices, gram_sum(): return lax.psum(local, 'shard')  114 us
    reshape x1, local copies, waits for them, and re-layouts, body(): patches = jnp.stack(slabs, axis=1).reshape(chans * 27, voxels)  103 us
    unnamed x30, local copies, waits for them, and re-layouts  90.2 us
    psum x1, waiting for transfers between devices, body(): grad = lax.psum(partial_grad, 'dp')  81.9 us
    another operation x2, local copies, waits for them, and re-layouts, body(): patches = jnp.stack(slabs, axis=1).reshape(chans * 27, voxels)  60.2 us
    dot_general x1, matrix products, body(): jnp.dot(patches, cotangent, preferred_element_type=jnp.float32)  19.1 us
    psum x1, blocking collectives, body(): squared = lax.psum(jnp.sum(momentum_new * momentum_new), 'shard')  17 us
    dot_general x2, matrix products, gram_sum(): lax.dot_general(block, block, (((0,), (0,)), ((), ())), precision=HIGH)  14.9 us
  transfers between devices with their start and end apart: 3, of which 3 were waited for; matrix products, arithmetic and copies ran while one was open for 0% of the time, Pallas kernels for 0%

commit v1 on v0

v1 whole, which is shorter than its diff:
```python
import functools

import jax
import jax.numpy as jnp
from jax import lax
from jax.experimental import pallas as pl
from jax.experimental.pallas import tpu as pltpu
from jax.sharding import PartitionSpec as P

HW = 32
ROWS = 10368
PW = HW + 2
LANE = 128
TAPS = 27
A1, B1, C1 = 3.4445, -4.775, 2.0315
F32 = jnp.float32
BF16 = jnp.bfloat16
VMEM = pl.BlockSpec(memory_space=pltpu.VMEM)
HBM = pl.BlockSpec(memory_space=pl.ANY)
SMEM = pl.BlockSpec(memory_space=pltpu.SMEM)
BLOCKS = (((0, 0), (0, 1), (0, 2), (0, 3), (1, 1)), ((1, 2), (1, 3), (2, 2), (2, 3), (3, 3)))


def column(rows):
    return pl.BlockSpec((rows, LANE), lambda c: (0, c))


def params():
    return pltpu.CompilerParams(vmem_limit_bytes=56 << 20)


def pair(tile, p, lane):
    t, c = divmod(p, LANE)
    if c + 64 <= LANE:
        return jnp.where(lane < c + 32, tile(t), tile(t + 4))
    if c + 32 <= LANE:
        far = jnp.where(lane < c, tile(t + 5), tile(t))
        if c + 32 == LANE:
            return far
        return jnp.where(lane < c + 32, far, tile(t + 4))
    near = jnp.where(lane < c + 32 - LANE, tile(t + 1), tile(t + 5))
    return jnp.where(lane < c, near, tile(t))


def build_slab(d0, half, xs, tail, v, cp):
    lane = lax.broadcasted_iota(jnp.int32, (16, LANE), 1)
    last = xs.shape[1] // LANE
    for g in range(cp // 16):
        rows = slice(16 * g, 16 * g + 16)

        def tile(t):
            return tail[rows, :] if t == last else xs[rows, LANE * t : LANE * t + LANE]

        for j in range(18):
            for kw in range(3):
                part = []
                for s1 in range(2):
                    p = (d0 + half * s1) * PW * PW + PW * j + kw
                    part.append(pltpu.roll(pair(tile, p, lane), (64 * s1 - p) % LANE, 1))
                r0 = (d0 * 3 + kw) * cp + 16 * g
                v[r0 : r0 + 16, LANE * j : LANE * j + LANE] = jnp.where(lane < 64, part[0], part[1])


def conv_kernel(depth, cp, taps, slots, q_ref, x_hbm, cot_hbm, *refs):
    outs = refs[:2]
    xs, tail, cot, v, xsem, csem = refs[2:]
    half = depth // 2
    ln = xs.shape[1]
    vox = HW * HW
    xcopy = pltpu.make_async_copy(x_hbm, xs, xsem)
    xcopy.start()
    copies = []
    for i in range(depth):
        rows = pl.ds(i * vox, vox)
        copies.append(pltpu.make_async_copy(cot_hbm.at[rows], cot.at[rows], csem.at[i]))
    for d in range(half):
        for s1 in range(2):
            copies[d + half * s1].start()
    xcopy.wait()
    n = ln // LANE * LANE
    if n < ln:
        tail[:, : ln - n] = xs[:, n:]
    for d0 in range(half + 2):
        build_slab(d0, half, xs, tail, v, cp)
    for d in range(half):
        for s1 in range(2):
            copies[d + half * s1].wait()
        for c in range(2):
            lhs = []
            for s in range(slots):
                for i in range(taps):
                    t = jnp.minimum(q_ref[slots * c + s] * taps + i, TAPS - 1)
                    kd, kh, kw = t // 9, t // 3 % 3, t % 3
                    r0 = pl.multiple_of(((d + kd) * 3 + kw) * cp, 16)
                    lhs.append(v[pl.ds(r0, cp), pl.ds(pl.multiple_of(LANE * kh, LANE), 16 * LANE)])
            rhs = []
            for h in range(16):
                for s1 in range(2):
                    for s0 in range(2):
                        r0 = (d + half * s1) * vox + (h + 16 * s0) * HW
                        rhs.append(cot[r0 : r0 + HW, 256 * c : 256 * c + 256])
            part = jnp.dot(jnp.concatenate(lhs, 0), jnp.concatenate(rhs, 0), preferred_element_type=F32)
            if d == 0:
                outs[c][...] = part
            else:
                outs[c][...] += part


def conv(x, cot, q, taps, slots):
    cp, ln = x.shape
    depth = cot.shape[0] // (HW * HW)
    return pl.pallas_call(
        functools.partial(conv_kernel, depth, cp, taps, slots),
        out_shape=[jax.ShapeDtypeStruct((slots * taps * cp, 256), F32)] * 2,
        in_specs=[SMEM, HBM, HBM],
        out_specs=[VMEM] * 2,
        scratch_shapes=[
            pltpu.VMEM((cp, ln), BF16),
            pltpu.VMEM((cp, LANE), BF16),
            pltpu.VMEM(cot.shape, BF16),
            pltpu.VMEM((3 * (depth // 2 + 2) * cp, 18 * LANE), BF16),
            pltpu.SemaphoreType.DMA,
            pltpu.SemaphoreType.DMA((depth,)),
        ],
        compiler_params=params(),
        name="conv_wgrad",
    )(q, x, cot)


def own_kernel(taps, cp, dp_ref, m_ref, o_ref):
    chans = m_ref.shape[0] // TAPS
    for i in range(taps):
        t = dp_ref[0] * taps + i
        rows = m_ref[pl.ds(jnp.minimum(t, TAPS - 1), chans, stride=TAPS), :]
        o_ref[cp * i : cp * i + chans, :] = jnp.where(t < TAPS, rows, 0.0)
        if cp > chans:
            o_ref[cp * i + chans : cp * i + cp, :] = jnp.zeros((cp - chans, LANE), F32)


def own_momentum(momentum, dp, taps, cp):
    return pl.pallas_call(
        functools.partial(own_kernel, taps, cp),
        out_shape=jax.ShapeDtypeStruct((taps * cp, momentum.shape[1]), F32),
        grid=(momentum.shape[1] // LANE,),
        in_specs=[SMEM, column(momentum.shape[0])],
        out_specs=column(taps * cp),
        compiler_params=params(),
        name="own_momentum",
    )(dp, momentum)


def split(x):
    hi = x.astype(BF16)
    return hi, (x - hi.astype(F32)).astype(BF16)


def dot_t(a, b):
    return lax.dot_general(a, b, (((0,), (0,)), ((), ())), preferred_element_type=F32)


def update(m_ref, grad, dp, taps, cp):
    rows = taps * cp
    tap = dp * taps + lax.broadcasted_iota(jnp.int32, (rows, 1), 0) // cp
    return jnp.where(tap < TAPS, 0.95 * m_ref[...] + grad, 0.0)


def upper_gram(m):
    hi, lo = split(m)
    out = []
    for i in range(4):
        a, b = slice(128 * i, 128 * i + 128), slice(128 * i, 512)
        out.append(dot_t(hi[:, a], hi[:, b]) + (dot_t(hi[:, a], lo[:, b]) + dot_t(lo[:, a], hi[:, b])))
    return out


def step_kernel(taps, cp, dp_ref, m_ref, a0, ra, a2, b0, rb, b2, o_ref, keep, send):
    rows = taps * cp
    dp, core = dp_ref[0], dp_ref[1]
    ga = a0[:rows] + ra[:rows] + a2[...]
    gb = b0[:rows] + rb[:rows] + b2[...]
    m = update(m_ref, jnp.concatenate([ga, gb], 1), dp, taps, cp)
    o_ref[...] = m
    gram = upper_gram(m)
    for half in range(2):
        mine = core == half
        for n, (i, j) in enumerate(BLOCKS[half]):
            block = gram[i][:, 128 * (j - i) : 128 * (j - i) + 128]
            for r in range(4):
                piece = block[32 * r : 32 * r + 32]

                @pl.when(mine)
                def _():
                    keep[r ^ dp, n] = piece

                @pl.when(jnp.logical_not(mine))
                def _():
                    send[r ^ dp, n] = piece


def step(dp, own, pieces, taps, cp):
    g = jax.ShapeDtypeStruct((4, 5, 32, 128), F32)
    return pl.pallas_call(
        functools.partial(step_kernel, taps, cp),
        out_shape=[jax.ShapeDtypeStruct(own.shape, F32), g, g],
        in_specs=[SMEM] + [VMEM] * 7,
        out_specs=[VMEM] * 3,
        compiler_params=params(),
        name="momentum_gram",
    )(dp, own, *pieces)


def any_step_kernel(taps, cp, dp_ref, m_ref, grad, o_ref, g_ref):
    m = update(m_ref, grad[...], dp_ref[0], taps, cp)
    o_ref[...] = m
    for i, rows in enumerate(upper_gram(m)):
        g_ref[128 * i : 128 * i + 128, :] = jnp.zeros((128, 512), F32)
        g_ref[128 * i : 128 * i + 128, 128 * i :] = rows


def any_step(dp, own, grad, taps, cp):
    return pl.pallas_call(
        functools.partial(any_step_kernel, taps, cp),
        out_shape=[jax.ShapeDtypeStruct(own.shape, F32), jax.ShapeDtypeStruct((512, 512), F32)],
        in_specs=[SMEM, VMEM, VMEM],
        out_specs=[VMEM] * 2,
        compiler_params=params(),
        name="momentum_gram",
    )(dp, own, grad)


def order_kernel(taps, cp, chans, dp_ref, *refs):
    o_ref = refs[-1]
    for r, ref in enumerate(refs[:-1]):
        for i in range(ref.shape[0] // cp):
            t = (dp_ref[0] ^ r) * taps + i if len(refs) > 2 else i
            if len(refs) == 2 and i >= TAPS:
                continue

            @pl.when(t < TAPS)
            def _():
                o_ref[pl.ds(t, chans, stride=TAPS), :] = ref[cp * i : cp * i + chans, :]


def order(dp, parts, taps, cp, chans):
    return pl.pallas_call(
        functools.partial(order_kernel, taps, cp, chans),
        out_shape=jax.ShapeDtypeStruct((chans * TAPS, parts[0].shape[1]), F32),
        grid=(parts[0].shape[1] // LANE,),
        in_specs=[SMEM] + [column(part.shape[0]) for part in parts],
        out_specs=column(chans * TAPS),
        compiler_params=params(),
        name="weight_order",
    )(dp, *parts)


def mm(a, b):
    ah, al = a
    bh, bl = b
    d = functools.partial(jnp.dot, preferred_element_type=F32)
    return d(ah, bh) + (d(ah, bl) + d(al, bh))


def apply_kernel(dp_ref, m_ref, *refs):
    parts, (o_ref, g_ref) = refs[:-2], refs[-2:]
    if len(parts) == 1:
        g_ref[...] = parts[0][...]
    else:
        dp, core = dp_ref[0], dp_ref[1]
        for n, part in enumerate(parts):
            which, r = divmod(n, 4)
            q = dp ^ r
            for half in range(2):

                @pl.when(core ^ which == half)
                def _():
                    for k, (i, j) in enumerate(BLOCKS[half]):
                        rows = pl.ds(pl.multiple_of(128 * i + 32 * q, 32), 32)
                        g_ref[rows, 128 * j : 128 * j + 128] = part[k]

    for i in range(4):
        for j in range(i + 1, 4):
            g_ref[128 * j : 128 * j + 128, 128 * i : 128 * i + 128] = g_ref[
                128 * i : 128 * i + 128, 128 * j : 128 * j + 128
            ].T
    gram = g_ref[...]
    n = gram.shape[0]
    diag = lax.broadcasted_iota(jnp.int32, (n, n), 0) == lax.broadcasted_iota(jnp.int32, (n, n), 1)
    trace = jnp.sum(jnp.where(diag, gram, 0.0), keepdims=True)
    scale = 1.0 / (jnp.sqrt(trace) + 1e-07)
    g = gram * scale * scale
    gs = split(g)
    p1 = jnp.where(diag, A1, 0.0) + B1 * g + C1 * mm(gs, gs)
    p1s = split(p1)
    g2 = mm(split(mm(gs, p1s)), p1s)
    g2s = split(g2)
    p2 = jnp.where(diag, A1, 0.0) + B1 * g2 + C1 * mm(g2s, g2s)
    qs = split(mm(p1s, split(p2)) * (scale * jnp.sqrt(F32(ROWS))))
    o_ref[...] = mm(split(m_ref[...]), qs)


def apply(dp, momentum_new, parts):
    return pl.pallas_call(
        apply_kernel,
        out_shape=jax.ShapeDtypeStruct(momentum_new.shape, F32),
        in_specs=[SMEM] + [VMEM] * (1 + len(parts)),
        out_specs=VMEM,
        scratch_shapes=[pltpu.VMEM((512, 512), F32)],
        compiler_params=params(),
        name="newton_schulz",
    )(dp, momentum_new, *parts)


def swap(x, axis, size, bit):
    return lax.ppermute(x, axis, [(i, i ^ bit) for i in range(size)])


def body_4x8(layer_input, cotangent, momentum):
    chans = momentum.shape[0] // TAPS
    cp = layer_input.shape[0]
    taps = 7
    dp = lax.axis_index("dp")
    ids = jnp.stack([dp, lax.axis_index("shard") % 2]).astype(jnp.int32)
    first = jnp.stack([dp ^ 1, dp ^ 3, dp ^ 2, dp ^ 3]).astype(jnp.int32)
    second = jnp.stack([dp, dp ^ 2, dp, dp ^ 1]).astype(jnp.int32)
    rows = taps * cp
    sa, sb = conv(layer_input, cotangent, first, taps, 2)
    ra = swap(sa, "dp", 4, 1)
    rb = swap(sb, "dp", 4, 2)
    ka, kb = conv(layer_input, cotangent, second, taps, 2)
    own = own_momentum(momentum, ids, taps, cp)
    a2 = swap(ra[rows:] + ka[rows:], "dp", 4, 2)
    b2 = swap(rb[rows:] + kb[rows:], "dp", 4, 1)
    mine, keep, send = step(ids, own, (ka, ra, a2, kb, rb, b2), taps, cp)
    got = swap(send, "shard", 8, 1)
    others = [swap(mine, "dp", 4, r) for r in (1, 2, 3)]
    g = keep + got
    g = g[0] + swap(g[1], "dp", 4, 1) + swap(g[2], "dp", 4, 2) + swap(g[3], "dp", 4, 3)
    g = g + swap(g, "shard", 8, 2) + swap(g, "shard", 8, 4) + swap(g, "shard", 8, 6)
    g = [g] + [swap(g, "dp", 4, r) for r in (1, 2, 3)]
    g = g + [swap(x, "shard", 8, 1) for x in g]
    momentum_new = order(ids, [mine] + others, taps, cp, chans)
    return momentum_new, apply(ids, momentum_new, g)


def body_any(n_dp, layer_input, cotangent, momentum):
    chans = layer_input.shape[0]
    cp = -(-chans // 16) * 16
    taps = -(-TAPS // n_dp)
    x = jnp.pad(layer_input, ((0, cp - chans), (0, 0)))
    ids = jnp.stack([lax.axis_index("dp"), lax.axis_index("shard")]).astype(jnp.int32)
    q = jnp.tile(jnp.arange(n_dp, dtype=jnp.int32), 2)
    part = jnp.concatenate(conv(x, cotangent, q, taps, n_dp), 1)
    grad = lax.psum_scatter(part, "dp", scatter_dimension=0, tiled=True)
    mine, gram = any_step(ids, own_momentum(momentum, ids, taps, cp), grad, taps, cp)
    gram = lax.psum(gram, ("dp", "shard"))
    momentum_new = order(ids, [lax.all_gather(mine, "dp", axis=0, tiled=True)], taps, cp, chans)
    return momentum_new, apply(ids, momentum_new, [gram])


def solution(mesh):
    n_dp = mesh.shape["dp"]
    known = (n_dp, mesh.shape["shard"]) == (4, 8)
    return jax.shard_map(
        body_4x8 if known else functools.partial(body_any, n_dp),
        mesh=mesh,
        in_specs=(P("shard", "dp"), P("dp", None), P("shard", None)),
        out_specs=(P("shard", None), P("shard", None)),
        check_vma=False,
    )
```

time: 554 us -> 121 us (0.22)
  local copies, waits for them, and re-layouts: 262 us -> 3.67 us
  waiting for transfers between devices: 196 us -> 35.8 us
  matrix products: 55 us -> 0 us
  Pallas kernels: 0 us -> 52.1 us
  starting transfers between devices: 0.53 us -> 23 us
  blocking collectives: 17 us -> 0 us
  between operations: 14.7 us -> 0.82 us
    psum x3 -> x0, waiting for transfers between devices: 196 us -> none  [the longest x2 114 us: gram_sum(): return lax.psum(local, 'shard')]
    reshape x2 -> x0, local copies, waits for them, and re-layouts: 111 us -> none  [the longest x1 103 us: body(): patches = jnp.stack(slabs, axis=1).reshape(chans * 27, voxels)]
    unnamed x30, local copies, waits for them, and re-layouts: 90.2 us -> 3.65 us
    another operation x2 -> x0, local copies, waits for them, and re-layouts: 60.2 us -> none  [body(): patches = jnp.stack(slabs, axis=1).reshape(chans * 27, voxels)]
    dot_general x7 -> x0, matrix products: 55 us -> none  [the longest x1 19.1 us: body(): jnp.dot(patches, cotangent, preferred_element_type=jnp.float32)]
    pallas_call x0 -> x6, Pallas kernels: none -> 52.1 us  [the longest x2 29 us: conv(): pl.pallas_call(functools.partial(conv_kernel, depth, cp, taps, slots), ou...]
    ppermute x0 -> x21, waiting for transfers between devices: none -> 35.8 us  [swap(): return lax.ppermute(x, axis, [(i, i ^ bit) for i in range(size)])]
    ppermute x0 -> x21, starting transfers between devices: none -> 23 us  [swap(): return lax.ppermute(x, axis, [(i, i ^ bit) for i in range(size)])]
  transfers between devices with their start and end apart: 3 -> 21, of which waited for: 3 -> 11; matrix products, arithmetic and copies ran while one was open for 0% -> 3% of each run, Pallas kernels for 0% -> 19%
where the time goes in v1:
time: 121 us; the launch traced here: 120 us
  Pallas kernels  52.1 us (43%)
  waiting for transfers between devices  35.8 us (30%)
  starting transfers between devices  23 us (19%)
  other arithmetic  4.76 us (4%)
  local copies, waits for them, and re-layouts  3.67 us (3%)
    ppermute x21, waiting for transfers between devices, swap(): return lax.ppermute(x, axis, [(i, i ^ bit) for i in range(size)])  35.8 us
    pallas_call x2, Pallas kernels, conv(): pl.pallas_call(functools.partial(conv_kernel, depth, cp, taps, slots), ou...  29 us
    ppermute x21, starting transfers between devices, swap(): return lax.ppermute(x, axis, [(i, i ^ bit) for i in range(size)])  23 us
    pallas_call x1, Pallas kernels, apply(): pl.pallas_call(apply_kernel, out_shape=jax.ShapeDtypeStruct(momentum_new....  10.6 us
    pallas_call x1, Pallas kernels, order(): pl.pallas_call(functools.partial(order_kernel, taps, cp, chans), out_shap...  4.53 us
    pallas_call x1, Pallas kernels, step(): pl.pallas_call(functools.partial(step_kernel, taps, cp), out_shape=[jax.S...  4.44 us
    unnamed x30, local copies, waits for them, and re-layouts  3.65 us
    pallas_call x1, Pallas kernels, own_momentum(): pl.pallas_call(functools.partial(own_kernel, taps, cp), out_shape=jax.Sha...  3.64 us
  transfers between devices with their start and end apart: 21, of which 11 were waited for; matrix products, arithmetic and copies ran while one was open for 3% of the time, Pallas kernels for 19%

profile of v1, /device:TPU:0, one launch (start us, length us, event | category | flops | bytes accessed | tf_op | source)
XLA Modules:
  0.0 120.2 jit_solution(11613071344096650412)
XLA Ops:
  0.6 0.6 pad_add_fusion.1
  1.2 14.4 %conv_wgrad.3 = (f32[672,256]{1,0:T(8,128)}, f32[672,256]{1,0:T(8,128)}) custom-call(s32[4]{0:T(128)} %get-tuple-element.20.q_ref, bf16[48,11560]{1,0:T(8,128)(2,1)} %x_hbm.3, bf16[8192,512]{1,0:T(8,128)(2,1)} %cot_hbm.3), custom_call_target="tpu_custom_call" | custom-call | tf_op jit(solution)/shard_map/conv_wgrad/pallas_call | solution.py:112
  15.6 3.0 %collective-permute-start = (f32[672,256]{1,0:T(8,128)}, f32[672,256]{1,0:T(8,128)S(1)}, u32[]{:S(2)}, u32[]{:S(2)}) collective-permute-start(f32[672,256]{1,0:T(8,128)} %get-tuple-element.10), channel_id=1, source_target_pairs={{0,8},{8,0},{16,24},{24,16},{1,9},{9,1},{17,25},{25,17},{2,10},{10... | collective-permute-start | bytes 2064392 | tf_op jit(solution)/shard_map/ppermute | solution.py:314
  18.6 1.5 %collective-permute-start.2 = (f32[672,256]{1,0:T(8,128)}, f32[672,256]{1,0:T(8,128)S(1)}, u32[]{:S(2)}, u32[]{:S(2)}) collective-permute-start(f32[672,256]{1,0:T(8,128)} %get-tuple-element.12), channel_id=1, source_target_pairs={{0,16},{8,24},{16,0},{24,8},{1,17},{9,25},{17,1},{25,9},{2,18},{10... | collective-permute-start | bytes 2064392 | tf_op jit(solution)/shard_map/ppermute | solution.py:314
  20.1 14.6 %conv_wgrad.2 = (f32[672,256]{1,0:T(8,128)}, f32[672,256]{1,0:T(8,128)}) custom-call(s32[4]{0:T(128)} %get-tuple-element.19.q_ref, bf16[48,11560]{1,0:T(8,128)(2,1)} %x_hbm.3, bf16[8192,512]{1,0:T(8,128)(2,1)} %cot_hbm.3), custom_call_target="tpu_custom_call" | custom-call | tf_op jit(solution)/shard_map/conv_wgrad/pallas_call | solution.py:112
  34.7 0.0 collective-permute-done.ra
  34.7 0.0 copy-start
  34.7 1.3 %slice_add_fusion.1 = f32[336,256]{1,0:T(8,128)S(1)} fusion(f32[672,256]{1,0:T(8,128)S(1)} %collective-permute-done.ra, f32[672,256]{1,0:T(8,128)} %get-tuple-element.9.a0), kind=kLoop, calls=%fused_computation.1 | loop fusion | flops 86016 | bytes 1032192 | tf_op jit(solution)/shard_map/add | solution.py:331
  36.0 1.3 %collective-permute-start.1 = (f32[336,256]{1,0:T(8,128)S(1)}, f32[336,256]{1,0:T(8,128)S(1)}, u32[]{:S(2)}, u32[]{:S(2)}) collective-permute-start(f32[336,256]{1,0:T(8,128)S(1)} %slice_add_fusion.1), channel_id=1, source_target_pairs={{0,16},{8,24},{16,0},{24,8},{1,17},{9,25},{17,1},{25,9},{2,18},{10... | collective-permute-start | bytes 1032200 | tf_op jit(solution)/shard_map/ppermute | solution.py:314
  37.3 0.0 collective-permute-done.2.rb
  37.3 1.2 %slice_add_fusion = f32[336,256]{1,0:T(8,128)S(1)} fusion(f32[672,256]{1,0:T(8,128)S(1)} %collective-permute-done.2.rb, f32[672,256]{1,0:T(8,128)} %get-tuple-element.11.b0), kind=kLoop, calls=%fused_computation | loop fusion | flops 86016 | bytes 1032192 | tf_op jit(solution)/shard_map/add | solution.py:332
  38.6 1.5 %collective-permute-start.3 = (f32[336,256]{1,0:T(8,128)S(1)}, f32[336,256]{1,0:T(8,128)S(1)}, u32[]{:S(2)}, u32[]{:S(2)}) collective-permute-start(f32[336,256]{1,0:T(8,128)S(1)} %slice_add_fusion), channel_id=1, source_target_pairs={{0,8},{8,0},{16,24},{24,16},{1,9},{9,1},{17,25},{25,17},{2,10},{10... | collective-permute-start | bytes 1032200 | tf_op jit(solution)/shard_map/ppermute | solution.py:314
  40.1 0.6 pad_add_fusion.dp_ref
  40.7 3.6 %own_momentum.1.m_ref = f32[336,512]{1,0:T(8,128)} custom-call(s32[2]{0:T(128)} %pad_add_fusion.dp_ref, f32[1296,512]{1,0:T(8,128)} %m_ref.1), custom_call_target="tpu_custom_call" | custom-call | tf_op jit(solution)/shard_map/own_momentum/pallas_call | solution.py:141
  44.3 0.0 copy-done
  44.3 1.0 collective-permute-done.1.a2
  45.3 2.0 %collective-permute-done.3.b2 = f32[336,256]{1,0:T(8,128)S(1)} collective-permute-done((f32[336,256]{1,0:T(8,128)S(1)}, f32[336,256]{1,0:T(8,128)S(1)}, u32[]{:S(2)}, u32[]{:S(2)}) %collective-permute-start.3) | collective-permute-done | bytes 344096 | tf_op jit(solution)/shard_map/ppermute | solution.py:314
  47.3 0.0 copy-done.1
  47.3 0.7 copy-done.6
  48.0 4.4 %momentum_gram.1 = (f32[336,512]{1,0:T(8,128)}, f32[4,5,32,128]{3,2,1,0:T(8,128)}, f32[4,5,32,128]{3,2,1,0:T(8,128)}) custom-call(s32[2]{0:T(128)} %pad_add_fusion.dp_ref, f32[336,512]{1,0:T(8,128)} %own_momentum.1.m_ref, f32[672,256]{1,0:T(8,128)} %get-tuple-element.9.a0, f32[672,256]{1,0:T(8,128)} %copy-done, f32[336,256]{1,0:T(8,128)} %copy-done.5, ...), custom_call_target="tpu_custom_call" | custom-call | tf_op jit(solution)/shard_map/momentum_gram/pallas_call | solution.py:202
  52.5 0.0 collective-permute-start.7
  52.5 1.8 %collective-permute-done.7 = f32[4,5,32,128]{3,2,1,0:T(8,128)S(1)} collective-permute-done((f32[4,5,32,128]{3,2,1,0:T(8,128)}, f32[4,5,32,128]{3,2,1,0:T(8,128)S(1)}, u32[]{:S(2)}, u32[]{:S(2)}) %collective-permute-start.7) | collective-permute-done | bytes 327712 | tf_op jit(solution)/shard_map/ppermute | solution.py:314
  54.3 1.0 add.34
  55.4 1.5 %collective-permute-start.8 = (f32[5,32,128]{2,1,0:T(8,128)S(1)}, f32[5,32,128]{2,1,0:T(8,128)S(1)}, u32[]{:S(2)}, u32[]{:S(2)}) collective-permute-start(f32[5,32,128]{2,1,0:T(8,128)S(1)} %get-tuple-element.16), channel_id=1, source_target_pairs={{0,8},{8,0},{16,24},{24,16},{1,9},{9,1},{17,25},{25,17},{2,10},{10... | collective-permute-start | bytes 245768 | tf_op jit(solution)/shard_map/ppermute | solution.py:314
  56.9 1.1 collective-permute-start.10
  58.0 1.0 collective-permute-start.9
  58.9 1.4 %collective-permute-start.6 = (f32[336,512]{1,0:T(8,128)}, f32[336,512]{1,0:T(8,128)S(1)}, u32[]{:S(2)}, u32[]{:S(2)}) collective-permute-start(f32[336,512]{1,0:T(8,128)} %get-tuple-element.13.refs_0_), channel_id=1, source_target_pairs={{0,24},{8,16},{16,8},{24,0},{1,25},{9,17},{17,9},{25,1},{2,26},{10... | collective-permute-start | bytes 2064392 | tf_op jit(solution)/shard_map/ppermute | solution.py:314
  60.4 1.5 %collective-permute-start.5 = (f32[336,512]{1,0:T(8,128)}, f32[336,512]{1,0:T(8,128)S(1)}, u32[]{:S(2)}, u32[]{:S(2)}) collective-permute-start(f32[336,512]{1,0:T(8,128)} %get-tuple-element.13.refs_0_), channel_id=1, source_target_pairs={{0,16},{8,24},{16,0},{24,8},{1,17},{9,25},{17,1},{25,9},{2,18},{10... | collective-permute-start | bytes 2064392 | tf_op jit(solution)/shard_map/ppermute | solution.py:314
  61.9 0.0 collective-permute-done.8
  61.9 0.6 collective-permute-start.4
  62.4 0.3 collective-permute-done.10
  62.7 16.1 %collective-permute-done.9 = f32[5,32,128]{2,1,0:T(8,128)S(1)} collective-permute-done((f32[5,32,128]{2,1,0:T(8,128)S(1)}, f32[5,32,128]{2,1,0:T(8,128)S(1)}, u32[]{:S(2)}, u32[]{:S(2)}) %collective-permute-start.9) | collective-permute-done | bytes 81952 | tf_op jit(solution)/shard_map/ppermute | solution.py:314
  78.8 3.7 %collective-permute-start.13 = (f32[5,32,128]{2,1,0:T(8,128)S(1)}, f32[5,32,128]{2,1,0:T(8,128)S(1)}, u32[]{:S(2)}, u32[]{:S(2)}) collective-permute-start(f32[5,32,128]{2,1,0:T(8,128)S(1)} %fusion.2), channel_id=1, source_target_pairs={{0,6},{1,7},{2,4},{3,5},{4,2},{5,3},{6,0},{7,1},{8,14},{9,15},{10,... | collective-permute-start | bytes 245768 | tf_op jit(solution)/shard_map/ppermute | solution.py:314
  82.5 0.0 collective-permute-start.12
  82.5 2.9 %collective-permute-done.13 = f32[5,32,128]{2,1,0:T(8,128)S(1)} collective-permute-done((f32[5,32,128]{2,1,0:T(8,128)S(1)}, f32[5,32,128]{2,1,0:T(8,128)S(1)}, u32[]{:S(2)}, u32[]{:S(2)}) %collective-permute-start.13) | collective-permute-done | bytes 81952 | tf_op jit(solution)/shard_map/ppermute | solution.py:314
  85.4 2.9 %collective-permute-start.11 = (f32[5,32,128]{2,1,0:T(8,128)S(1)}, f32[5,32,128]{2,1,0:T(8,128)S(1)}, u32[]{:S(2)}, u32[]{:S(2)}) collective-permute-start(f32[5,32,128]{2,1,0:T(8,128)S(1)} %fusion.2), channel_id=1, source_target_pairs={{0,2},{1,3},{2,0},{3,1},{4,6},{5,7},{6,4},{7,5},{8,10},{9,11},{10,... | collective-permute-start | bytes 245768 | tf_op jit(solution)/shard_map/ppermute | solution.py:314
  88.3 0.5 collective-permute-done.12
  88.8 2.0 %collective-permute-done.11 = f32[5,32,128]{2,1,0:T(8,128)S(1)} collective-permute-done((f32[5,32,128]{2,1,0:T(8,128)S(1)}, f32[5,32,128]{2,1,0:T(8,128)S(1)}, u32[]{:S(2)}, u32[]{:S(2)}) %collective-permute-start.11) | collective-permute-done | bytes 81952 | tf_op jit(solution)/shard_map/ppermute | solution.py:314
  90.8 1.3 %collective-permute-start.16 = (f32[5,32,128]{2,1,0:T(8,128)S(1)}, f32[5,32,128]{2,1,0:T(8,128)S(1)}, u32[]{:S(2)}, u32[]{:S(2)}) collective-permute-start(f32[5,32,128]{2,1,0:T(8,128)S(1)} %add_add_fusion.refs_0_), channel_id=1, source_target_pairs={{0,24},{8,16},{16,8},{24,0},{1,25},{9,17},{17,9},{25,1},{2,26},{10... | collective-permute-start | bytes 245768 | tf_op jit(solution)/shard_map/ppermute | solution.py:314
  92.1 0.1 collective-permute-start.15
  92.2 4.9 %collective-permute-done.16.refs_3_ = f32[5,32,128]{2,1,0:T(8,128)S(1)} collective-permute-done((f32[5,32,128]{2,1,0:T(8,128)S(1)}, f32[5,32,128]{2,1,0:T(8,128)S(1)}, u32[]{:S(2)}, u32[]{:S(2)}) %collective-permute-start.16) | collective-permute-done | bytes 81952 | tf_op jit(solution)/shard_map/ppermute | solution.py:314
  97.1 0.0 collective-permute-start.14
  97.1 0.1 collective-permute-done.15.refs_2_
  97.2 0.0 collective-permute-start.17
  97.2 4.3 %collective-permute-done.14.refs_1_ = f32[5,32,128]{2,1,0:T(8,128)S(1)} collective-permute-done((f32[5,32,128]{2,1,0:T(8,128)S(1)}, f32[5,32,128]{2,1,0:T(8,128)S(1)}, u32[]{:S(2)}, u32[]{:S(2)}) %collective-permute-start.14) | collective-permute-done | bytes 81952 | tf_op jit(solution)/shard_map/ppermute | solution.py:314
  101.5 0.0 collective-permute-start.20
  101.5 0.0 collective-permute-done.6.refs_3_
  101.6 0.5 collective-permute-start.19
  102.1 0.0 collective-permute-done.5.refs_2_
  102.1 0.1 collective-permute-start.18
  102.2 0.0 collective-permute-done.4.refs_1_
  102.2 0.3 copy-done.2
  102.4 0.5 copy-done.3
  103.0 0.8 copy-done.4
  103.8 4.5 %weight_order.1.m_ref = f32[1296,512]{1,0:T(8,128)} custom-call(s32[2]{0:T(128)} %pad_add_fusion.dp_ref, f32[336,512]{1,0:T(8,128)} %get-tuple-element.13.refs_0_, f32[336,512]{1,0:T(8,128)} %copy-done.4, f32[336,512]{1,0:T(8,128)} %copy-done.3, f32[336,512]{1,0:T(8,128)} %copy-done.2), custom_call_target="tpu_custom_call" | custom-call | tf_op jit(solution)/shard_map/weight_order/pallas_call | solution.py:245
  108.3 0.0 collective-permute-done.17.refs_4_
  108.3 0.0 collective-permute-done.20.refs_7_
  108.4 0.0 collective-permute-done.19.refs_6_
  108.4 0.0 collective-permute-done.18.refs_5_
  108.4 0.5 copy-done.11
  109.0 0.0 copy-done.12
  109.0 0.0 copy-done.13
  109.0 0.6 copy-done.14
  109.7 10.6 %newton_schulz.1 = f32[1296,512]{1,0:T(8,128)} custom-call(s32[2]{0:T(128)} %pad_add_fusion.dp_ref, f32[1296,512]{1,0:T(8,128)} %weight_order.1.m_ref, f32[5,32,128]{2,1,0:T(8,128)} %copy-done.7, f32[5,32,128]{2,1,0:T(8,128)} %copy-done.10, f32[5,32,128]{2,1,0:T(8,128)} %copy-done.9, f32[5,32,128]{2,1,0:T(8,128)} %copy-done.8, f32[5,32,128]{2,1,0:T(8,128)} %copy-done.11, ...), custom_call_target="tpu_custom_call" | custom-call | tf_op jit(solution)/shard_map/newton_schulz/pallas_call | solution.py:302
  (22 shorter events, 0.1 us)
Async XLA Ops:
  15.6 19.1 %collective-permute-start = (f32[672,256]{1,0:T(8,128)}, f32[672,256]{1,0:T(8,128)S(1)}, u32[]{:S(2)}, u32[]{:S(2)}) collective-permute-start(f32[672,256]{1,0:T(8,128)} %get-tuple-element.10), channel_id=1, source_target_pairs={{0,8},{8,0},{16,24},{24,16},{1,9},{9,1},{17,25},{25,17},{2,10},{10... | collective-permute-start | bytes 2064392 | tf_op jit(solution)/shard_map/ppermute | solution.py:314
  18.6 18.7 %collective-permute-start.2 = (f32[672,256]{1,0:T(8,128)}, f32[672,256]{1,0:T(8,128)S(1)}, u32[]{:S(2)}, u32[]{:S(2)}) collective-permute-start(f32[672,256]{1,0:T(8,128)} %get-tuple-element.12), channel_id=1, source_target_pairs={{0,16},{8,24},{16,0},{24,8},{1,17},{9,25},{17,1},{25,9},{2,18},{10... | collective-permute-start | bytes 2064392 | tf_op jit(solution)/shard_map/ppermute | solution.py:314
  34.7 9.6 %copy-start = (f32[672,256]{1,0:T(8,128)}, f32[672,256]{1,0:T(8,128)S(1)}, u32[]{:S(2)}) copy-start(f32[672,256]{1,0:T(8,128)S(1)} %collective-permute-done.ra) | copy-start | bytes 2064388
  36.0 9.3 %collective-permute-start.1 = (f32[336,256]{1,0:T(8,128)S(1)}, f32[336,256]{1,0:T(8,128)S(1)}, u32[]{:S(2)}, u32[]{:S(2)}) collective-permute-start(f32[336,256]{1,0:T(8,128)S(1)} %slice_add_fusion.1), channel_id=1, source_target_pairs={{0,16},{8,24},{16,0},{24,8},{1,17},{9,25},{17,1},{25,9},{2,18},{10... | collective-permute-start | bytes 1032200 | tf_op jit(solution)/shard_map/ppermute | solution.py:314
  37.3 10.0 %copy-start.1 = (f32[672,256]{1,0:T(8,128)}, f32[672,256]{1,0:T(8,128)S(1)}, u32[]{:S(2)}) copy-start(f32[672,256]{1,0:T(8,128)S(1)} %collective-permute-done.2.rb) | copy-start | bytes 2064388
  38.6 8.7 %collective-permute-start.3 = (f32[336,256]{1,0:T(8,128)S(1)}, f32[336,256]{1,0:T(8,128)S(1)}, u32[]{:S(2)}, u32[]{:S(2)}) collective-permute-start(f32[336,256]{1,0:T(8,128)S(1)} %slice_add_fusion), channel_id=1, source_target_pairs={{0,8},{8,0},{16,24},{24,16},{1,9},{9,1},{17,25},{25,17},{2,10},{10... | collective-permute-start | bytes 1032200 | tf_op jit(solution)/shard_map/ppermute | solution.py:314
  45.3 2.0 %copy-start.5 = (f32[336,256]{1,0:T(8,128)}, f32[336,256]{1,0:T(8,128)S(1)}, u32[]{:S(2)}) copy-start(f32[336,256]{1,0:T(8,128)S(1)} %collective-permute-done.1.a2) | copy-start | bytes 1032196
  47.3 0.7 copy-start.6
  52.5 1.8 %collective-permute-start.7 = (f32[4,5,32,128]{3,2,1,0:T(8,128)}, f32[4,5,32,128]{3,2,1,0:T(8,128)S(1)}, u32[]{:S(2)}, u32[]{:S(2)}) collective-permute-start(f32[4,5,32,128]{3,2,1,0:T(8,128)} %get-tuple-element.15), channel_id=1, source_target_pairs={{0,1},{1,0},{2,3},{3,2},{4,5},{5,4},{6,7},{7,6},{8,9},{9,8},{10,11... | collective-permute-start | bytes 983048 | tf_op jit(solution)/shard_map/ppermute | solution.py:314
  55.4 6.5 %collective-permute-start.8 = (f32[5,32,128]{2,1,0:T(8,128)S(1)}, f32[5,32,128]{2,1,0:T(8,128)S(1)}, u32[]{:S(2)}, u32[]{:S(2)}) collective-permute-start(f32[5,32,128]{2,1,0:T(8,128)S(1)} %get-tuple-element.16), channel_id=1, source_target_pairs={{0,8},{8,0},{16,24},{24,16},{1,9},{9,1},{17,25},{25,17},{2,10},{10... | collective-permute-start | bytes 245768 | tf_op jit(solution)/shard_map/ppermute | solution.py:314
  56.9 5.8 %collective-permute-start.10 = (f32[5,32,128]{2,1,0:T(8,128)S(1)}, f32[5,32,128]{2,1,0:T(8,128)S(1)}, u32[]{:S(2)}, u32[]{:S(2)}) collective-permute-start(f32[5,32,128]{2,1,0:T(8,128)S(1)} %get-tuple-element.17), channel_id=1, source_target_pairs={{0,24},{8,16},{16,8},{24,0},{1,25},{9,17},{17,9},{25,1},{2,26},{10... | collective-permute-start | bytes 245768 | tf_op jit(solution)/shard_map/ppermute | solution.py:314
  58.0 20.8 %collective-permute-start.9 = (f32[5,32,128]{2,1,0:T(8,128)S(1)}, f32[5,32,128]{2,1,0:T(8,128)S(1)}, u32[]{:S(2)}, u32[]{:S(2)}) collective-permute-start(f32[5,32,128]{2,1,0:T(8,128)S(1)} %get-tuple-element.18), channel_id=1, source_target_pairs={{0,16},{8,24},{16,0},{24,8},{1,17},{9,25},{17,1},{25,9},{2,18},{10... | collective-permute-start | bytes 245768 | tf_op jit(solution)/shard_map/ppermute | solution.py:314
  58.9 42.6 %collective-permute-start.6 = (f32[336,512]{1,0:T(8,128)}, f32[336,512]{1,0:T(8,128)S(1)}, u32[]{:S(2)}, u32[]{:S(2)}) collective-permute-start(f32[336,512]{1,0:T(8,128)} %get-tuple-element.13.refs_0_), channel_id=1, source_target_pairs={{0,24},{8,16},{16,8},{24,0},{1,25},{9,17},{17,9},{25,1},{2,26},{10... | collective-permute-start | bytes 2064392 | tf_op jit(solution)/shard_map/ppermute | solution.py:314
  60.4 41.7 %collective-permute-start.5 = (f32[336,512]{1,0:T(8,128)}, f32[336,512]{1,0:T(8,128)S(1)}, u32[]{:S(2)}, u32[]{:S(2)}) collective-permute-start(f32[336,512]{1,0:T(8,128)} %get-tuple-element.13.refs_0_), channel_id=1, source_target_pairs={{0,16},{8,24},{16,0},{24,8},{1,17},{9,25},{17,1},{25,9},{2,18},{10... | collective-permute-start | bytes 2064392 | tf_op jit(solution)/shard_map/ppermute | solution.py:314
  61.9 40.3 %collective-permute-start.4 = (f32[336,512]{1,0:T(8,128)}, f32[336,512]{1,0:T(8,128)S(1)}, u32[]{:S(2)}, u32[]{:S(2)}) collective-permute-start(f32[336,512]{1,0:T(8,128)} %get-tuple-element.13.refs_0_), channel_id=1, source_target_pairs={{0,8},{8,0},{16,24},{24,16},{1,9},{9,1},{17,25},{25,17},{2,10},{10... | collective-permute-start | bytes 2064392 | tf_op jit(solution)/shard_map/ppermute | solution.py:314
  78.8 6.5 %collective-permute-start.13 = (f32[5,32,128]{2,1,0:T(8,128)S(1)}, f32[5,32,128]{2,1,0:T(8,128)S(1)}, u32[]{:S(2)}, u32[]{:S(2)}) collective-permute-start(f32[5,32,128]{2,1,0:T(8,128)S(1)} %fusion.2), channel_id=1, source_target_pairs={{0,6},{1,7},{2,4},{3,5},{4,2},{5,3},{6,0},{7,1},{8,14},{9,15},{10,... | collective-permute-start | bytes 245768 | tf_op jit(solution)/shard_map/ppermute | solution.py:314
  82.5 6.2 %collective-permute-start.12 = (f32[5,32,128]{2,1,0:T(8,128)S(1)}, f32[5,32,128]{2,1,0:T(8,128)S(1)}, u32[]{:S(2)}, u32[]{:S(2)}) collective-permute-start(f32[5,32,128]{2,1,0:T(8,128)S(1)} %fusion.2), channel_id=1, source_target_pairs={{0,4},{1,5},{2,6},{3,7},{4,0},{5,1},{6,2},{7,3},{8,12},{9,13},{10,... | collective-permute-start | bytes 245768 | tf_op jit(solution)/shard_map/ppermute | solution.py:314
  85.4 5.3 %collective-permute-start.11 = (f32[5,32,128]{2,1,0:T(8,128)S(1)}, f32[5,32,128]{2,1,0:T(8,128)S(1)}, u32[]{:S(2)}, u32[]{:S(2)}) collective-permute-start(f32[5,32,128]{2,1,0:T(8,128)S(1)} %fusion.2), channel_id=1, source_target_pairs={{0,2},{1,3},{2,0},{3,1},{4,6},{5,7},{6,4},{7,5},{8,10},{9,11},{10,... | collective-permute-start | bytes 245768 | tf_op jit(solution)/shard_map/ppermute | solution.py:314
  90.7 17.7 %copy-start.7 = (f32[5,32,128]{2,1,0:T(8,128)}, f32[5,32,128]{2,1,0:T(8,128)S(1)}, u32[]{:S(2)}) copy-start(f32[5,32,128]{2,1,0:T(8,128)S(1)} %add_add_fusion.refs_0_) | copy-start | bytes 245764
  90.8 6.3 %collective-permute-start.16 = (f32[5,32,128]{2,1,0:T(8,128)S(1)}, f32[5,32,128]{2,1,0:T(8,128)S(1)}, u32[]{:S(2)}, u32[]{:S(2)}) collective-permute-start(f32[5,32,128]{2,1,0:T(8,128)S(1)} %add_add_fusion.refs_0_), channel_id=1, source_target_pairs={{0,24},{8,16},{16,8},{24,0},{1,25},{9,17},{17,9},{25,1},{2,26},{10... | collective-permute-start | bytes 245768 | tf_op jit(solution)/shard_map/ppermute | solution.py:314
  92.1 5.1 %collective-permute-start.15 = (f32[5,32,128]{2,1,0:T(8,128)S(1)}, f32[5,32,128]{2,1,0:T(8,128)S(1)}, u32[]{:S(2)}, u32[]{:S(2)}) collective-permute-start(f32[5,32,128]{2,1,0:T(8,128)S(1)} %add_add_fusion.refs_0_), channel_id=1, source_target_pairs={{0,16},{8,24},{16,0},{24,8},{1,17},{9,25},{17,1},{25,9},{2,18},{10... | collective-permute-start | bytes 245768 | tf_op jit(solution)/shard_map/ppermute | solution.py:314
  97.1 11.3 %copy-start.8 = (f32[5,32,128]{2,1,0:T(8,128)}, f32[5,32,128]{2,1,0:T(8,128)S(1)}, u32[]{:S(2)}) copy-start(f32[5,32,128]{2,1,0:T(8,128)S(1)} %collective-permute-done.16.refs_3_) | copy-start | bytes 245764
  97.1 4.4 %collective-permute-start.14 = (f32[5,32,128]{2,1,0:T(8,128)S(1)}, f32[5,32,128]{2,1,0:T(8,128)S(1)}, u32[]{:S(2)}, u32[]{:S(2)}) collective-permute-start(f32[5,32,128]{2,1,0:T(8,128)S(1)} %add_add_fusion.refs_0_), channel_id=1, source_target_pairs={{0,8},{8,0},{16,24},{24,16},{1,9},{9,1},{17,25},{25,17},{2,10},{10... | collective-permute-start | bytes 245768 | tf_op jit(solution)/shard_map/ppermute | solution.py:314
  97.2 11.2 %copy-start.9 = (f32[5,32,128]{2,1,0:T(8,128)}, f32[5,32,128]{2,1,0:T(8,128)S(1)}, u32[]{:S(2)}) copy-start(f32[5,32,128]{2,1,0:T(8,128)S(1)} %collective-permute-done.15.refs_2_) | copy-start | bytes 245764
  97.2 11.1 %collective-permute-start.17 = (f32[5,32,128]{2,1,0:T(8,128)S(1)}, f32[5,32,128]{2,1,0:T(8,128)S(1)}, u32[]{:S(2)}, u32[]{:S(2)}) collective-permute-start(f32[5,32,128]{2,1,0:T(8,128)S(1)} %add_add_fusion.refs_0_), channel_id=1, source_target_pairs={{0,1},{1,0},{2,3},{3,2},{4,5},{5,4},{6,7},{7,6},{8,9},{9,8},{10,11... | collective-permute-start | bytes 245768 | tf_op jit(solution)/shard_map/ppermute | solution.py:314
  101.5 6.9 %copy-start.10 = (f32[5,32,128]{2,1,0:T(8,128)}, f32[5,32,128]{2,1,0:T(8,128)S(1)}, u32[]{:S(2)}) copy-start(f32[5,32,128]{2,1,0:T(8,128)S(1)} %collective-permute-done.14.refs_1_) | copy-start | bytes 245764
  101.5 6.8 %collective-permute-start.20 = (f32[5,32,128]{2,1,0:T(8,128)S(1)}, f32[5,32,128]{2,1,0:T(8,128)S(1)}, u32[]{:S(2)}, u32[]{:S(2)}) collective-permute-start(f32[5,32,128]{2,1,0:T(8,128)S(1)} %collective-permute-done.16.refs_3_), channel_id=1, source_target_pairs={{0,1},{1,0},{2,3},{3,2},{4,5},{5,4},{6,7},{7,6},{8,9},{9,8},{10,11... | collective-permute-start | bytes 245768 | tf_op jit(solution)/shard_map/ppermute | solution.py:314
  101.6 0.9 copy-start.2
  101.6 6.8 %collective-permute-start.19 = (f32[5,32,128]{2,1,0:T(8,128)S(1)}, f32[5,32,128]{2,1,0:T(8,128)S(1)}, u32[]{:S(2)}, u32[]{:S(2)}) collective-permute-start(f32[5,32,128]{2,1,0:T(8,128)S(1)} %collective-permute-done.15.refs_2_), channel_id=1, source_target_pairs={{0,1},{1,0},{2,3},{3,2},{4,5},{5,4},{6,7},{7,6},{8,9},{9,8},{10,11... | collective-permute-start | bytes 245768 | tf_op jit(solution)/shard_map/ppermute | solution.py:314
  102.1 0.9 copy-start.3
  102.1 6.3 %collective-permute-start.18 = (f32[5,32,128]{2,1,0:T(8,128)S(1)}, f32[5,32,128]{2,1,0:T(8,128)S(1)}, u32[]{:S(2)}, u32[]{:S(2)}) collective-permute-start(f32[5,32,128]{2,1,0:T(8,128)S(1)} %collective-permute-done.14.refs_1_), channel_id=1, source_target_pairs={{0,1},{1,0},{2,3},{3,2},{4,5},{5,4},{6,7},{7,6},{8,9},{9,8},{10,11... | collective-permute-start | bytes 245768 | tf_op jit(solution)/shard_map/ppermute | solution.py:314
  103.0 0.8 copy-start.4
  108.3 0.6 copy-start.11
  108.4 0.7 copy-start.12
  108.4 0.7 copy-start.13
  109.0 0.6 copy-start.14

commit v2 on v1

v2 whole, which is shorter than its diff:
```python
import functools

import jax
import jax.numpy as jnp
from jax import lax
from jax.experimental import pallas as pl
from jax.experimental.pallas import tpu as pltpu
from jax.sharding import PartitionSpec as P

HW = 32
ROWS = 10368
PW = HW + 2
LANE = 128
TAPS = 27
A1, B1, C1 = 3.4445, -4.775, 2.0315
F32 = jnp.float32
BF16 = jnp.bfloat16
VMEM = pl.BlockSpec(memory_space=pltpu.VMEM)
HBM = pl.BlockSpec(memory_space=pl.ANY)
BLOCKS = (((0, 0), (0, 1), (0, 2), (0, 3), (1, 1)), ((1, 2), (1, 3), (2, 2), (2, 3), (3, 3)))


def column(rows):
    return pl.BlockSpec((rows, LANE), lambda c: (0, c))


def params(mib=24):
    return pltpu.CompilerParams(vmem_limit_bytes=mib << 20)


def near(x):
    return pltpu.with_memory_space_constraint(x, pltpu.VMEM)


def pair(tile, p, lane):
    t, c = divmod(p, LANE)
    if c + 64 <= LANE:
        return jnp.where(lane < c + 32, tile(t), tile(t + 4))
    if c + 32 <= LANE:
        far = jnp.where(lane < c, tile(t + 5), tile(t))
        if c + 32 == LANE:
            return far
        return jnp.where(lane < c + 32, far, tile(t + 4))
    near = jnp.where(lane < c + 32 - LANE, tile(t + 1), tile(t + 5))
    return jnp.where(lane < c, near, tile(t))


def build_slab(d0, half, xs, tail, v, cp):
    lane = lax.broadcasted_iota(jnp.int32, (16, LANE), 1)
    last = xs.shape[1] // LANE
    for g in range(cp // 16):
        rows = slice(16 * g, 16 * g + 16)

        def tile(t):
            return tail[rows, :] if t == last else xs[rows, LANE * t : LANE * t + LANE]

        for j in range(18):
            for kw in range(3):
                part = []
                for s1 in range(2):
                    p = (d0 + half * s1) * PW * PW + PW * j + kw
                    part.append(pltpu.roll(pair(tile, p, lane), (64 * s1 - p) % LANE, 1))
                r0 = (d0 * 3 + kw) * cp + 16 * g
                v[r0 : r0 + 16, LANE * j : LANE * j + LANE] = jnp.where(lane < 64, part[0], part[1])


def conv_part(d, half, taps, cp, qs, cot, v, outs):
    vox = HW * HW
    for c in range(2):
        lhs = []
        for q in qs[c]:
            for i in range(taps):
                t = jnp.minimum(q * taps + i, TAPS - 1)
                kd, kh, kw = t // 9, t // 3 % 3, t % 3
                r0 = pl.multiple_of(((d + kd) * 3 + kw) * cp, 16)
                lhs.append(v[pl.ds(r0, cp), pl.ds(pl.multiple_of(LANE * kh, LANE), 16 * LANE)])
        rhs = []
        for h in range(16):
            for s1 in range(2):
                for s0 in range(2):
                    r0 = (d + half * s1) * vox + (h + 16 * s0) * HW
                    rhs.append(cot[r0 : r0 + HW, 256 * c : 256 * c + 256])
        part = jnp.dot(jnp.concatenate(lhs, 0), jnp.concatenate(rhs, 0), preferred_element_type=F32)
        if d == 0:
            outs[c][...] = part
        else:
            outs[c][...] += part


def conv_kernel(depth, cp, taps, chunks, x_hbm, cot_hbm, *refs):
    outs = refs[:2]
    cot, v, xs, tail, xsem, csem = refs[2:]
    half = depth // 2
    ln = xs.shape[1]
    vox = HW * HW
    xcopy = pltpu.make_async_copy(x_hbm, xs, xsem)
    xcopy.start()
    copies = []
    for i in range(depth):
        rows = pl.ds(i * vox, vox)
        copies.append(pltpu.make_async_copy(cot_hbm.at[rows], cot.at[rows], csem.at[i]))
    for d in range(half):
        for s1 in range(2):
            copies[d + half * s1].start()
    xcopy.wait()
    n = ln // LANE * LANE
    if n < ln:
        tail[:, : ln - n] = xs[:, n:]
    for d0 in range(half + 2):
        build_slab(d0, half, xs, tail, v, cp)
    qs = chunks()
    for d in range(half):
        for s1 in range(2):
            copies[d + half * s1].wait()
        conv_part(d, half, taps, cp, qs, cot, v, outs)


def conv(x, cot, chunks, slots, taps):
    cp, ln = x.shape
    depth = cot.shape[0] // (HW * HW)
    return pl.pallas_call(
        functools.partial(conv_kernel, depth, cp, taps, chunks),
        out_shape=[pltpu.VMEM((slots * taps * cp, 256), F32)] * 2
        + [pltpu.VMEM(cot.shape, BF16), pltpu.VMEM((3 * (depth // 2 + 2) * cp, 18 * LANE), BF16)],
        in_specs=[HBM, HBM],
        out_specs=[VMEM] * 4,
        scratch_shapes=[
            pltpu.VMEM((cp, ln), BF16),
            pltpu.VMEM((cp, LANE), BF16),
            pltpu.SemaphoreType.DMA,
            pltpu.SemaphoreType.DMA((depth,)),
        ],
        compiler_params=params(),
        name="conv_first",
    )(x, cot)


def more_kernel(depth, cp, taps, chunks, cot, v, *outs):
    qs = chunks()
    for d in range(depth // 2):
        conv_part(d, depth // 2, taps, cp, qs, cot, v, outs)


def conv_more(cot, v, chunks, slots, taps, cp):
    depth = cot.shape[0] // (HW * HW)
    return pl.pallas_call(
        functools.partial(more_kernel, depth, cp, taps, chunks),
        out_shape=[pltpu.VMEM((slots * taps * cp, 256), F32)] * 2,
        in_specs=[VMEM] * 2,
        out_specs=[VMEM] * 2,
        compiler_params=params(),
        name="conv_more",
    )(near(cot), near(v))


def own_kernel(taps, cp, m_ref, o_ref):
    chans = m_ref.shape[0] // TAPS
    for i in range(taps):
        t = lax.axis_index("dp") * taps + i
        rows = m_ref[pl.ds(jnp.minimum(t, TAPS - 1), chans, stride=TAPS), :]
        o_ref[cp * i : cp * i + chans, :] = jnp.where(t < TAPS, rows, 0.0)
        if cp > chans:
            o_ref[cp * i + chans : cp * i + cp, :] = jnp.zeros((cp - chans, LANE), F32)


def own_momentum(momentum, taps, cp):
    return pl.pallas_call(
        functools.partial(own_kernel, taps, cp),
        out_shape=jax.ShapeDtypeStruct((taps * cp, momentum.shape[1]), F32),
        grid=(momentum.shape[1] // LANE,),
        in_specs=[column(momentum.shape[0])],
        out_specs=column(taps * cp),
        compiler_params=params(),
        name="own_momentum",
    )(momentum)


def split(x):
    hi = x.astype(BF16)
    return hi, (x - hi.astype(F32)).astype(BF16)


def dot_t(a, b):
    return lax.dot_general(a, b, (((0,), (0,)), ((), ())), preferred_element_type=F32)


def update(m, grad, taps, cp):
    tap = lax.axis_index("dp") * taps + lax.broadcasted_iota(jnp.int32, (taps * cp, 1), 0) // cp
    return jnp.where(tap < TAPS, 0.95 * m + grad, 0.0)


def update_kernel(taps, cp, m_ref, *refs):
    parts, outs = refs[:-2], refs[-2:]
    for c in range(2):
        grad = parts[c][...]
        for n in range(2 + c, len(parts), 2):
            grad = grad + parts[n][...]
        outs[c][...] = update(m_ref[:, 256 * c : 256 * c + 256], grad, taps, cp)


def momentum_update(own, parts, taps, cp):
    return pl.pallas_call(
        functools.partial(update_kernel, taps, cp),
        out_shape=[pltpu.VMEM((taps * cp, 256), F32)] * 2,
        in_specs=[VMEM] * (1 + len(parts)),
        out_specs=[VMEM] * 2,
        compiler_params=params(),
        name="momentum_update",
    )(near(own), *map(near, parts))


def upper_gram(m):
    hi, lo = split(m)
    out = []
    for i in range(4):
        a, b = slice(128 * i, 128 * i + 128), slice(128 * i, 512)
        out.append(dot_t(hi[:, a], hi[:, b]) + (dot_t(hi[:, a], lo[:, b]) + dot_t(lo[:, a], hi[:, b])))
    return out


def gram_kernel(ma, mb, keep, send):
    dp, core = lax.axis_index("dp"), lax.axis_index("shard") % 2
    gram = upper_gram(jnp.concatenate([ma[...], mb[...]], 1))
    for half in range(2):
        for n, (i, j) in enumerate(BLOCKS[half]):
            block = gram[i][:, 128 * (j - i) : 128 * (j - i) + 128]
            for r in range(4):
                piece = block[32 * r : 32 * r + 32]

                @pl.when(core == half)
                def _():
                    keep[r ^ dp, n] = piece

                @pl.when(core != half)
                def _():
                    send[r ^ dp, n] = piece


def own_gram(ma, mb):
    return pl.pallas_call(
        gram_kernel,
        out_shape=[pltpu.VMEM((4, 5, 32, 128), F32)] * 2,
        in_specs=[VMEM] * 2,
        out_specs=[VMEM] * 2,
        compiler_params=params(),
        name="own_gram",
    )(near(ma), near(mb))


def any_gram_kernel(ma, mb, g_ref):
    for i, rows in enumerate(upper_gram(jnp.concatenate([ma[...], mb[...]], 1))):
        g_ref[128 * i : 128 * i + 128, :] = jnp.zeros((128, 512), F32)
        g_ref[128 * i : 128 * i + 128, 128 * i :] = rows


def any_gram(ma, mb):
    return pl.pallas_call(
        any_gram_kernel,
        out_shape=jax.ShapeDtypeStruct((512, 512), F32),
        in_specs=[VMEM] * 2,
        out_specs=VMEM,
        compiler_params=params(),
        name="own_gram",
    )(near(ma), near(mb))


def order_kernel(taps, cp, chans, known, *refs):
    parts, (out, hi, lo, cols, sem) = refs[:-5], refs[-5:]
    copies = []
    for c in range(4):
        for r in range(len(parts) // 2):
            ref = parts[2 * r + c // 2]
            for i in range(ref.shape[0] // cp):
                t = (lax.axis_index("dp") ^ r) * taps + i if known else i
                if not known and i >= TAPS:
                    continue
                rows = ref[cp * i : cp * i + chans, LANE * (c % 2) : LANE * (c % 2) + LANE]

                @pl.when(t < TAPS)
                def _():
                    cols.at[c][pl.ds(t, chans, stride=TAPS), :] = rows

        copies.append(pltpu.make_async_copy(cols.at[c], out.at[:, pl.ds(LANE * c, LANE)], sem.at[c]))
        copies[c].start()
        hi[:, LANE * c : LANE * c + LANE], lo[:, LANE * c : LANE * c + LANE] = split(cols[c])
    for copy in copies:
        copy.wait()


def order(parts, taps, cp, chans, known):
    rows = chans * TAPS
    return pl.pallas_call(
        functools.partial(order_kernel, taps, cp, chans, known),
        out_shape=[jax.ShapeDtypeStruct((rows, 512), F32)] + [pltpu.VMEM((rows, 512), BF16)] * 2,
        in_specs=[VMEM] * len(parts),
        out_specs=[HBM, VMEM, VMEM],
        scratch_shapes=[pltpu.VMEM((4, rows, LANE), F32), pltpu.SemaphoreType.DMA((4,))],
        compiler_params=params(),
        name="weight_order",
    )(*map(near, parts))


def mm(a, b):
    ah, al = a
    bh, bl = b
    d = functools.partial(jnp.dot, preferred_element_type=F32)
    return d(ah, bh) + (d(ah, bl) + d(al, bh))


def row_cuts(rows):
    cuts = [min(rows, -(-rows * k // 24) * 8) for k in range(4)]
    return [(a, b) for a, b in zip(cuts, cuts[1:]) if b > a]


def apply_kernel(hi, lo, *refs):
    parts, (out, g_ref, acc, sem) = refs[:-4], refs[-4:]
    if len(parts) == 1:
        g_ref[...] = parts[0][...]
    else:
        dp, core = lax.axis_index("dp"), lax.axis_index("shard") % 2
        for n, part in enumerate(parts):
            which, r = divmod(n, 4)
            for half in range(2):

                @pl.when(core ^ which == half)
                def _():
                    for k, (i, j) in enumerate(BLOCKS[half]):
                        rows = pl.ds(pl.multiple_of(128 * i + 32 * (dp ^ r), 32), 32)
                        g_ref[rows, 128 * j : 128 * j + 128] = part[k]

    for i in range(4):
        for j in range(i + 1, 4):
            g_ref[128 * j : 128 * j + 128, 128 * i : 128 * i + 128] = g_ref[
                128 * i : 128 * i + 128, 128 * j : 128 * j + 128
            ].T
    gram = g_ref[...]
    n = gram.shape[0]
    diag = lax.broadcasted_iota(jnp.int32, (n, n), 0) == lax.broadcasted_iota(jnp.int32, (n, n), 1)
    trace = jnp.sum(jnp.where(diag, gram, 0.0), keepdims=True)
    scale = 1.0 / (jnp.sqrt(trace) + 1e-07)
    g = gram * scale * scale
    gs = split(g)
    p1 = jnp.where(diag, A1, 0.0) + B1 * g + C1 * mm(gs, gs)
    p1s = split(p1)
    g2 = mm(split(mm(gs, p1s)), p1s)
    g2s = split(g2)
    p2 = jnp.where(diag, A1, 0.0) + B1 * g2 + C1 * mm(g2s, g2s)
    qs = split(mm(p1s, split(p2)) * (scale * jnp.sqrt(F32(ROWS))))
    copies = []
    for k, (a, b) in enumerate(row_cuts(hi.shape[0])):
        acc[a:b, :] = mm((hi[a:b, :], lo[a:b, :]), qs)
        copies.append(pltpu.make_async_copy(acc.at[pl.ds(a, b - a)], out.at[pl.ds(a, b - a)], sem.at[k]))
        copies[k].start()
    for copy in copies:
        copy.wait()


def apply(hi, lo, parts):
    return pl.pallas_call(
        apply_kernel,
        out_shape=jax.ShapeDtypeStruct(hi.shape, F32),
        in_specs=[VMEM] * (2 + len(parts)),
        out_specs=HBM,
        scratch_shapes=[pltpu.VMEM((512, 512), F32), pltpu.VMEM(hi.shape, F32), pltpu.SemaphoreType.DMA((3,))],
        compiler_params=params(),
        name="newton_schulz",
    )(near(hi), near(lo), *map(near, parts))


def swap(x, axis, size, bit):
    return lax.ppermute(x, axis, [(i, i ^ bit) for i in range(size)])


def over_x(x):
    return swap(x, "dp", 4, 1)


def over_y(x):
    return swap(x, "dp", 4, 2)


def over_core(x):
    return swap(x, "shard", 8, 1)


def chunk_pair(a, b):
    def chunks():
        dp = lax.axis_index("dp")
        return [dp ^ a], [dp ^ b]

    return chunks


def body_4x8(layer_input, cotangent, momentum):
    chans = momentum.shape[0] // TAPS
    cp = layer_input.shape[0]
    taps = 7
    a3, b3, cot, v = conv(layer_input, cotangent, chunk_pair(3, 3), 1, taps)
    a3, b3 = over_x(a3), over_y(b3)
    a1, b1 = conv_more(cot, v, chunk_pair(1, 2), 1, taps, cp)
    a1, b1 = over_x(a1), over_y(b1)
    a2, b2 = conv_more(cot, v, chunk_pair(2, 1), 1, taps, cp)
    a2, b2 = over_y(a2 + a3), over_x(b2 + b3)
    a0, b0 = conv_more(cot, v, chunk_pair(0, 0), 1, taps, cp)
    own = own_momentum(momentum, taps, cp)
    ma, mb = momentum_update(own, (a0, b0, a1, b1, a2, b2), taps, cp)
    max_, mby = over_x(ma), over_y(mb)
    keep, send = own_gram(ma, mb)
    g = keep + over_core(send)
    g = g[0] + over_x(g[1]) + over_y(g[2]) + swap(g[3], "dp", 4, 3)
    ma_, mb_, max_, mby, g = lax.optimization_barrier((ma, mb, max_, mby, g))
    may, mbx, mad, mbd = over_y(ma_), over_x(mb_), over_y(max_), over_x(mby)
    g = g + swap(g, "shard", 8, 2) + swap(g, "shard", 8, 4) + swap(g, "shard", 8, 6)
    g = [g] + [swap(g, "dp", 4, r) for r in (1, 2, 3)]
    g = g + [over_core(x) for x in g]
    momentum_new, hi, lo = order((ma, mb, max_, mbx, may, mby, mad, mbd), taps, cp, chans, True)
    return momentum_new, apply(hi, lo, g)


def body_any(n_dp, layer_input, cotangent, momentum):
    chans = layer_input.shape[0]
    cp = -(-chans // 16) * 16
    taps = -(-TAPS // n_dp)
    x = jnp.pad(layer_input, ((0, cp - chans), (0, 0)))
    part = conv(x, cotangent, lambda: [list(range(n_dp))] * 2, n_dp, taps)[:2]
    grad = [lax.psum_scatter(p, "dp", scatter_dimension=0, tiled=True) for p in part]
    ma, mb = momentum_update(own_momentum(momentum, taps, cp), grad, taps, cp)
    gram = lax.psum(any_gram(ma, mb), ("dp", "shard"))
    full = [lax.all_gather(m, "dp", axis=0, tiled=True) for m in (ma, mb)]
    momentum_new, hi, lo = order(full, taps, cp, chans, False)
    return momentum_new, apply(hi, lo, [gram])


def solution(mesh):
    n_dp = mesh.shape["dp"]
    known = (n_dp, mesh.shape["shard"]) == (4, 8)
    return jax.shard_map(
        body_4x8 if known else functools.partial(body_any, n_dp),
        mesh=mesh,
        in_specs=(P("shard", "dp"), P("dp", None), P("shard", None)),
        out_specs=(P("shard", None), P("shard", None)),
        check_vma=False,
    )
```

time: 121 us -> 98.5 us (0.81)
  Pallas kernels: 52.1 us -> 27.1 us
  other arithmetic: 4.76 us -> 0.18 us
  waiting for transfers between devices: 35.8 us -> 40.2 us
  starting transfers between devices: 23 us -> 25.2 us
    pallas_call x5 -> x8, Pallas kernels: 48.5 us -> 26.6 us  [the longest x3 9.3 us: conv_more(): pl.pallas_call(functools.partial(more_kernel, depth, cp, taps, chunks), o...]
    ppermute x21 -> x26, waiting for transfers between devices: 35.8 us -> 40.2 us  [swap(): return lax.ppermute(x, axis, [(i, i ^ bit) for i in range(size)])]
    add x4, other arithmetic: 3.56 us -> 0.16 us  [the longest x2 0.09 us: body_4x8(): a2, b2 = (over_y(a2 + a3), over_x(b2 + b3))]
    pallas_call x1, Pallas kernels: 3.64 us -> 0.58 us  [own_momentum(): pl.pallas_call(functools.partial(own_kernel, taps, cp), out_shape=jax.Sha...]
    ppermute x21 -> x26, starting transfers between devices: 23 us -> 25.2 us  [swap(): return lax.ppermute(x, axis, [(i, i ^ bit) for i in range(size)])]
    unnamed x30 -> x6, local copies, waits for them, and re-layouts: 3.65 us -> 4.63 us
  transfers between devices with their start and end apart: 21 -> 26, of which waited for: 11 -> 9; matrix products, arithmetic and copies ran while one was open for 3% -> 0% of each run, Pallas kernels for 19% -> 12%
where the time goes in v2:
time: 98.5 us; the launch traced here: 98.3 us
  waiting for transfers between devices  40.2 us (41%)
  Pallas kernels  27.1 us (28%)
  starting transfers between devices  25.2 us (26%)
  local copies, waits for them, and re-layouts  4.65 us (5%)
    ppermute x26, waiting for transfers between devices, swap(): return lax.ppermute(x, axis, [(i, i ^ bit) for i in range(size)])  40.2 us
    ppermute x26, starting transfers between devices, swap(): return lax.ppermute(x, axis, [(i, i ^ bit) for i in range(size)])  25.2 us
    pallas_call x3, Pallas kernels, conv_more(): pl.pallas_call(functools.partial(more_kernel, depth, cp, taps, chunks), o...  9.3 us
    pallas_call x1, Pallas kernels, apply(): pl.pallas_call(apply_kernel, out_shape=jax.ShapeDtypeStruct(hi.shape, F32...  8.03 us
    pallas_call x1, Pallas kernels, conv(): pl.pallas_call(functools.partial(conv_kernel, depth, cp, taps, chunks), o...  6.09 us
    unnamed x6, local copies, waits for them, and re-layouts  4.63 us
  transfers between devices with their start and end apart: 26, of which 9 were waited for; matrix products, arithmetic and copies ran while one was open for 0% of the time, Pallas kernels for 12%

profile of v2, /device:TPU:0, one launch (start us, length us, event | category | flops | bytes accessed | tf_op | source)
XLA Modules:
  0.0 98.3 jit_solution(5824674751771120461)
XLA Ops:
  0.6 3.4 %copy-done = bf16[8192,512]{1,0:T(8,128)(2,1)S(1)} copy-done((bf16[8192,512]{1,0:T(8,128)(2,1)S(1)}, bf16[8192,512]{1,0:T(8,128)(2,1)}, u32[]{:S(2)}) %copy-start) | copy-done | bytes 8388632
  4.0 1.2 %copy-done.2 = bf16[48,11560]{1,0:T(8,128)(2,1)S(1)} copy-done((bf16[48,11560]{1,0:T(8,128)(2,1)S(1)}, bf16[48,11560]{1,0:T(8,128)(2,1)}, u32[]{:S(2)}) %copy-start.2) | copy-done | bytes 1109784
  5.3 6.1 %conv_first.1 = (f32[336,256]{1,0:T(8,128)S(1)}, f32[336,256]{1,0:T(8,128)S(1)}, bf16[8192,512]{1,0:T(8,128)(2,1)S(1)}, bf16[864,2304]{1,0:T(8,128)(2,1)S(1)}) custom-call(bf16[48,11560]{1,0:T(8,128)(2,1)S(1)} %copy-done.2, bf16[8192,512]{1,0:T(8,128)(2,1)S(1)} %copy-done), custom_call_target="tpu_custom_call" | custom-call | tf_op jit(solution)/shard_map/conv_first/pallas_call | solution.py:121
  11.4 3.0 %collective-permute-start.4 = (f32[336,256]{1,0:T(8,128)S(1)}, f32[336,256]{1,0:T(8,128)S(1)}, u32[]{:S(2)}, u32[]{:S(2)}) collective-permute-start(f32[336,256]{1,0:T(8,128)S(1)} %get-tuple-element.33), channel_id=1, source_target_pairs={{0,16},{8,24},{16,0},{24,8},{1,17},{9,25},{17,1},{25,9},{2,18},{10... | collective-permute-start | bytes 1032200 | tf_op jit(solution)/shard_map/ppermute | solution.py:371
  14.4 1.5 %collective-permute-start.2 = (f32[336,256]{1,0:T(8,128)S(1)}, f32[336,256]{1,0:T(8,128)S(1)}, u32[]{:S(2)}, u32[]{:S(2)}) collective-permute-start(f32[336,256]{1,0:T(8,128)S(1)} %get-tuple-element.31), channel_id=1, source_target_pairs={{0,8},{8,0},{16,24},{24,16},{1,9},{9,1},{17,25},{25,17},{2,10},{10... | collective-permute-start | bytes 1032200 | tf_op jit(solution)/shard_map/ppermute | solution.py:371
  15.9 3.1 %conv_more.4 = (f32[336,256]{1,0:T(8,128)S(1)}, f32[336,256]{1,0:T(8,128)S(1)}) custom-call(bf16[8192,512]{1,0:T(8,128)(2,1)S(1)} %get-tuple-element.24.cot, bf16[864,2304]{1,0:T(8,128)(2,1)S(1)} %get-tuple-element.25.v), custom_call_target="tpu_custom_call" | custom-call | tf_op jit(solution)/shard_map/conv_more/pallas_call | solution.py:146
  19.0 0.7 collective-permute-start
  19.7 0.0 collective-permute-start.1
  19.7 3.1 %conv_more.5 = (f32[336,256]{1,0:T(8,128)S(1)}, f32[336,256]{1,0:T(8,128)S(1)}) custom-call(bf16[8192,512]{1,0:T(8,128)(2,1)S(1)} %get-tuple-element.24.cot, bf16[864,2304]{1,0:T(8,128)(2,1)S(1)} %get-tuple-element.25.v), custom_call_target="tpu_custom_call" | custom-call | tf_op jit(solution)/shard_map/conv_more/pallas_call | solution.py:146
  22.9 0.4 collective-permute-done.4
  23.3 2.1 %collective-permute-start.5 = (f32[336,256]{1,0:T(8,128)S(1)}, f32[336,256]{1,0:T(8,128)S(1)}, u32[]{:S(2)}, u32[]{:S(2)}) collective-permute-start(f32[336,256]{1,0:T(8,128)S(1)} %add.28), channel_id=1, source_target_pairs={{0,8},{8,0},{16,24},{24,16},{1,9},{9,1},{17,25},{25,17},{2,10},{10... | collective-permute-start | bytes 1032200 | tf_op jit(solution)/shard_map/ppermute | solution.py:371
  25.4 0.0 collective-permute-done.2
  25.5 0.0 copy-start.1
  25.5 1.6 %collective-permute-start.3 = (f32[336,256]{1,0:T(8,128)S(1)}, f32[336,256]{1,0:T(8,128)S(1)}, u32[]{:S(2)}, u32[]{:S(2)}) collective-permute-start(f32[336,256]{1,0:T(8,128)S(1)} %add.27), channel_id=1, source_target_pairs={{0,16},{8,24},{16,0},{24,8},{1,17},{9,25},{17,1},{25,9},{2,18},{10... | collective-permute-start | bytes 1032200 | tf_op jit(solution)/shard_map/ppermute | solution.py:371
  27.1 3.0 %conv_more.3 = (f32[336,256]{1,0:T(8,128)S(1)}, f32[336,256]{1,0:T(8,128)S(1)}) custom-call(bf16[8192,512]{1,0:T(8,128)(2,1)S(1)} %get-tuple-element.24.cot, bf16[864,2304]{1,0:T(8,128)(2,1)S(1)} %get-tuple-element.25.v), custom_call_target="tpu_custom_call" | custom-call | tf_op jit(solution)/shard_map/conv_more/pallas_call | solution.py:146
  30.1 0.6 own_momentum.1.m_ref
  30.7 2.1 %collective-permute-done.refs_2_ = f32[336,256]{1,0:T(8,128)S(1)} collective-permute-done((f32[336,256]{1,0:T(8,128)S(1)}, f32[336,256]{1,0:T(8,128)S(1)}, u32[]{:S(2)}, u32[]{:S(2)}) %collective-permute-start) | collective-permute-done | bytes 344096 | tf_op jit(solution)/shard_map/ppermute | solution.py:371
  32.8 0.0 collective-permute-done.1.refs_3_
  32.8 5.9 %collective-permute-done.5.refs_5_ = f32[336,256]{1,0:T(8,128)S(1)} collective-permute-done((f32[336,256]{1,0:T(8,128)S(1)}, f32[336,256]{1,0:T(8,128)S(1)}, u32[]{:S(2)}, u32[]{:S(2)}) %collective-permute-start.5) | collective-permute-done | bytes 344096 | tf_op jit(solution)/shard_map/ppermute | solution.py:371
  38.7 0.0 collective-permute-done.3.refs_4_
  38.7 0.2 momentum_update.1
  38.8 1.3 %own_gram.1 = (f32[4,5,32,128]{3,2,1,0:T(8,128)S(1)}, f32[4,5,32,128]{3,2,1,0:T(8,128)S(1)}) custom-call(f32[336,256]{1,0:T(8,128)S(1)} %get-tuple-element.40.ma.refs_0_, f32[336,256]{1,0:T(8,128)S(1)} %get-tuple-element.39.mb.refs_1_), custom_call_target="tpu_custom_call" | custom-call | tf_op jit(solution)/shard_map/own_gram/pallas_call | solution.py:240
  40.1 0.1 collective-permute-start.8
  40.2 1.6 %collective-permute-start.6 = (f32[336,256]{1,0:T(8,128)S(1)}, f32[336,256]{1,0:T(8,128)S(1)}, u32[]{:S(2)}, u32[]{:S(2)}) collective-permute-start(f32[336,256]{1,0:T(8,128)S(1)} %get-tuple-element.40.ma.refs_0_), channel_id=1, source_target_pairs={{0,8},{8,0},{16,24},{24,16},{1,9},{9,1},{17,25},{25,17},{2,10},{10... | collective-permute-start | bytes 1032200 | tf_op jit(solution)/shard_map/ppermute | solution.py:371
  41.7 0.5 collective-permute-start.7
  42.2 0.0 collective-permute-done.8
  42.3 1.6 %collective-permute-start.10 = (f32[5,32,128]{2,1,0:T(8,128)S(1)}, f32[5,32,128]{2,1,0:T(8,128)S(1)}, u32[]{:S(2)}, u32[]{:S(2)}) collective-permute-start(f32[5,32,128]{2,1,0:T(8,128)S(1)} %get-tuple-element.48), channel_id=1, source_target_pairs={{0,16},{8,24},{16,0},{24,8},{1,17},{9,25},{17,1},{25,9},{2,18},{10... | collective-permute-start | bytes 245768 | tf_op jit(solution)/shard_map/ppermute | solution.py:371
  43.9 1.0 collective-permute-start.11
  44.9 1.0 %collective-permute-start.9 = (f32[5,32,128]{2,1,0:T(8,128)S(1)}, f32[5,32,128]{2,1,0:T(8,128)S(1)}, u32[]{:S(2)}, u32[]{:S(2)}) collective-permute-start(f32[5,32,128]{2,1,0:T(8,128)S(1)} %get-tuple-element.46), channel_id=1, source_target_pairs={{0,8},{8,0},{16,24},{24,16},{1,9},{9,1},{17,25},{25,17},{2,10},{10... | collective-permute-start | bytes 245768 | tf_op jit(solution)/shard_map/ppermute | solution.py:371
  45.9 9.5 %collective-permute-done.10 = f32[5,32,128]{2,1,0:T(8,128)S(1)} collective-permute-done((f32[5,32,128]{2,1,0:T(8,128)S(1)}, f32[5,32,128]{2,1,0:T(8,128)S(1)}, u32[]{:S(2)}, u32[]{:S(2)}) %collective-permute-start.10) | collective-permute-done | bytes 81952 | tf_op jit(solution)/shard_map/ppermute | solution.py:371
  55.4 0.0 collective-permute-done.11
  55.4 0.0 collective-permute-done.9
  55.4 0.0 collective-permute-done.6.refs_2_
  55.4 0.0 collective-permute-done.7.refs_5_
  55.4 1.6 %collective-permute-start.16 = (f32[5,32,128]{2,1,0:T(8,128)S(1)}, f32[5,32,128]{2,1,0:T(8,128)S(1)}, u32[]{:S(2)}, u32[]{:S(2)}) collective-permute-start(f32[5,32,128]{2,1,0:T(8,128)S(1)} %fusion.2), channel_id=1, source_target_pairs={{0,2},{1,3},{2,0},{3,1},{4,6},{5,7},{6,4},{7,5},{8,10},{9,11},{10,... | collective-permute-start | bytes 245768 | tf_op jit(solution)/shard_map/ppermute | solution.py:371
  57.1 2.6 %collective-permute-start.17 = (f32[5,32,128]{2,1,0:T(8,128)S(1)}, f32[5,32,128]{2,1,0:T(8,128)S(1)}, u32[]{:S(2)}, u32[]{:S(2)}) collective-permute-start(f32[5,32,128]{2,1,0:T(8,128)S(1)} %fusion.2), channel_id=1, source_target_pairs={{0,4},{1,5},{2,6},{3,7},{4,0},{5,1},{6,2},{7,3},{8,12},{9,13},{10,... | collective-permute-start | bytes 245768 | tf_op jit(solution)/shard_map/ppermute | solution.py:371
  59.7 0.2 collective-permute-start.18
  59.9 0.5 collective-permute-start.12
  60.4 0.4 collective-permute-start.13
  60.8 0.0 collective-permute-done.16
  60.8 1.7 %collective-permute-start.14 = (f32[336,256]{1,0:T(8,128)S(1)}, f32[336,256]{1,0:T(8,128)S(1)}, u32[]{:S(2)}, u32[]{:S(2)}) collective-permute-start(f32[336,256]{1,0:T(8,128)S(1)} %collective-permute-done.6.refs_2_), channel_id=1, source_target_pairs={{0,16},{8,24},{16,0},{24,8},{1,17},{9,25},{17,1},{25,9},{2,18},{10... | collective-permute-start | bytes 1032200 | tf_op jit(solution)/shard_map/ppermute | solution.py:371
  62.5 2.4 %collective-permute-done.17 = f32[5,32,128]{2,1,0:T(8,128)S(1)} collective-permute-done((f32[5,32,128]{2,1,0:T(8,128)S(1)}, f32[5,32,128]{2,1,0:T(8,128)S(1)}, u32[]{:S(2)}, u32[]{:S(2)}) %collective-permute-start.17) | collective-permute-done | bytes 81952 | tf_op jit(solution)/shard_map/ppermute | solution.py:371
  64.9 0.6 collective-permute-start.15
  65.5 0.5 collective-permute-done.18
  66.0 1.0 collective-permute-start.19
  67.0 10.5 %collective-permute-done.19.refs_1_ = f32[5,32,128]{2,1,0:T(8,128)S(1)} collective-permute-done((f32[5,32,128]{2,1,0:T(8,128)S(1)}, f32[5,32,128]{2,1,0:T(8,128)S(1)}, u32[]{:S(2)}, u32[]{:S(2)}) %collective-permute-start.19) | collective-permute-done | bytes 81952 | tf_op jit(solution)/shard_map/ppermute | solution.py:371
  77.5 0.5 collective-permute-start.20
  78.0 3.9 %collective-permute-done.20.refs_2_ = f32[5,32,128]{2,1,0:T(8,128)S(1)} collective-permute-done((f32[5,32,128]{2,1,0:T(8,128)S(1)}, f32[5,32,128]{2,1,0:T(8,128)S(1)}, u32[]{:S(2)}, u32[]{:S(2)}) %collective-permute-start.20) | collective-permute-done | bytes 81952 | tf_op jit(solution)/shard_map/ppermute | solution.py:371
  82.0 0.5 collective-permute-start.21
  82.5 4.8 %collective-permute-done.21.refs_3_ = f32[5,32,128]{2,1,0:T(8,128)S(1)} collective-permute-done((f32[5,32,128]{2,1,0:T(8,128)S(1)}, f32[5,32,128]{2,1,0:T(8,128)S(1)}, u32[]{:S(2)}, u32[]{:S(2)}) %collective-permute-start.21) | collective-permute-done | bytes 81952 | tf_op jit(solution)/shard_map/ppermute | solution.py:371
  87.3 0.0 collective-permute-start.22
  87.3 0.0 collective-permute-done.12.refs_3_
  87.3 0.5 collective-permute-start.23
  87.8 0.0 collective-permute-done.13.refs_4_
  87.8 0.1 collective-permute-start.24
  87.9 0.0 collective-permute-done.14.refs_6_
  87.9 0.4 collective-permute-start.25
  88.4 0.0 collective-permute-done.15.refs_7_
  88.4 1.7 %weight_order.1 = (f32[1296,512]{1,0:T(8,128)}, bf16[1296,512]{1,0:T(8,128)(2,1)S(1)}, bf16[1296,512]{1,0:T(8,128)(2,1)S(1)}) custom-call(f32[336,256]{1,0:T(8,128)S(1)} %get-tuple-element.40.ma.refs_0_, f32[336,256]{1,0:T(8,128)S(1)} %get-tuple-element.39.mb.refs_1_, f32[336,256]{1,0:T(8,128)S(1)} %collective-permute-done.6.refs_2_, ...), custom_call_target="tpu_custom_call" | custom-call | tf_op jit(solution)/shard_map/weight_order/pallas_call | solution.py:292
  90.1 0.0 collective-permute-done.22.refs_4_
  90.1 0.0 collective-permute-done.23.refs_5_
  90.1 0.0 collective-permute-done.24.refs_6_
  90.1 0.0 collective-permute-done.25.refs_7_
  90.1 8.0 %newton_schulz.1 = f32[1296,512]{1,0:T(8,128)} custom-call(bf16[1296,512]{1,0:T(8,128)(2,1)S(1)} %get-tuple-element.43.hi, bf16[1296,512]{1,0:T(8,128)(2,1)S(1)} %get-tuple-element.44.lo, f32[5,32,128]{2,1,0:T(8,128)S(1)} %add_add_fusion.refs_0_, f32[5,32,128]{2,1,0:T(8,128)S(1)} %collective-permute-done.19.refs_1_, ...), custom_call_target="tpu_custom_call" | custom-call | tf_op jit(solution)/shard_map/newton_schulz/pallas_call | solution.py:359
  (9 shorter events, 0.2 us)
Async XLA Ops:
  0.6 3.4 %copy-start = (bf16[8192,512]{1,0:T(8,128)(2,1)S(1)}, bf16[8192,512]{1,0:T(8,128)(2,1)}, u32[]{:S(2)}) copy-start(bf16[8192,512]{1,0:T(8,128)(2,1)} %cot_hbm.1) | copy-start | bytes 25165828
  4.0 1.2 %copy-start.2 = (bf16[48,11560]{1,0:T(8,128)(2,1)S(1)}, bf16[48,11560]{1,0:T(8,128)(2,1)}, u32[]{:S(2)}) copy-start(bf16[48,11560]{1,0:T(8,128)(2,1)} %x_hbm.1) | copy-start | bytes 3329284
  11.4 11.9 %collective-permute-start.4 = (f32[336,256]{1,0:T(8,128)S(1)}, f32[336,256]{1,0:T(8,128)S(1)}, u32[]{:S(2)}, u32[]{:S(2)}) collective-permute-start(f32[336,256]{1,0:T(8,128)S(1)} %get-tuple-element.33), channel_id=1, source_target_pairs={{0,16},{8,24},{16,0},{24,8},{1,17},{9,25},{17,1},{25,9},{2,18},{10... | collective-permute-start | bytes 1032200 | tf_op jit(solution)/shard_map/ppermute | solution.py:371
  14.4 11.0 %collective-permute-start.2 = (f32[336,256]{1,0:T(8,128)S(1)}, f32[336,256]{1,0:T(8,128)S(1)}, u32[]{:S(2)}, u32[]{:S(2)}) collective-permute-start(f32[336,256]{1,0:T(8,128)S(1)} %get-tuple-element.31), channel_id=1, source_target_pairs={{0,8},{8,0},{16,24},{24,16},{1,9},{9,1},{17,25},{25,17},{2,10},{10... | collective-permute-start | bytes 1032200 | tf_op jit(solution)/shard_map/ppermute | solution.py:371
  19.0 13.7 %collective-permute-start = (f32[336,256]{1,0:T(8,128)S(1)}, f32[336,256]{1,0:T(8,128)S(1)}, u32[]{:S(2)}, u32[]{:S(2)}) collective-permute-start(f32[336,256]{1,0:T(8,128)S(1)} %get-tuple-element.28), channel_id=1, source_target_pairs={{0,8},{8,0},{16,24},{24,16},{1,9},{9,1},{17,25},{25,17},{2,10},{10... | collective-permute-start | bytes 1032200 | tf_op jit(solution)/shard_map/ppermute | solution.py:371
  19.7 13.1 %collective-permute-start.1 = (f32[336,256]{1,0:T(8,128)S(1)}, f32[336,256]{1,0:T(8,128)S(1)}, u32[]{:S(2)}, u32[]{:S(2)}) collective-permute-start(f32[336,256]{1,0:T(8,128)S(1)} %get-tuple-element.29), channel_id=1, source_target_pairs={{0,16},{8,24},{16,0},{24,8},{1,17},{9,25},{17,1},{25,9},{2,18},{10... | collective-permute-start | bytes 1032200 | tf_op jit(solution)/shard_map/ppermute | solution.py:371
  23.3 15.3 %collective-permute-start.5 = (f32[336,256]{1,0:T(8,128)S(1)}, f32[336,256]{1,0:T(8,128)S(1)}, u32[]{:S(2)}, u32[]{:S(2)}) collective-permute-start(f32[336,256]{1,0:T(8,128)S(1)} %add.28), channel_id=1, source_target_pairs={{0,8},{8,0},{16,24},{24,16},{1,9},{9,1},{17,25},{25,17},{2,10},{10... | collective-permute-start | bytes 1032200 | tf_op jit(solution)/shard_map/ppermute | solution.py:371
  25.5 4.6 %copy-start.1 = (f32[1296,512]{1,0:T(8,128)S(1)}, f32[1296,512]{1,0:T(8,128)}, u32[]{:S(2)}) copy-start(f32[1296,512]{1,0:T(8,128)} %m_ref.1) | copy-start | bytes 7962628
  25.5 13.2 %collective-permute-start.3 = (f32[336,256]{1,0:T(8,128)S(1)}, f32[336,256]{1,0:T(8,128)S(1)}, u32[]{:S(2)}, u32[]{:S(2)}) collective-permute-start(f32[336,256]{1,0:T(8,128)S(1)} %add.27), channel_id=1, source_target_pairs={{0,16},{8,24},{16,0},{24,8},{1,17},{9,25},{17,1},{25,9},{2,18},{10... | collective-permute-start | bytes 1032200 | tf_op jit(solution)/shard_map/ppermute | solution.py:371
  40.1 2.1 %collective-permute-start.8 = (f32[4,5,32,128]{3,2,1,0:T(8,128)S(1)}, f32[4,5,32,128]{3,2,1,0:T(8,128)S(1)}, u32[]{:S(2)}, u32[]{:S(2)}) collective-permute-start(f32[4,5,32,128]{3,2,1,0:T(8,128)S(1)} %get-tuple-element.37), channel_id=1, source_target_pairs={{0,1},{1,0},{2,3},{3,2},{4,5},{5,4},{6,7},{7,6},{8,9},{9,8},{10,11... | collective-permute-start | bytes 983048 | tf_op jit(solution)/shard_map/ppermute | solution.py:371
  40.2 15.2 %collective-permute-start.6 = (f32[336,256]{1,0:T(8,128)S(1)}, f32[336,256]{1,0:T(8,128)S(1)}, u32[]{:S(2)}, u32[]{:S(2)}) collective-permute-start(f32[336,256]{1,0:T(8,128)S(1)} %get-tuple-element.40.ma.refs_0_), channel_id=1, source_target_pairs={{0,8},{8,0},{16,24},{24,16},{1,9},{9,1},{17,25},{25,17},{2,10},{10... | collective-permute-start | bytes 1032200 | tf_op jit(solution)/shard_map/ppermute | solution.py:371
  41.7 13.7 %collective-permute-start.7 = (f32[336,256]{1,0:T(8,128)S(1)}, f32[336,256]{1,0:T(8,128)S(1)}, u32[]{:S(2)}, u32[]{:S(2)}) collective-permute-start(f32[336,256]{1,0:T(8,128)S(1)} %get-tuple-element.39.mb.refs_1_), channel_id=1, source_target_pairs={{0,16},{8,24},{16,0},{24,8},{1,17},{9,25},{17,1},{25,9},{2,18},{10... | collective-permute-start | bytes 1032200 | tf_op jit(solution)/shard_map/ppermute | solution.py:371
  42.3 13.1 %collective-permute-start.10 = (f32[5,32,128]{2,1,0:T(8,128)S(1)}, f32[5,32,128]{2,1,0:T(8,128)S(1)}, u32[]{:S(2)}, u32[]{:S(2)}) collective-permute-start(f32[5,32,128]{2,1,0:T(8,128)S(1)} %get-tuple-element.48), channel_id=1, source_target_pairs={{0,16},{8,24},{16,0},{24,8},{1,17},{9,25},{17,1},{25,9},{2,18},{10... | collective-permute-start | bytes 245768 | tf_op jit(solution)/shard_map/ppermute | solution.py:371
  43.9 11.5 %collective-permute-start.11 = (f32[5,32,128]{2,1,0:T(8,128)S(1)}, f32[5,32,128]{2,1,0:T(8,128)S(1)}, u32[]{:S(2)}, u32[]{:S(2)}) collective-permute-start(f32[5,32,128]{2,1,0:T(8,128)S(1)} %get-tuple-element.47), channel_id=1, source_target_pairs={{0,24},{8,16},{16,8},{24,0},{1,25},{9,17},{17,9},{25,1},{2,26},{10... | collective-permute-start | bytes 245768 | tf_op jit(solution)/shard_map/ppermute | solution.py:371
  44.9 10.5 %collective-permute-start.9 = (f32[5,32,128]{2,1,0:T(8,128)S(1)}, f32[5,32,128]{2,1,0:T(8,128)S(1)}, u32[]{:S(2)}, u32[]{:S(2)}) collective-permute-start(f32[5,32,128]{2,1,0:T(8,128)S(1)} %get-tuple-element.46), channel_id=1, source_target_pairs={{0,8},{8,0},{16,24},{24,16},{1,9},{9,1},{17,25},{25,17},{2,10},{10... | collective-permute-start | bytes 245768 | tf_op jit(solution)/shard_map/ppermute | solution.py:371
  55.4 5.4 %collective-permute-start.16 = (f32[5,32,128]{2,1,0:T(8,128)S(1)}, f32[5,32,128]{2,1,0:T(8,128)S(1)}, u32[]{:S(2)}, u32[]{:S(2)}) collective-permute-start(f32[5,32,128]{2,1,0:T(8,128)S(1)} %fusion.2), channel_id=1, source_target_pairs={{0,2},{1,3},{2,0},{3,1},{4,6},{5,7},{6,4},{7,5},{8,10},{9,11},{10,... | collective-permute-start | bytes 245768 | tf_op jit(solution)/shard_map/ppermute | solution.py:371
  57.1 7.8 %collective-permute-start.17 = (f32[5,32,128]{2,1,0:T(8,128)S(1)}, f32[5,32,128]{2,1,0:T(8,128)S(1)}, u32[]{:S(2)}, u32[]{:S(2)}) collective-permute-start(f32[5,32,128]{2,1,0:T(8,128)S(1)} %fusion.2), channel_id=1, source_target_pairs={{0,4},{1,5},{2,6},{3,7},{4,0},{5,1},{6,2},{7,3},{8,12},{9,13},{10,... | collective-permute-start | bytes 245768 | tf_op jit(solution)/shard_map/ppermute | solution.py:371
  59.7 6.3 %collective-permute-start.18 = (f32[5,32,128]{2,1,0:T(8,128)S(1)}, f32[5,32,128]{2,1,0:T(8,128)S(1)}, u32[]{:S(2)}, u32[]{:S(2)}) collective-permute-start(f32[5,32,128]{2,1,0:T(8,128)S(1)} %fusion.2), channel_id=1, source_target_pairs={{0,6},{1,7},{2,4},{3,5},{4,2},{5,3},{6,0},{7,1},{8,14},{9,15},{10,... | collective-permute-start | bytes 245768 | tf_op jit(solution)/shard_map/ppermute | solution.py:371
  59.9 27.5 %collective-permute-start.12 = (f32[336,256]{1,0:T(8,128)S(1)}, f32[336,256]{1,0:T(8,128)S(1)}, u32[]{:S(2)}, u32[]{:S(2)}) collective-permute-start(f32[336,256]{1,0:T(8,128)S(1)} %get-tuple-element.39.mb.refs_1_), channel_id=1, source_target_pairs={{0,8},{8,0},{16,24},{24,16},{1,9},{9,1},{17,25},{25,17},{2,10},{10... | collective-permute-start | bytes 1032200 | tf_op jit(solution)/shard_map/ppermute | solution.py:371
  60.4 27.4 %collective-permute-start.13 = (f32[336,256]{1,0:T(8,128)S(1)}, f32[336,256]{1,0:T(8,128)S(1)}, u32[]{:S(2)}, u32[]{:S(2)}) collective-permute-start(f32[336,256]{1,0:T(8,128)S(1)} %get-tuple-element.40.ma.refs_0_), channel_id=1, source_target_pairs={{0,16},{8,24},{16,0},{24,8},{1,17},{9,25},{17,1},{25,9},{2,18},{10... | collective-permute-start | bytes 1032200 | tf_op jit(solution)/shard_map/ppermute | solution.py:371
  60.8 27.1 %collective-permute-start.14 = (f32[336,256]{1,0:T(8,128)S(1)}, f32[336,256]{1,0:T(8,128)S(1)}, u32[]{:S(2)}, u32[]{:S(2)}) collective-permute-start(f32[336,256]{1,0:T(8,128)S(1)} %collective-permute-done.6.refs_2_), channel_id=1, source_target_pairs={{0,16},{8,24},{16,0},{24,8},{1,17},{9,25},{17,1},{25,9},{2,18},{10... | collective-permute-start | bytes 1032200 | tf_op jit(solution)/shard_map/ppermute | solution.py:371
  64.9 23.5 %collective-permute-start.15 = (f32[336,256]{1,0:T(8,128)S(1)}, f32[336,256]{1,0:T(8,128)S(1)}, u32[]{:S(2)}, u32[]{:S(2)}) collective-permute-start(f32[336,256]{1,0:T(8,128)S(1)} %collective-permute-done.7.refs_5_), channel_id=1, source_target_pairs={{0,8},{8,0},{16,24},{24,16},{1,9},{9,1},{17,25},{25,17},{2,10},{10... | collective-permute-start | bytes 1032200 | tf_op jit(solution)/shard_map/ppermute | solution.py:371
  66.0 11.5 %collective-permute-start.19 = (f32[5,32,128]{2,1,0:T(8,128)S(1)}, f32[5,32,128]{2,1,0:T(8,128)S(1)}, u32[]{:S(2)}, u32[]{:S(2)}) collective-permute-start(f32[5,32,128]{2,1,0:T(8,128)S(1)} %add_add_fusion.refs_0_), channel_id=1, source_target_pairs={{0,8},{8,0},{16,24},{24,16},{1,9},{9,1},{17,25},{25,17},{2,10},{10... | collective-permute-start | bytes 245768 | tf_op jit(solution)/shard_map/ppermute | solution.py:371
  77.5 4.5 %collective-permute-start.20 = (f32[5,32,128]{2,1,0:T(8,128)S(1)}, f32[5,32,128]{2,1,0:T(8,128)S(1)}, u32[]{:S(2)}, u32[]{:S(2)}) collective-permute-start(f32[5,32,128]{2,1,0:T(8,128)S(1)} %add_add_fusion.refs_0_), channel_id=1, source_target_pairs={{0,16},{8,24},{16,0},{24,8},{1,17},{9,25},{17,1},{25,9},{2,18},{10... | collective-permute-start | bytes 245768 | tf_op jit(solution)/shard_map/ppermute | solution.py:371
  82.0 5.3 %collective-permute-start.21 = (f32[5,32,128]{2,1,0:T(8,128)S(1)}, f32[5,32,128]{2,1,0:T(8,128)S(1)}, u32[]{:S(2)}, u32[]{:S(2)}) collective-permute-start(f32[5,32,128]{2,1,0:T(8,128)S(1)} %add_add_fusion.refs_0_), channel_id=1, source_target_pairs={{0,24},{8,16},{16,8},{24,0},{1,25},{9,17},{17,9},{25,1},{2,26},{10... | collective-permute-start | bytes 245768 | tf_op jit(solution)/shard_map/ppermute | solution.py:371
  87.3 2.7 %collective-permute-start.22 = (f32[5,32,128]{2,1,0:T(8,128)S(1)}, f32[5,32,128]{2,1,0:T(8,128)S(1)}, u32[]{:S(2)}, u32[]{:S(2)}) collective-permute-start(f32[5,32,128]{2,1,0:T(8,128)S(1)} %add_add_fusion.refs_0_), channel_id=1, source_target_pairs={{0,1},{1,0},{2,3},{3,2},{4,5},{5,4},{6,7},{7,6},{8,9},{9,8},{10,11... | collective-permute-start | bytes 245768 | tf_op jit(solution)/shard_map/ppermute | solution.py:371
  87.3 2.8 %collective-permute-start.23 = (f32[5,32,128]{2,1,0:T(8,128)S(1)}, f32[5,32,128]{2,1,0:T(8,128)S(1)}, u32[]{:S(2)}, u32[]{:S(2)}) collective-permute-start(f32[5,32,128]{2,1,0:T(8,128)S(1)} %collective-permute-done.19.refs_1_), channel_id=1, source_target_pairs={{0,1},{1,0},{2,3},{3,2},{4,5},{5,4},{6,7},{7,6},{8,9},{9,8},{10,11... | collective-permute-start | bytes 245768 | tf_op jit(solution)/shard_map/ppermute | solution.py:371
  87.8 2.3 %collective-permute-start.24 = (f32[5,32,128]{2,1,0:T(8,128)S(1)}, f32[5,32,128]{2,1,0:T(8,128)S(1)}, u32[]{:S(2)}, u32[]{:S(2)}) collective-permute-start(f32[5,32,128]{2,1,0:T(8,128)S(1)} %collective-permute-done.20.refs_2_), channel_id=1, source_target_pairs={{0,1},{1,0},{2,3},{3,2},{4,5},{5,4},{6,7},{7,6},{8,9},{9,8},{10,11... | collective-permute-start | bytes 245768 | tf_op jit(solution)/shard_map/ppermute | solution.py:371
  87.9 2.2 %collective-permute-start.25 = (f32[5,32,128]{2,1,0:T(8,128)S(1)}, f32[5,32,128]{2,1,0:T(8,128)S(1)}, u32[]{:S(2)}, u32[]{:S(2)}) collective-permute-start(f32[5,32,128]{2,1,0:T(8,128)S(1)} %collective-permute-done.21.refs_3_), channel_id=1, source_target_pairs={{0,1},{1,0},{2,3},{3,2},{4,5},{5,4},{6,7},{7,6},{8,9},{9,8},{10,11... | collective-permute-start | bytes 245768 | tf_op jit(solution)/shard_map/ppermute | solution.py:371

commit v3 on v2

--- a/solution.py
+++ b/solution.py
@@ -16,7 +16,7 @@
 F32 = jnp.float32
 BF16 = jnp.bfloat16
 VMEM = pl.BlockSpec(memory_space=pltpu.VMEM)
-HBM = pl.BlockSpec(memory_space=pl.ANY)
+HBM = pl.BlockSpec(memory_space=pltpu.HBM)
 BLOCKS = (((0, 0), (0, 1), (0, 2), (0, 3), (1, 1)), ((1, 2), (1, 3), (2, 2), (2, 3), (3, 3)))
 
 
@@ -30,6 +30,10 @@
 
 def near(x):
     return pltpu.with_memory_space_constraint(x, pltpu.VMEM)
+
+
+def far(x):
+    return pltpu.with_memory_space_constraint(x, pltpu.HBM)
 
 
 def pair(tile, p, lane):
@@ -132,7 +136,7 @@
         ],
         compiler_params=params(),
         name="conv_first",
-    )(x, cot)
+    )(far(x), far(cot))
 
 
 def more_kernel(depth, cp, taps, chunks, cot, v, *outs):
@@ -190,20 +194,21 @@
 
 
 def update_kernel(taps, cp, m_ref, *refs):
-    parts, outs = refs[:-2], refs[-2:]
+    parts, out = refs[:-1], refs[-1]
+    rows = taps * cp
     for c in range(2):
         grad = parts[c][...]
         for n in range(2 + c, len(parts), 2):
             grad = grad + parts[n][...]
-        outs[c][...] = update(m_ref[:, 256 * c : 256 * c + 256], grad, taps, cp)
+        out[rows * c : rows * c + rows, :] = update(m_ref[:, 256 * c : 256 * c + 256], grad, taps, cp)
 
 
 def momentum_update(own, parts, taps, cp):
     return pl.pallas_call(
         functools.partial(update_kernel, taps, cp),
-        out_shape=[pltpu.VMEM((taps * cp, 256), F32)] * 2,
+        out_shape=pltpu.VMEM((2 * taps * cp, 256), F32),
         in_specs=[VMEM] * (1 + len(parts)),
-        out_specs=[VMEM] * 2,
+        out_specs=VMEM,
         compiler_params=params(),
         name="momentum_update",
     )(near(own), *map(near, parts))
@@ -218,9 +223,10 @@
     return out
 
 
-def gram_kernel(ma, mb, keep, send):
-    dp, core = lax.axis_index("dp"), lax.axis_index("shard") % 2
-    gram = upper_gram(jnp.concatenate([ma[...], mb[...]], 1))
+def gram_kernel(m, keep, send):
+    z, core = lax.axis_index("shard") // 2, lax.axis_index("shard") % 2
+    rows = m.shape[0] // 2
+    gram = upper_gram(jnp.concatenate([m[:rows], m[rows:]], 1))
     for half in range(2):
         for n, (i, j) in enumerate(BLOCKS[half]):
             block = gram[i][:, 128 * (j - i) : 128 * (j - i) + 128]
@@ -229,52 +235,54 @@
 
                 @pl.when(core == half)
                 def _():
-                    keep[r ^ dp, n] = piece
+                    keep[r ^ z, n] = piece
 
                 @pl.when(core != half)
                 def _():
-                    send[r ^ dp, n] = piece
-
-
-def own_gram(ma, mb):
+                    send[r ^ z, n] = piece
+
+
+def own_gram(m):
     return pl.pallas_call(
         gram_kernel,
         out_shape=[pltpu.VMEM((4, 5, 32, 128), F32)] * 2,
-        in_specs=[VMEM] * 2,
+        in_specs=[VMEM],
         out_specs=[VMEM] * 2,
         compiler_params=params(),
         name="own_gram",
-    )(near(ma), near(mb))
-
-
-def any_gram_kernel(ma, mb, g_ref):
-    for i, rows in enumerate(upper_gram(jnp.concatenate([ma[...], mb[...]], 1))):
+    )(near(m))
+
+
+def any_gram_kernel(m, g_ref):
+    half = m.shape[0] // 2
+    for i, rows in enumerate(upper_gram(jnp.concatenate([m[:half], m[half:]], 1))):
         g_ref[128 * i : 128 * i + 128, :] = jnp.zeros((128, 512), F32)
         g_ref[128 * i : 128 * i + 128, 128 * i :] = rows
 
 
-def any_gram(ma, mb):
+def any_gram(m):
     return pl.pallas_call(
         any_gram_kernel,
         out_shape=jax.ShapeDtypeStruct((512, 512), F32),
-        in_specs=[VMEM] * 2,
+        in_specs=[VMEM],
         out_specs=VMEM,
         compiler_params=params(),
         name="own_gram",
-    )(near(ma), near(mb))
-
-
-def order_kernel(taps, cp, chans, known, *refs):
+    )(near(m))
+
+
+def order_kernel(taps, cp, chans, known, stacked, *refs):
     parts, (out, hi, lo, cols, sem) = refs[:-5], refs[-5:]
     copies = []
     for c in range(4):
         for r in range(len(parts) // 2):
             ref = parts[2 * r + c // 2]
-            for i in range(ref.shape[0] // cp):
+            base = ref.shape[0] // 2 * (c // 2) if stacked[r] else 0
+            for i in range(ref.shape[0] // cp // (2 if stacked[r] else 1)):
                 t = (lax.axis_index("dp") ^ r) * taps + i if known else i
                 if not known and i >= TAPS:
                     continue
-                rows = ref[cp * i : cp * i + chans, LANE * (c % 2) : LANE * (c % 2) + LANE]
+                rows = ref[base + cp * i : base + cp * i + chans, LANE * (c % 2) : LANE * (c % 2) + LANE]
 
                 @pl.when(t < TAPS)
                 def _():
@@ -289,8 +297,9 @@
 
 def order(parts, taps, cp, chans, known):
     rows = chans * TAPS
-    return pl.pallas_call(
-        functools.partial(order_kernel, taps, cp, chans, known),
+    stacked = [a is b for a, b in zip(parts[::2], parts[1::2])]
+    return pl.pallas_call(
+        functools.partial(order_kernel, taps, cp, chans, known, stacked),
         out_shape=[jax.ShapeDtypeStruct((rows, 512), F32)] + [pltpu.VMEM((rows, 512), BF16)] * 2,
         in_specs=[VMEM] * len(parts),
         out_specs=[HBM, VMEM, VMEM],
@@ -317,7 +326,7 @@
     if len(parts) == 1:
         g_ref[...] = parts[0][...]
     else:
-        dp, core = lax.axis_index("dp"), lax.axis_index("shard") % 2
+        z, core = lax.axis_index("shard") // 2, lax.axis_index("shard") % 2
         for n, part in enumerate(parts):
             which, r = divmod(n, 4)
             for half in range(2):
@@ -325,7 +334,7 @@
                 @pl.when(core ^ which == half)
                 def _():
                     for k, (i, j) in enumerate(BLOCKS[half]):
-                        rows = pl.ds(pl.multiple_of(128 * i + 32 * (dp ^ r), 32), 32)
+                        rows = pl.ds(pl.multiple_of(128 * i + 32 * (z ^ r), 32), 32)
                         g_ref[rows, 128 * j : 128 * j + 128] = part[k]
 
     for i in range(4):
@@ -383,6 +392,10 @@
     return swap(x, "shard", 8, 1)
 
 
+def over_z(x, r):
+    return swap(x, "shard", 8, 2 * r)
+
+
 def chunk_pair(a, b):
     def chunks():
         dp = lax.axis_index("dp")
@@ -403,17 +416,17 @@
     a2, b2 = over_y(a2 + a3), over_x(b2 + b3)
     a0, b0 = conv_more(cot, v, chunk_pair(0, 0), 1, taps, cp)
     own = own_momentum(momentum, taps, cp)
-    ma, mb = momentum_update(own, (a0, b0, a1, b1, a2, b2), taps, cp)
-    max_, mby = over_x(ma), over_y(mb)
-    keep, send = own_gram(ma, mb)
+    m = momentum_update(own, (a0, b0, a1, b1, a2, b2), taps, cp)
+    mx, my = over_x(m), over_y(m)
+    keep, send = own_gram(m)
     g = keep + over_core(send)
-    g = g[0] + over_x(g[1]) + over_y(g[2]) + swap(g[3], "dp", 4, 3)
-    ma_, mb_, max_, mby, g = lax.optimization_barrier((ma, mb, max_, mby, g))
-    may, mbx, mad, mbd = over_y(ma_), over_x(mb_), over_y(max_), over_x(mby)
-    g = g + swap(g, "shard", 8, 2) + swap(g, "shard", 8, 4) + swap(g, "shard", 8, 6)
-    g = [g] + [swap(g, "dp", 4, r) for r in (1, 2, 3)]
+    g = g[0] + over_z(g[1], 1) + over_z(g[2], 2) + over_z(g[3], 3)
+    g = (g + over_x(g)) + (over_y(g) + swap(g, "dp", 4, 3))
+    g = [g] + [over_z(g, r) for r in (1, 2, 3)]
     g = g + [over_core(x) for x in g]
-    momentum_new, hi, lo = order((ma, mb, max_, mbx, may, mby, mad, mbd), taps, cp, chans, True)
+    rows = taps * cp
+    ad, bd = over_y(mx[:rows]), over_x(my[rows:])
+    momentum_new, hi, lo = order((m, m, mx, mx, my, my, ad, bd), taps, cp, chans, True)
     return momentum_new, apply(hi, lo, g)
 
 
@@ -424,9 +437,10 @@
     x = jnp.pad(layer_input, ((0, cp - chans), (0, 0)))
     part = conv(x, cotangent, lambda: [list(range(n_dp))] * 2, n_dp, taps)[:2]
     grad = [lax.psum_scatter(p, "dp", scatter_dimension=0, tiled=True) for p in part]
-    ma, mb = momentum_update(own_momentum(momentum, taps, cp), grad, taps, cp)
-    gram = lax.psum(any_gram(ma, mb), ("dp", "shard"))
-    full = [lax.all_gather(m, "dp", axis=0, tiled=True) for m in (ma, mb)]
+    m = momentum_update(own_momentum(momentum, taps, cp), grad, taps, cp)
+    gram = lax.psum(any_gram(m), ("dp", "shard"))
+    rows = taps * cp
+    full = [lax.all_gather(half, "dp", axis=0, tiled=True) for half in (m[:rows], m[rows:])]
     momentum_new, hi, lo = order(full, taps, cp, chans, False)
     return momentum_new, apply(hi, lo, [gram])
 

time: 98.5 us -> 82.7 us (0.84)
  waiting for transfers between devices: 40.2 us -> 27.1 us
  local copies, waits for them, and re-layouts: 4.65 us -> 0.07 us
  Pallas kernels: 27.1 us -> 29.8 us
    ppermute x26 -> x24, waiting for transfers between devices: 40.2 us -> 27.1 us  [swap(): return lax.ppermute(x, axis, [(i, i ^ bit) for i in range(size)])]
    unnamed x6 -> x2, local copies, waits for them, and re-layouts: 4.63 us -> 0.01 us
    pallas_call x1, Pallas kernels: 6.09 us -> 8.8 us  [conv(): pl.pallas_call(functools.partial(conv_kernel, depth, cp, taps, chunks), o...]
    ppermute x26 -> x24, starting transfers between devices: 25.2 us -> 24.5 us  [swap(): return lax.ppermute(x, axis, [(i, i ^ bit) for i in range(size)])]
  transfers between devices with their start and end apart: 26 -> 24, of which waited for: 9 -> 11; matrix products, arithmetic and copies ran while one was open for 0% -> 0% of each run, Pallas kernels for 12% -> 14%
where the time goes in v3:
time: 82.7 us; the launch traced here: 82.6 us
  Pallas kernels  29.8 us (36%)
  waiting for transfers between devices  27.1 us (33%)
  starting transfers between devices  24.5 us (30%)
  between operations  0.97 us (1%)
    ppermute x24, waiting for transfers between devices, swap(): return lax.ppermute(x, axis, [(i, i ^ bit) for i in range(size)])  27.1 us
    ppermute x24, starting transfers between devices, swap(): return lax.ppermute(x, axis, [(i, i ^ bit) for i in range(size)])  24.5 us
    pallas_call x3, Pallas kernels, conv_more(): pl.pallas_call(functools.partial(more_kernel, depth, cp, taps, chunks), o...  9.3 us
    pallas_call x1, Pallas kernels, conv(): pl.pallas_call(functools.partial(conv_kernel, depth, cp, taps, chunks), o...  8.8 us
    pallas_call x1, Pallas kernels, apply(): pl.pallas_call(apply_kernel, out_shape=jax.ShapeDtypeStruct(hi.shape, F32...  8.03 us
    pallas_call x1, Pallas kernels, order(): pl.pallas_call(functools.partial(order_kernel, taps, cp, chans, known, st...  1.71 us
  transfers between devices with their start and end apart: 24, of which 11 were waited for; matrix products, arithmetic and copies ran while one was open for 0% of the time, Pallas kernels for 14%

profile of v3, /device:TPU:0, one launch (start us, length us, event | category | flops | bytes accessed | tf_op | source)
XLA Modules:
  0.0 82.6 jit_solution(15951476279533889282)
XLA Ops:
  0.6 8.8 %conv_first.1 = (f32[336,256]{1,0:T(8,128)S(1)}, f32[336,256]{1,0:T(8,128)S(1)}, bf16[8192,512]{1,0:T(8,128)(2,1)S(1)}, bf16[864,2304]{1,0:T(8,128)(2,1)S(1)}) custom-call(bf16[48,11560]{1,0:T(8,128)(2,1)} %x_hbm.1, bf16[8192,512]{1,0:T(8,128)(2,1)} %cot_hbm.1), custom_call_target="tpu_custom_call" | custom-call | tf_op jit(solution)/shard_map/conv_first/pallas_call | solution.py:125
  9.4 3.0 %collective-permute-start.4 = (f32[336,256]{1,0:T(8,128)S(1)}, f32[336,256]{1,0:T(8,128)S(1)}, u32[]{:S(2)}, u32[]{:S(2)}) collective-permute-start(f32[336,256]{1,0:T(8,128)S(1)} %get-tuple-element.26), channel_id=1, source_target_pairs={{0,16},{8,24},{16,0},{24,8},{1,17},{9,25},{17,1},{25,9},{2,18},{10... | collective-permute-start | bytes 1032200 | tf_op jit(solution)/shard_map/ppermute | solution.py:380
  12.5 1.5 %collective-permute-start.2 = (f32[336,256]{1,0:T(8,128)S(1)}, f32[336,256]{1,0:T(8,128)S(1)}, u32[]{:S(2)}, u32[]{:S(2)}) collective-permute-start(f32[336,256]{1,0:T(8,128)S(1)} %get-tuple-element.24), channel_id=1, source_target_pairs={{0,8},{8,0},{16,24},{24,16},{1,9},{9,1},{17,25},{25,17},{2,10},{10... | collective-permute-start | bytes 1032200 | tf_op jit(solution)/shard_map/ppermute | solution.py:380
  14.0 3.1 %conv_more.4 = (f32[336,256]{1,0:T(8,128)S(1)}, f32[336,256]{1,0:T(8,128)S(1)}) custom-call(bf16[8192,512]{1,0:T(8,128)(2,1)S(1)} %get-tuple-element.17.cot, bf16[864,2304]{1,0:T(8,128)(2,1)S(1)} %get-tuple-element.18.v), custom_call_target="tpu_custom_call" | custom-call | tf_op jit(solution)/shard_map/conv_more/pallas_call | solution.py:150
  17.1 0.7 collective-permute-start
  17.8 0.0 collective-permute-start.1
  17.8 3.1 %conv_more.5 = (f32[336,256]{1,0:T(8,128)S(1)}, f32[336,256]{1,0:T(8,128)S(1)}) custom-call(bf16[8192,512]{1,0:T(8,128)(2,1)S(1)} %get-tuple-element.17.cot, bf16[864,2304]{1,0:T(8,128)(2,1)S(1)} %get-tuple-element.18.v), custom_call_target="tpu_custom_call" | custom-call | tf_op jit(solution)/shard_map/conv_more/pallas_call | solution.py:150
  20.9 0.4 collective-permute-done.4
  21.4 2.1 %collective-permute-start.5 = (f32[336,256]{1,0:T(8,128)S(1)}, f32[336,256]{1,0:T(8,128)S(1)}, u32[]{:S(2)}, u32[]{:S(2)}) collective-permute-start(f32[336,256]{1,0:T(8,128)S(1)} %add.28), channel_id=1, source_target_pairs={{0,8},{8,0},{16,24},{24,16},{1,9},{9,1},{17,25},{25,17},{2,10},{10... | collective-permute-start | bytes 1032200 | tf_op jit(solution)/shard_map/ppermute | solution.py:380
  23.5 0.0 collective-permute-done.2
  23.5 0.0 copy-start
  23.6 1.6 %collective-permute-start.3 = (f32[336,256]{1,0:T(8,128)S(1)}, f32[336,256]{1,0:T(8,128)S(1)}, u32[]{:S(2)}, u32[]{:S(2)}) collective-permute-start(f32[336,256]{1,0:T(8,128)S(1)} %add.27), channel_id=1, source_target_pairs={{0,16},{8,24},{16,0},{24,8},{1,17},{9,25},{17,1},{25,9},{2,18},{10... | collective-permute-start | bytes 1032200 | tf_op jit(solution)/shard_map/ppermute | solution.py:380
  25.1 3.0 %conv_more.3 = (f32[336,256]{1,0:T(8,128)S(1)}, f32[336,256]{1,0:T(8,128)S(1)}) custom-call(bf16[8192,512]{1,0:T(8,128)(2,1)S(1)} %get-tuple-element.17.cot, bf16[864,2304]{1,0:T(8,128)(2,1)S(1)} %get-tuple-element.18.v), custom_call_target="tpu_custom_call" | custom-call | tf_op jit(solution)/shard_map/conv_more/pallas_call | solution.py:150
  28.2 0.0 copy-done
  28.2 0.6 own_momentum.1.m_ref
  28.8 2.1 %collective-permute-done.refs_2_ = f32[336,256]{1,0:T(8,128)S(1)} collective-permute-done((f32[336,256]{1,0:T(8,128)S(1)}, f32[336,256]{1,0:T(8,128)S(1)}, u32[]{:S(2)}, u32[]{:S(2)}) %collective-permute-start) | collective-permute-done | bytes 344096 | tf_op jit(solution)/shard_map/ppermute | solution.py:380
  30.8 0.0 collective-permute-done.1.refs_3_
  30.8 5.9 %collective-permute-done.5.refs_5_ = f32[336,256]{1,0:T(8,128)S(1)} collective-permute-done((f32[336,256]{1,0:T(8,128)S(1)}, f32[336,256]{1,0:T(8,128)S(1)}, u32[]{:S(2)}, u32[]{:S(2)}) %collective-permute-start.5) | collective-permute-done | bytes 344096 | tf_op jit(solution)/shard_map/ppermute | solution.py:380
  36.7 0.0 collective-permute-done.3.refs_4_
  36.7 0.2 momentum_update.1.refs_0_.refs_1_.m
  36.9 1.3 %own_gram.1 = (f32[4,5,32,128]{3,2,1,0:T(8,128)S(1)}, f32[4,5,32,128]{3,2,1,0:T(8,128)S(1)}) custom-call(f32[672,256]{1,0:T(8,128)S(1)} %momentum_update.1.refs_0_.refs_1_.m), custom_call_target="tpu_custom_call" | custom-call | tf_op jit(solution)/shard_map/own_gram/pallas_call | solution.py:246
  38.2 0.1 collective-permute-start.10
  38.2 1.6 %collective-permute-start.6 = (f32[672,256]{1,0:T(8,128)S(1)}, f32[672,256]{1,0:T(8,128)S(1)}, u32[]{:S(2)}, u32[]{:S(2)}) collective-permute-start(f32[672,256]{1,0:T(8,128)S(1)} %momentum_update.1.refs_0_.refs_1_.m), channel_id=1, source_target_pairs={{0,8},{8,0},{16,24},{24,16},{1,9},{9,1},{17,25},{25,17},{2,10},{10... | collective-permute-start | bytes 2064392 | tf_op jit(solution)/shard_map/ppermute | solution.py:380
  39.8 0.5 collective-permute-start.7
  40.3 0.0 collective-permute-done.10
  40.4 1.6 %collective-permute-start.11 = (f32[5,32,128]{2,1,0:T(8,128)S(1)}, f32[5,32,128]{2,1,0:T(8,128)S(1)}, u32[]{:S(2)}, u32[]{:S(2)}) collective-permute-start(f32[5,32,128]{2,1,0:T(8,128)S(1)} %get-tuple-element.32), channel_id=1, source_target_pairs={{0,2},{1,3},{2,0},{3,1},{4,6},{5,7},{6,4},{7,5},{8,10},{9,11},{10,... | collective-permute-start | bytes 245768 | tf_op jit(solution)/shard_map/ppermute | solution.py:380
  42.0 2.6 %collective-permute-start.12 = (f32[5,32,128]{2,1,0:T(8,128)S(1)}, f32[5,32,128]{2,1,0:T(8,128)S(1)}, u32[]{:S(2)}, u32[]{:S(2)}) collective-permute-start(f32[5,32,128]{2,1,0:T(8,128)S(1)} %get-tuple-element.34), channel_id=1, source_target_pairs={{0,4},{1,5},{2,6},{3,7},{4,0},{5,1},{6,2},{7,3},{8,12},{9,13},{10,... | collective-permute-start | bytes 245768 | tf_op jit(solution)/shard_map/ppermute | solution.py:380
  44.6 0.2 collective-permute-start.13
  44.8 0.1 collective-permute-done.11
  44.9 6.4 %collective-permute-done.12 = f32[5,32,128]{2,1,0:T(8,128)S(1)} collective-permute-done((f32[5,32,128]{2,1,0:T(8,128)S(1)}, f32[5,32,128]{2,1,0:T(8,128)S(1)}, u32[]{:S(2)}, u32[]{:S(2)}) %collective-permute-start.12) | collective-permute-done | bytes 81952 | tf_op jit(solution)/shard_map/ppermute | solution.py:380
  51.3 0.0 collective-permute-done.13
  51.3 1.3 %collective-permute-start.14 = (f32[5,32,128]{2,1,0:T(8,128)S(1)}, f32[5,32,128]{2,1,0:T(8,128)S(1)}, u32[]{:S(2)}, u32[]{:S(2)}) collective-permute-start(f32[5,32,128]{2,1,0:T(8,128)S(1)} %fusion.2), channel_id=1, source_target_pairs={{0,8},{8,0},{16,24},{24,16},{1,9},{9,1},{17,25},{25,17},{2,10},{10... | collective-permute-start | bytes 245768 | tf_op jit(solution)/shard_map/ppermute | solution.py:380
  52.6 0.8 collective-permute-start.15
  53.4 1.4 %collective-permute-start.16 = (f32[5,32,128]{2,1,0:T(8,128)S(1)}, f32[5,32,128]{2,1,0:T(8,128)S(1)}, u32[]{:S(2)}, u32[]{:S(2)}) collective-permute-start(f32[5,32,128]{2,1,0:T(8,128)S(1)} %fusion.2), channel_id=1, source_target_pairs={{0,24},{8,16},{16,8},{24,0},{1,25},{9,17},{17,9},{25,1},{2,26},{10... | collective-permute-start | bytes 245768 | tf_op jit(solution)/shard_map/ppermute | solution.py:380
  54.9 1.7 %collective-permute-done.6.refs_2_.refs_3_ = f32[672,256]{1,0:T(8,128)S(1)} collective-permute-done((f32[672,256]{1,0:T(8,128)S(1)}, f32[672,256]{1,0:T(8,128)S(1)}, u32[]{:S(2)}, u32[]{:S(2)}) %collective-permute-start.6) | collective-permute-done | bytes 688160 | tf_op jit(solution)/shard_map/ppermute | solution.py:380
  56.6 0.4 collective-permute-start.8
  57.0 2.8 %collective-permute-done.7.refs_4_.refs_5_ = f32[672,256]{1,0:T(8,128)S(1)} collective-permute-done((f32[672,256]{1,0:T(8,128)S(1)}, f32[672,256]{1,0:T(8,128)S(1)}, u32[]{:S(2)}, u32[]{:S(2)}) %collective-permute-start.7) | collective-permute-done | bytes 688160 | tf_op jit(solution)/shard_map/ppermute | solution.py:380
  59.9 0.1 collective-permute-start.9
  59.9 0.0 collective-permute-done.14
  60.0 1.6 %collective-permute-done.15 = f32[5,32,128]{2,1,0:T(8,128)S(1)} collective-permute-done((f32[5,32,128]{2,1,0:T(8,128)S(1)}, f32[5,32,128]{2,1,0:T(8,128)S(1)}, u32[]{:S(2)}, u32[]{:S(2)}) %collective-permute-start.15) | collective-permute-done | bytes 81952 | tf_op jit(solution)/shard_map/ppermute | solution.py:380
  61.6 0.0 collective-permute-done.16
  61.6 1.6 %collective-permute-start.17 = (f32[5,32,128]{2,1,0:T(8,128)S(1)}, f32[5,32,128]{2,1,0:T(8,128)S(1)}, u32[]{:S(2)}, u32[]{:S(2)}) collective-permute-start(f32[5,32,128]{2,1,0:T(8,128)S(1)} %add_add_fusion.refs_0_), channel_id=1, source_target_pairs={{0,2},{1,3},{2,0},{3,1},{4,6},{5,7},{6,4},{7,5},{8,10},{9,11},{10,... | collective-permute-start | bytes 245768 | tf_op jit(solution)/shard_map/ppermute | solution.py:380
  63.3 2.6 %collective-permute-start.18 = (f32[5,32,128]{2,1,0:T(8,128)S(1)}, f32[5,32,128]{2,1,0:T(8,128)S(1)}, u32[]{:S(2)}, u32[]{:S(2)}) collective-permute-start(f32[5,32,128]{2,1,0:T(8,128)S(1)} %add_add_fusion.refs_0_), channel_id=1, source_target_pairs={{0,4},{1,5},{2,6},{3,7},{4,0},{5,1},{6,2},{7,3},{8,12},{9,13},{10,... | collective-permute-start | bytes 245768 | tf_op jit(solution)/shard_map/ppermute | solution.py:380
  65.9 0.2 collective-permute-start.19
  66.1 0.7 collective-permute-done.17.refs_1_
  66.7 0.0 collective-permute-start.20
  66.7 3.6 %collective-permute-done.18.refs_2_ = f32[5,32,128]{2,1,0:T(8,128)S(1)} collective-permute-done((f32[5,32,128]{2,1,0:T(8,128)S(1)}, f32[5,32,128]{2,1,0:T(8,128)S(1)}, u32[]{:S(2)}, u32[]{:S(2)}) %collective-permute-start.18) | collective-permute-done | bytes 81952 | tf_op jit(solution)/shard_map/ppermute | solution.py:380
  70.4 0.0 collective-permute-start.21
  70.4 1.8 %collective-permute-done.19.refs_3_ = f32[5,32,128]{2,1,0:T(8,128)S(1)} collective-permute-done((f32[5,32,128]{2,1,0:T(8,128)S(1)}, f32[5,32,128]{2,1,0:T(8,128)S(1)}, u32[]{:S(2)}, u32[]{:S(2)}) %collective-permute-start.19) | collective-permute-done | bytes 81952 | tf_op jit(solution)/shard_map/ppermute | solution.py:380
  72.1 0.0 collective-permute-start.22
  72.1 0.0 collective-permute-done.8.refs_6_
  72.1 0.5 collective-permute-start.23
  72.6 0.0 collective-permute-done.9.refs_7_
  72.6 1.7 %weight_order.1 = (f32[1296,512]{1,0:T(8,128)}, bf16[1296,512]{1,0:T(8,128)(2,1)S(1)}, bf16[1296,512]{1,0:T(8,128)(2,1)S(1)}) custom-call(f32[672,256]{1,0:T(8,128)S(1)} %momentum_update.1.refs_0_.refs_1_.m, f32[672,256]{1,0:T(8,128)S(1)} %momentum_update.1.refs_0_.refs_1_.m, f32[672,256]{1,0:T(8,128)S(1)} %collective-permute-done.6.refs_2_.refs_3_, ...), custom_call_target="tpu_custom_call" | custom-call | tf_op jit(solution)/shard_map/weight_order/pallas_call | solution.py:301
  74.4 0.0 collective-permute-done.20.refs_4_
  74.4 0.0 collective-permute-done.21.refs_5_
  74.4 0.0 collective-permute-done.22.refs_6_
  74.4 0.0 collective-permute-done.23.refs_7_
  74.4 8.0 %newton_schulz.1 = f32[1296,512]{1,0:T(8,128)} custom-call(bf16[1296,512]{1,0:T(8,128)(2,1)S(1)} %get-tuple-element.28.hi, bf16[1296,512]{1,0:T(8,128)(2,1)S(1)} %get-tuple-element.29.lo, f32[5,32,128]{2,1,0:T(8,128)S(1)} %add_add_fusion.refs_0_, f32[5,32,128]{2,1,0:T(8,128)S(1)} %collective-permute-done.17.refs_1_, ...), custom_call_target="tpu_custom_call" | custom-call | tf_op jit(solution)/shard_map/newton_schulz/pallas_call | solution.py:368
  (8 shorter events, 0.2 us)
Async XLA Ops:
  9.4 11.9 %collective-permute-start.4 = (f32[336,256]{1,0:T(8,128)S(1)}, f32[336,256]{1,0:T(8,128)S(1)}, u32[]{:S(2)}, u32[]{:S(2)}) collective-permute-start(f32[336,256]{1,0:T(8,128)S(1)} %get-tuple-element.26), channel_id=1, source_target_pairs={{0,16},{8,24},{16,0},{24,8},{1,17},{9,25},{17,1},{25,9},{2,18},{10... | collective-permute-start | bytes 1032200 | tf_op jit(solution)/shard_map/ppermute | solution.py:380
  12.5 11.0 %collective-permute-start.2 = (f32[336,256]{1,0:T(8,128)S(1)}, f32[336,256]{1,0:T(8,128)S(1)}, u32[]{:S(2)}, u32[]{:S(2)}) collective-permute-start(f32[336,256]{1,0:T(8,128)S(1)} %get-tuple-element.24), channel_id=1, source_target_pairs={{0,8},{8,0},{16,24},{24,16},{1,9},{9,1},{17,25},{25,17},{2,10},{10... | collective-permute-start | bytes 1032200 | tf_op jit(solution)/shard_map/ppermute | solution.py:380
  17.1 13.7 %collective-permute-start = (f32[336,256]{1,0:T(8,128)S(1)}, f32[336,256]{1,0:T(8,128)S(1)}, u32[]{:S(2)}, u32[]{:S(2)}) collective-permute-start(f32[336,256]{1,0:T(8,128)S(1)} %get-tuple-element.21), channel_id=1, source_target_pairs={{0,8},{8,0},{16,24},{24,16},{1,9},{9,1},{17,25},{25,17},{2,10},{10... | collective-permute-start | bytes 1032200 | tf_op jit(solution)/shard_map/ppermute | solution.py:380
  17.8 13.1 %collective-permute-start.1 = (f32[336,256]{1,0:T(8,128)S(1)}, f32[336,256]{1,0:T(8,128)S(1)}, u32[]{:S(2)}, u32[]{:S(2)}) collective-permute-start(f32[336,256]{1,0:T(8,128)S(1)} %get-tuple-element.22), channel_id=1, source_target_pairs={{0,16},{8,24},{16,0},{24,8},{1,17},{9,25},{17,1},{25,9},{2,18},{10... | collective-permute-start | bytes 1032200 | tf_op jit(solution)/shard_map/ppermute | solution.py:380
  21.4 15.3 %collective-permute-start.5 = (f32[336,256]{1,0:T(8,128)S(1)}, f32[336,256]{1,0:T(8,128)S(1)}, u32[]{:S(2)}, u32[]{:S(2)}) collective-permute-start(f32[336,256]{1,0:T(8,128)S(1)} %add.28), channel_id=1, source_target_pairs={{0,8},{8,0},{16,24},{24,16},{1,9},{9,1},{17,25},{25,17},{2,10},{10... | collective-permute-start | bytes 1032200 | tf_op jit(solution)/shard_map/ppermute | solution.py:380
  23.5 4.6 %copy-start = (f32[1296,512]{1,0:T(8,128)S(1)}, f32[1296,512]{1,0:T(8,128)}, u32[]{:S(2)}) copy-start(f32[1296,512]{1,0:T(8,128)} %m_ref.1) | copy-start | bytes 7962628
  23.6 13.2 %collective-permute-start.3 = (f32[336,256]{1,0:T(8,128)S(1)}, f32[336,256]{1,0:T(8,128)S(1)}, u32[]{:S(2)}, u32[]{:S(2)}) collective-permute-start(f32[336,256]{1,0:T(8,128)S(1)} %add.27), channel_id=1, source_target_pairs={{0,16},{8,24},{16,0},{24,8},{1,17},{9,25},{17,1},{25,9},{2,18},{10... | collective-permute-start | bytes 1032200 | tf_op jit(solution)/shard_map/ppermute | solution.py:380
  38.2 2.1 %collective-permute-start.10 = (f32[4,5,32,128]{3,2,1,0:T(8,128)S(1)}, f32[4,5,32,128]{3,2,1,0:T(8,128)S(1)}, u32[]{:S(2)}, u32[]{:S(2)}) collective-permute-start(f32[4,5,32,128]{3,2,1,0:T(8,128)S(1)} %get-tuple-element.31), channel_id=1, source_target_pairs={{0,1},{1,0},{2,3},{3,2},{4,5},{5,4},{6,7},{7,6},{8,9},{9,8},{10,11... | collective-permute-start | bytes 983048 | tf_op jit(solution)/shard_map/ppermute | solution.py:380
  38.2 18.3 %collective-permute-start.6 = (f32[672,256]{1,0:T(8,128)S(1)}, f32[672,256]{1,0:T(8,128)S(1)}, u32[]{:S(2)}, u32[]{:S(2)}) collective-permute-start(f32[672,256]{1,0:T(8,128)S(1)} %momentum_update.1.refs_0_.refs_1_.m), channel_id=1, source_target_pairs={{0,8},{8,0},{16,24},{24,16},{1,9},{9,1},{17,25},{25,17},{2,10},{10... | collective-permute-start | bytes 2064392 | tf_op jit(solution)/shard_map/ppermute | solution.py:380
  39.8 20.0 %collective-permute-start.7 = (f32[672,256]{1,0:T(8,128)S(1)}, f32[672,256]{1,0:T(8,128)S(1)}, u32[]{:S(2)}, u32[]{:S(2)}) collective-permute-start(f32[672,256]{1,0:T(8,128)S(1)} %momentum_update.1.refs_0_.refs_1_.m), channel_id=1, source_target_pairs={{0,16},{8,24},{16,0},{24,8},{1,17},{9,25},{17,1},{25,9},{2,18},{10... | collective-permute-start | bytes 2064392 | tf_op jit(solution)/shard_map/ppermute | solution.py:380
  40.4 4.5 %collective-permute-start.11 = (f32[5,32,128]{2,1,0:T(8,128)S(1)}, f32[5,32,128]{2,1,0:T(8,128)S(1)}, u32[]{:S(2)}, u32[]{:S(2)}) collective-permute-start(f32[5,32,128]{2,1,0:T(8,128)S(1)} %get-tuple-element.32), channel_id=1, source_target_pairs={{0,2},{1,3},{2,0},{3,1},{4,6},{5,7},{6,4},{7,5},{8,10},{9,11},{10,... | collective-permute-start | bytes 245768 | tf_op jit(solution)/shard_map/ppermute | solution.py:380
  42.0 9.3 %collective-permute-start.12 = (f32[5,32,128]{2,1,0:T(8,128)S(1)}, f32[5,32,128]{2,1,0:T(8,128)S(1)}, u32[]{:S(2)}, u32[]{:S(2)}) collective-permute-start(f32[5,32,128]{2,1,0:T(8,128)S(1)} %get-tuple-element.34), channel_id=1, source_target_pairs={{0,4},{1,5},{2,6},{3,7},{4,0},{5,1},{6,2},{7,3},{8,12},{9,13},{10,... | collective-permute-start | bytes 245768 | tf_op jit(solution)/shard_map/ppermute | solution.py:380
  44.6 6.7 %collective-permute-start.13 = (f32[5,32,128]{2,1,0:T(8,128)S(1)}, f32[5,32,128]{2,1,0:T(8,128)S(1)}, u32[]{:S(2)}, u32[]{:S(2)}) collective-permute-start(f32[5,32,128]{2,1,0:T(8,128)S(1)} %get-tuple-element.33), channel_id=1, source_target_pairs={{0,6},{1,7},{2,4},{3,5},{4,2},{5,3},{6,0},{7,1},{8,14},{9,15},{10,... | collective-permute-start | bytes 245768 | tf_op jit(solution)/shard_map/ppermute | solution.py:380
  51.3 8.6 %collective-permute-start.14 = (f32[5,32,128]{2,1,0:T(8,128)S(1)}, f32[5,32,128]{2,1,0:T(8,128)S(1)}, u32[]{:S(2)}, u32[]{:S(2)}) collective-permute-start(f32[5,32,128]{2,1,0:T(8,128)S(1)} %fusion.2), channel_id=1, source_target_pairs={{0,8},{8,0},{16,24},{24,16},{1,9},{9,1},{17,25},{25,17},{2,10},{10... | collective-permute-start | bytes 245768 | tf_op jit(solution)/shard_map/ppermute | solution.py:380
  52.6 9.0 %collective-permute-start.15 = (f32[5,32,128]{2,1,0:T(8,128)S(1)}, f32[5,32,128]{2,1,0:T(8,128)S(1)}, u32[]{:S(2)}, u32[]{:S(2)}) collective-permute-start(f32[5,32,128]{2,1,0:T(8,128)S(1)} %fusion.2), channel_id=1, source_target_pairs={{0,16},{8,24},{16,0},{24,8},{1,17},{9,25},{17,1},{25,9},{2,18},{10... | collective-permute-start | bytes 245768 | tf_op jit(solution)/shard_map/ppermute | solution.py:380
  53.4 8.2 %collective-permute-start.16 = (f32[5,32,128]{2,1,0:T(8,128)S(1)}, f32[5,32,128]{2,1,0:T(8,128)S(1)}, u32[]{:S(2)}, u32[]{:S(2)}) collective-permute-start(f32[5,32,128]{2,1,0:T(8,128)S(1)} %fusion.2), channel_id=1, source_target_pairs={{0,24},{8,16},{16,8},{24,0},{1,25},{9,17},{17,9},{25,1},{2,26},{10... | collective-permute-start | bytes 245768 | tf_op jit(solution)/shard_map/ppermute | solution.py:380
  56.6 15.5 %collective-permute-start.8 = (f32[336,256]{1,0:T(8,128)S(1)}, f32[336,256]{1,0:T(8,128)S(1)}, u32[]{:S(2)}, u32[]{:S(2)}) collective-permute-start(f32[336,256]{1,0:T(8,128)S(1)} %slice.24), channel_id=1, source_target_pairs={{0,16},{8,24},{16,0},{24,8},{1,17},{9,25},{17,1},{25,9},{2,18},{10... | collective-permute-start | bytes 1032200 | tf_op jit(solution)/shard_map/ppermute | solution.py:380
  59.9 12.8 %collective-permute-start.9 = (f32[336,256]{1,0:T(8,128)S(1)}, f32[336,256]{1,0:T(8,128)S(1)}, u32[]{:S(2)}, u32[]{:S(2)}) collective-permute-start(f32[336,256]{1,0:T(8,128)S(1)} %slice.25), channel_id=1, source_target_pairs={{0,8},{8,0},{16,24},{24,16},{1,9},{9,1},{17,25},{25,17},{2,10},{10... | collective-permute-start | bytes 1032200 | tf_op jit(solution)/shard_map/ppermute | solution.py:380
  61.6 5.1 %collective-permute-start.17 = (f32[5,32,128]{2,1,0:T(8,128)S(1)}, f32[5,32,128]{2,1,0:T(8,128)S(1)}, u32[]{:S(2)}, u32[]{:S(2)}) collective-permute-start(f32[5,32,128]{2,1,0:T(8,128)S(1)} %add_add_fusion.refs_0_), channel_id=1, source_target_pairs={{0,2},{1,3},{2,0},{3,1},{4,6},{5,7},{6,4},{7,5},{8,10},{9,11},{10,... | collective-permute-start | bytes 245768 | tf_op jit(solution)/shard_map/ppermute | solution.py:380
  63.3 7.1 %collective-permute-start.18 = (f32[5,32,128]{2,1,0:T(8,128)S(1)}, f32[5,32,128]{2,1,0:T(8,128)S(1)}, u32[]{:S(2)}, u32[]{:S(2)}) collective-permute-start(f32[5,32,128]{2,1,0:T(8,128)S(1)} %add_add_fusion.refs_0_), channel_id=1, source_target_pairs={{0,4},{1,5},{2,6},{3,7},{4,0},{5,1},{6,2},{7,3},{8,12},{9,13},{10,... | collective-permute-start | bytes 245768 | tf_op jit(solution)/shard_map/ppermute | solution.py:380
  65.9 6.3 %collective-permute-start.19 = (f32[5,32,128]{2,1,0:T(8,128)S(1)}, f32[5,32,128]{2,1,0:T(8,128)S(1)}, u32[]{:S(2)}, u32[]{:S(2)}) collective-permute-start(f32[5,32,128]{2,1,0:T(8,128)S(1)} %add_add_fusion.refs_0_), channel_id=1, source_target_pairs={{0,6},{1,7},{2,4},{3,5},{4,2},{5,3},{6,0},{7,1},{8,14},{9,15},{10,... | collective-permute-start | bytes 245768 | tf_op jit(solution)/shard_map/ppermute | solution.py:380
  66.7 7.6 %collective-permute-start.20 = (f32[5,32,128]{2,1,0:T(8,128)S(1)}, f32[5,32,128]{2,1,0:T(8,128)S(1)}, u32[]{:S(2)}, u32[]{:S(2)}) collective-permute-start(f32[5,32,128]{2,1,0:T(8,128)S(1)} %add_add_fusion.refs_0_), channel_id=1, source_target_pairs={{0,1},{1,0},{2,3},{3,2},{4,5},{5,4},{6,7},{7,6},{8,9},{9,8},{10,11... | collective-permute-start | bytes 245768 | tf_op jit(solution)/shard_map/ppermute | solution.py:380
  70.4 4.0 %collective-permute-start.21 = (f32[5,32,128]{2,1,0:T(8,128)S(1)}, f32[5,32,128]{2,1,0:T(8,128)S(1)}, u32[]{:S(2)}, u32[]{:S(2)}) collective-permute-start(f32[5,32,128]{2,1,0:T(8,128)S(1)} %collective-permute-done.17.refs_1_), channel_id=1, source_target_pairs={{0,1},{1,0},{2,3},{3,2},{4,5},{5,4},{6,7},{7,6},{8,9},{9,8},{10,11... | collective-permute-start | bytes 245768 | tf_op jit(solution)/shard_map/ppermute | solution.py:380
  72.1 2.3 %collective-permute-start.22 = (f32[5,32,128]{2,1,0:T(8,128)S(1)}, f32[5,32,128]{2,1,0:T(8,128)S(1)}, u32[]{:S(2)}, u32[]{:S(2)}) collective-permute-start(f32[5,32,128]{2,1,0:T(8,128)S(1)} %collective-permute-done.18.refs_2_), channel_id=1, source_target_pairs={{0,1},{1,0},{2,3},{3,2},{4,5},{5,4},{6,7},{7,6},{8,9},{9,8},{10,11... | collective-permute-start | bytes 245768 | tf_op jit(solution)/shard_map/ppermute | solution.py:380
  72.1 2.3 %collective-permute-start.23 = (f32[5,32,128]{2,1,0:T(8,128)S(1)}, f32[5,32,128]{2,1,0:T(8,128)S(1)}, u32[]{:S(2)}, u32[]{:S(2)}) collective-permute-start(f32[5,32,128]{2,1,0:T(8,128)S(1)} %collective-permute-done.19.refs_3_), channel_id=1, source_target_pairs={{0,1},{1,0},{2,3},{3,2},{4,5},{5,4},{6,7},{7,6},{8,9},{9,8},{10,11... | collective-permute-start | bytes 245768 | tf_op jit(solution)/shard_map/ppermute | solution.py:380

commit v4 on v3

--- a/solution.py
+++ b/solution.py
@@ -17,7 +17,8 @@
 BF16 = jnp.bfloat16
 VMEM = pl.BlockSpec(memory_space=pltpu.VMEM)
 HBM = pl.BlockSpec(memory_space=pltpu.HBM)
-BLOCKS = (((0, 0), (0, 1), (0, 2), (0, 3), (1, 1)), ((1, 2), (1, 3), (2, 2), (2, 3), (3, 3)))
+BLOCKS = (((0, 1), (0, 2), (0, 3)), ((1, 2), (1, 3), (2, 3)))
+PIECE = (136, 128)
 
 
 def column(rows):
@@ -49,23 +50,22 @@
     return jnp.where(lane < c, near, tile(t))
 
 
-def build_slab(d0, half, xs, tail, v, cp):
+def build_slab(d0, half, g, xs, tail, v, cp):
     lane = lax.broadcasted_iota(jnp.int32, (16, LANE), 1)
     last = xs.shape[1] // LANE
-    for g in range(cp // 16):
-        rows = slice(16 * g, 16 * g + 16)
-
-        def tile(t):
-            return tail[rows, :] if t == last else xs[rows, LANE * t : LANE * t + LANE]
-
-        for j in range(18):
-            for kw in range(3):
-                part = []
-                for s1 in range(2):
-                    p = (d0 + half * s1) * PW * PW + PW * j + kw
-                    part.append(pltpu.roll(pair(tile, p, lane), (64 * s1 - p) % LANE, 1))
-                r0 = (d0 * 3 + kw) * cp + 16 * g
-                v[r0 : r0 + 16, LANE * j : LANE * j + LANE] = jnp.where(lane < 64, part[0], part[1])
+    rows = slice(16 * g, 16 * g + 16)
+
+    def tile(t):
+        return tail[rows, :] if t == last else xs[rows, LANE * t : LANE * t + LANE]
+
+    for j in range(18):
+        for kw in range(3):
+            part = []
+            for s1 in range(2):
+                p = (d0 + half * s1) * PW * PW + PW * j + kw
+                part.append(pltpu.roll(pair(tile, p, lane), (64 * s1 - p) % LANE, 1))
+            r0 = (d0 * 3 + kw) * cp + 16 * g
+            v[r0 : r0 + 16, LANE * j : LANE * j + LANE] = jnp.where(lane < 64, part[0], part[1])
 
 
 def conv_part(d, half, taps, cp, qs, cot, v, outs):
@@ -97,21 +97,25 @@
     half = depth // 2
     ln = xs.shape[1]
     vox = HW * HW
-    xcopy = pltpu.make_async_copy(x_hbm, xs, xsem)
-    xcopy.start()
+    groups = [pl.ds(16 * g, 16) for g in range(cp // 16)]
+    xcopies = [pltpu.make_async_copy(x_hbm.at[r], xs.at[r], xsem.at[g]) for g, r in enumerate(groups)]
+    for copy in xcopies:
+        copy.start()
     copies = []
     for i in range(depth):
         rows = pl.ds(i * vox, vox)
         copies.append(pltpu.make_async_copy(cot_hbm.at[rows], cot.at[rows], csem.at[i]))
-    for d in range(half):
-        for s1 in range(2):
-            copies[d + half * s1].start()
-    xcopy.wait()
     n = ln // LANE * LANE
-    if n < ln:
-        tail[:, : ln - n] = xs[:, n:]
-    for d0 in range(half + 2):
-        build_slab(d0, half, xs, tail, v, cp)
+    for g, copy in enumerate(xcopies):
+        copy.wait()
+        if g == 0:
+            for d in range(half):
+                for s1 in range(2):
+                    copies[d + half * s1].start()
+        if n < ln:
+            tail[16 * g : 16 * g + 16, : ln - n] = xs[16 * g : 16 * g + 16, n:]
+        for d0 in range(half + 2):
+            build_slab(d0, half, g, xs, tail, v, cp)
     qs = chunks()
     for d in range(half):
         for s1 in range(2):
@@ -131,7 +135,7 @@
         scratch_shapes=[
             pltpu.VMEM((cp, ln), BF16),
             pltpu.VMEM((cp, LANE), BF16),
-            pltpu.SemaphoreType.DMA,
+            pltpu.SemaphoreType.DMA((cp // 16,)),
             pltpu.SemaphoreType.DMA((depth,)),
         ],
         compiler_params=params(),
@@ -227,25 +231,32 @@
     z, core = lax.axis_index("shard") // 2, lax.axis_index("shard") % 2
     rows = m.shape[0] // 2
     gram = upper_gram(jnp.concatenate([m[:rows], m[rows:]], 1))
+    row = lax.broadcasted_iota(jnp.int32, (128, 128), 0)
+    col = lax.broadcasted_iota(jnp.int32, (128, 128), 1)
     for half in range(2):
-        for n, (i, j) in enumerate(BLOCKS[half]):
-            block = gram[i][:, 128 * (j - i) : 128 * (j - i) + 128]
-            for r in range(4):
-                piece = block[32 * r : 32 * r + 32]
-
-                @pl.when(core == half)
-                def _():
-                    keep[r ^ z, n] = piece
-
-                @pl.when(core != half)
-                def _():
-                    send[r ^ z, n] = piece
+        blocks = [gram[i][:, 128 * (j - i) : 128 * (j - i) + 128] for i, j in BLOCKS[half]]
+        even, odd = gram[2 * half][:, :128], gram[2 * half + 1][:, :128]
+        blocks.append(jnp.where(row <= col, even, odd))
+        diag = jnp.where(row == col, odd, 0.0)
+        for r in range(4):
+            cut = slice(32 * r, 32 * r + 32)
+            last = jnp.sum(diag[cut], axis=0, keepdims=True)
+            last = jnp.where(row[:8] == 0, jnp.broadcast_to(last, (8, 128)), 0.0)
+            piece = jnp.concatenate([block[cut] for block in blocks] + [last], 0)
+
+            @pl.when(core == half)
+            def _():
+                keep[r ^ z] = piece
+
+            @pl.when(core != half)
+            def _():
+                send[r ^ z] = piece
 
 
 def own_gram(m):
     return pl.pallas_call(
         gram_kernel,
-        out_shape=[pltpu.VMEM((4, 5, 32, 128), F32)] * 2,
+        out_shape=[pltpu.VMEM((4,) + PIECE, F32)] * 2,
         in_specs=[VMEM],
         out_specs=[VMEM] * 2,
         compiler_params=params(),
@@ -322,20 +333,33 @@
 
 
 def apply_kernel(hi, lo, *refs):
-    parts, (out, g_ref, acc, sem) = refs[:-4], refs[-4:]
+    parts, (out, g_ref, p_ref, d_ref, acc, sem) = refs[:-6], refs[-6:]
     if len(parts) == 1:
         g_ref[...] = parts[0][...]
     else:
         z, core = lax.axis_index("shard") // 2, lax.axis_index("shard") % 2
         for n, part in enumerate(parts):
-            which, r = divmod(n, 4)
+            which, r = n // 4, 3 - n % 4
+            q = z ^ r
             for half in range(2):
 
                 @pl.when(core ^ which == half)
                 def _():
                     for k, (i, j) in enumerate(BLOCKS[half]):
-                        rows = pl.ds(pl.multiple_of(128 * i + 32 * (z ^ r), 32), 32)
-                        g_ref[rows, 128 * j : 128 * j + 128] = part[k]
+                        rows = pl.ds(pl.multiple_of(128 * i + 32 * q, 32), 32)
+                        g_ref[rows, 128 * j : 128 * j + 128] = part[32 * k : 32 * k + 32]
+                    p_ref[half, pl.ds(pl.multiple_of(32 * q, 32), 32), :] = part[96:128]
+                    d_ref[half, 8 * r : 8 * r + 8, :] = part[128:136]
+
+        row = lax.broadcasted_iota(jnp.int32, (128, 128), 0)
+        col = lax.broadcasted_iota(jnp.int32, (128, 128), 1)
+        for half in range(2):
+            up = p_ref[half]
+            down = up.T
+            odd = jnp.broadcast_to(jnp.sum(d_ref[half], axis=0, keepdims=True), (128, 128))
+            a = 256 * half
+            g_ref[a : a + 128, a : a + 128] = jnp.where(row <= col, up, down)
+            g_ref[a + 128 : a + 256, a + 128 : a + 256] = jnp.where(row > col, up, jnp.where(row < col, down, odd))
 
     for i in range(4):
         for j in range(i + 1, 4):
@@ -370,7 +394,13 @@
         out_shape=jax.ShapeDtypeStruct(hi.shape, F32),
         in_specs=[VMEM] * (2 + len(parts)),
         out_specs=HBM,
-        scratch_shapes=[pltpu.VMEM((512, 512), F32), pltpu.VMEM(hi.shape, F32), pltpu.SemaphoreType.DMA((3,))],
+        scratch_shapes=[
+            pltpu.VMEM((512, 512), F32),
+            pltpu.VMEM((2, 128, 128), F32),
+            pltpu.VMEM((2, 32, 128), F32),
+            pltpu.VMEM(hi.shape, F32),
+            pltpu.SemaphoreType.DMA((3,)),
+        ],
         compiler_params=params(),
         name="newton_schulz",
     )(near(hi), near(lo), *map(near, parts))
@@ -420,9 +450,12 @@
     mx, my = over_x(m), over_y(m)
     keep, send = own_gram(m)
     g = keep + over_core(send)
-    g = g[0] + over_z(g[1], 1) + over_z(g[2], 2) + over_z(g[3], 3)
-    g = (g + over_x(g)) + (over_y(g) + swap(g, "dp", 4, 3))
-    g = [g] + [over_z(g, r) for r in (1, 2, 3)]
+    z3, z2, z1 = [over_z(g[r], r) for r in (3, 2, 1)]
+    g = (z3 + z2) + (z1 + g[0])
+    d3, d1, d2 = [swap(g, "dp", 4, r) for r in (3, 1, 2)]
+    g = (d3 + d2) + (d1 + g)
+    z3, z2, z1 = [over_z(g, r) for r in (3, 2, 1)]
+    g = [z3, z2, z1, g]
     g = g + [over_core(x) for x in g]
     rows = taps * cp
     ad, bd = over_y(mx[:rows]), over_x(my[rows:])

time: 82.7 us -> 78.3 us (0.947)
  waiting for transfers between devices: 27.1 us -> 24.5 us
  Pallas kernels: 29.8 us -> 27.5 us
    ppermute x24, waiting for transfers between devices: 27.1 us -> 24.5 us  [swap(): return lax.ppermute(x, axis, [(i, i ^ bit) for i in range(size)])]
    pallas_call x1, Pallas kernels: 8.8 us -> 6.53 us  [conv(): pl.pallas_call(functools.partial(conv_kernel, depth, cp, taps, chunks), o...]
  transfers between devices with their start and end apart: 24 -> 24, of which waited for: 11 -> 10; matrix products, arithmetic and copies ran while one was open for 0% -> 0% of each run, Pallas kernels for 14% -> 15%
where the time goes in v4:
time: 78.3 us; the launch traced here: 78.2 us
  Pallas kernels  27.5 us (35%)
  starting transfers between devices  25.1 us (32%)
  waiting for transfers between devices  24.5 us (31%)
  between operations  0.95 us (1%)
    ppermute x24, starting transfers between devices, swap(): return lax.ppermute(x, axis, [(i, i ^ bit) for i in range(size)])  25.1 us
    ppermute x24, waiting for transfers between devices, swap(): return lax.ppermute(x, axis, [(i, i ^ bit) for i in range(size)])  24.5 us
    pallas_call x3, Pallas kernels, conv_more(): pl.pallas_call(functools.partial(more_kernel, depth, cp, taps, chunks), o...  9.3 us
    pallas_call x1, Pallas kernels, apply(): pl.pallas_call(apply_kernel, out_shape=jax.ShapeDtypeStruct(hi.shape, F32...  8.11 us
    pallas_call x1, Pallas kernels, conv(): pl.pallas_call(functools.partial(conv_kernel, depth, cp, taps, chunks), o...  6.53 us
    pallas_call x1, Pallas kernels, order(): pl.pallas_call(functools.partial(order_kernel, taps, cp, chans, known, st...  1.71 us
  transfers between devices with their start and end apart: 24, of which 10 were waited for; matrix products, arithmetic and copies ran while one was open for 0% of the time, Pallas kernels for 15%

profile of v4, /device:TPU:0, one launch (start us, length us, event | category | flops | bytes accessed | tf_op | source)
XLA Modules:
  0.0 78.2 jit_solution(2127890240171143733)
XLA Ops:
  0.6 6.5 %conv_first.1 = (f32[336,256]{1,0:T(8,128)S(1)}, f32[336,256]{1,0:T(8,128)S(1)}, bf16[8192,512]{1,0:T(8,128)(2,1)S(1)}, bf16[864,2304]{1,0:T(8,128)(2,1)S(1)}) custom-call(bf16[48,11560]{1,0:T(8,128)(2,1)} %x_hbm.1, bf16[8192,512]{1,0:T(8,128)(2,1)} %cot_hbm.1), custom_call_target="tpu_custom_call" | custom-call | tf_op jit(solution)/shard_map/conv_first/pallas_call | solution.py:129
  7.2 3.0 %collective-permute-start.4 = (f32[336,256]{1,0:T(8,128)S(1)}, f32[336,256]{1,0:T(8,128)S(1)}, u32[]{:S(2)}, u32[]{:S(2)}) collective-permute-start(f32[336,256]{1,0:T(8,128)S(1)} %get-tuple-element.26), channel_id=1, source_target_pairs={{0,16},{8,24},{16,0},{24,8},{1,17},{9,25},{17,1},{25,9},{2,18},{10... | collective-permute-start | bytes 1032200 | tf_op jit(solution)/shard_map/ppermute | solution.py:410
  10.2 1.5 %collective-permute-start.2 = (f32[336,256]{1,0:T(8,128)S(1)}, f32[336,256]{1,0:T(8,128)S(1)}, u32[]{:S(2)}, u32[]{:S(2)}) collective-permute-start(f32[336,256]{1,0:T(8,128)S(1)} %get-tuple-element.24), channel_id=1, source_target_pairs={{0,8},{8,0},{16,24},{24,16},{1,9},{9,1},{17,25},{25,17},{2,10},{10... | collective-permute-start | bytes 1032200 | tf_op jit(solution)/shard_map/ppermute | solution.py:410
  11.7 3.1 %conv_more.4 = (f32[336,256]{1,0:T(8,128)S(1)}, f32[336,256]{1,0:T(8,128)S(1)}) custom-call(bf16[8192,512]{1,0:T(8,128)(2,1)S(1)} %get-tuple-element.17.cot, bf16[864,2304]{1,0:T(8,128)(2,1)S(1)} %get-tuple-element.18.v), custom_call_target="tpu_custom_call" | custom-call | tf_op jit(solution)/shard_map/conv_more/pallas_call | solution.py:154
  14.8 0.7 collective-permute-start
  15.5 0.0 collective-permute-start.1
  15.5 3.1 %conv_more.5 = (f32[336,256]{1,0:T(8,128)S(1)}, f32[336,256]{1,0:T(8,128)S(1)}) custom-call(bf16[8192,512]{1,0:T(8,128)(2,1)S(1)} %get-tuple-element.17.cot, bf16[864,2304]{1,0:T(8,128)(2,1)S(1)} %get-tuple-element.18.v), custom_call_target="tpu_custom_call" | custom-call | tf_op jit(solution)/shard_map/conv_more/pallas_call | solution.py:154
  18.7 0.4 collective-permute-done.4
  19.1 2.1 %collective-permute-start.5 = (f32[336,256]{1,0:T(8,128)S(1)}, f32[336,256]{1,0:T(8,128)S(1)}, u32[]{:S(2)}, u32[]{:S(2)}) collective-permute-start(f32[336,256]{1,0:T(8,128)S(1)} %add.28), channel_id=1, source_target_pairs={{0,8},{8,0},{16,24},{24,16},{1,9},{9,1},{17,25},{25,17},{2,10},{10... | collective-permute-start | bytes 1032200 | tf_op jit(solution)/shard_map/ppermute | solution.py:410
  21.2 0.0 collective-permute-done.2
  21.3 0.0 copy-start
  21.3 1.6 %collective-permute-start.3 = (f32[336,256]{1,0:T(8,128)S(1)}, f32[336,256]{1,0:T(8,128)S(1)}, u32[]{:S(2)}, u32[]{:S(2)}) collective-permute-start(f32[336,256]{1,0:T(8,128)S(1)} %add.27), channel_id=1, source_target_pairs={{0,16},{8,24},{16,0},{24,8},{1,17},{9,25},{17,1},{25,9},{2,18},{10... | collective-permute-start | bytes 1032200 | tf_op jit(solution)/shard_map/ppermute | solution.py:410
  22.9 3.0 %conv_more.3 = (f32[336,256]{1,0:T(8,128)S(1)}, f32[336,256]{1,0:T(8,128)S(1)}) custom-call(bf16[8192,512]{1,0:T(8,128)(2,1)S(1)} %get-tuple-element.17.cot, bf16[864,2304]{1,0:T(8,128)(2,1)S(1)} %get-tuple-element.18.v), custom_call_target="tpu_custom_call" | custom-call | tf_op jit(solution)/shard_map/conv_more/pallas_call | solution.py:154
  25.9 0.0 copy-done
  25.9 0.6 own_momentum.1.m_ref
  26.5 2.1 %collective-permute-done.refs_2_ = f32[336,256]{1,0:T(8,128)S(1)} collective-permute-done((f32[336,256]{1,0:T(8,128)S(1)}, f32[336,256]{1,0:T(8,128)S(1)}, u32[]{:S(2)}, u32[]{:S(2)}) %collective-permute-start) | collective-permute-done | bytes 344096 | tf_op jit(solution)/shard_map/ppermute | solution.py:410
  28.6 0.0 collective-permute-done.1.refs_3_
  28.6 5.9 %collective-permute-done.5.refs_5_ = f32[336,256]{1,0:T(8,128)S(1)} collective-permute-done((f32[336,256]{1,0:T(8,128)S(1)}, f32[336,256]{1,0:T(8,128)S(1)}, u32[]{:S(2)}, u32[]{:S(2)}) %collective-permute-start.5) | collective-permute-done | bytes 344096 | tf_op jit(solution)/shard_map/ppermute | solution.py:410
  34.5 0.0 collective-permute-done.3.refs_4_
  34.5 0.2 momentum_update.1.refs_0_.refs_1_.m
  34.6 1.1 %own_gram.1 = (f32[4,136,128]{2,1,0:T(8,128)S(1)}, f32[4,136,128]{2,1,0:T(8,128)S(1)}) custom-call(f32[672,256]{1,0:T(8,128)S(1)} %momentum_update.1.refs_0_.refs_1_.m), custom_call_target="tpu_custom_call" | custom-call | tf_op jit(solution)/shard_map/own_gram/pallas_call | solution.py:257
  35.7 0.1 collective-permute-start.10
  35.8 1.6 %collective-permute-start.6 = (f32[672,256]{1,0:T(8,128)S(1)}, f32[672,256]{1,0:T(8,128)S(1)}, u32[]{:S(2)}, u32[]{:S(2)}) collective-permute-start(f32[672,256]{1,0:T(8,128)S(1)} %momentum_update.1.refs_0_.refs_1_.m), channel_id=1, source_target_pairs={{0,8},{8,0},{16,24},{24,16},{1,9},{9,1},{17,25},{25,17},{2,10},{10... | collective-permute-start | bytes 2064392 | tf_op jit(solution)/shard_map/ppermute | solution.py:410
  37.4 0.5 collective-permute-start.7
  37.9 0.0 collective-permute-done.10
  37.9 3.7 %collective-permute-start.11 = (f32[136,128]{1,0:T(8,128)S(1)}, f32[136,128]{1,0:T(8,128)S(1)}, u32[]{:S(2)}, u32[]{:S(2)}) collective-permute-start(f32[136,128]{1,0:T(8,128)S(1)} %get-tuple-element.34), channel_id=1, source_target_pairs={{0,6},{1,7},{2,4},{3,5},{4,2},{5,3},{6,0},{7,1},{8,14},{9,15},{10,... | collective-permute-start | bytes 208904 | tf_op jit(solution)/shard_map/ppermute | solution.py:410
  41.6 0.0 collective-permute-start.12
  41.6 0.8 collective-permute-start.13
  42.4 2.2 %collective-permute-done.11 = f32[136,128]{1,0:T(8,128)S(1)} collective-permute-done((f32[136,128]{1,0:T(8,128)S(1)}, f32[136,128]{1,0:T(8,128)S(1)}, u32[]{:S(2)}, u32[]{:S(2)}) %collective-permute-start.11) | collective-permute-done | bytes 69664 | tf_op jit(solution)/shard_map/ppermute | solution.py:410
  44.6 3.0 %collective-permute-done.12 = f32[136,128]{1,0:T(8,128)S(1)} collective-permute-done((f32[136,128]{1,0:T(8,128)S(1)}, f32[136,128]{1,0:T(8,128)S(1)}, u32[]{:S(2)}, u32[]{:S(2)}) %collective-permute-start.12) | collective-permute-done | bytes 69664 | tf_op jit(solution)/shard_map/ppermute | solution.py:410
  47.6 0.0 collective-permute-done.13
  47.6 1.6 %collective-permute-start.14 = (f32[136,128]{1,0:T(8,128)S(1)}, f32[136,128]{1,0:T(8,128)S(1)}, u32[]{:S(2)}, u32[]{:S(2)}) collective-permute-start(f32[136,128]{1,0:T(8,128)S(1)} %fusion.1), channel_id=1, source_target_pairs={{0,24},{8,16},{16,8},{24,0},{1,25},{9,17},{17,9},{25,1},{2,26},{10... | collective-permute-start | bytes 208904 | tf_op jit(solution)/shard_map/ppermute | solution.py:410
  49.1 1.2 %collective-permute-start.15 = (f32[136,128]{1,0:T(8,128)S(1)}, f32[136,128]{1,0:T(8,128)S(1)}, u32[]{:S(2)}, u32[]{:S(2)}) collective-permute-start(f32[136,128]{1,0:T(8,128)S(1)} %fusion.1), channel_id=1, source_target_pairs={{0,16},{8,24},{16,0},{24,8},{1,17},{9,25},{17,1},{25,9},{2,18},{10... | collective-permute-start | bytes 208904 | tf_op jit(solution)/shard_map/ppermute | solution.py:410
  50.3 0.8 %collective-permute-start.16 = (f32[136,128]{1,0:T(8,128)S(1)}, f32[136,128]{1,0:T(8,128)S(1)}, u32[]{:S(2)}, u32[]{:S(2)}) collective-permute-start(f32[136,128]{1,0:T(8,128)S(1)} %fusion.1), channel_id=1, source_target_pairs={{0,8},{8,0},{16,24},{24,16},{1,9},{9,1},{17,25},{25,17},{2,10},{10... | collective-permute-start | bytes 208904 | tf_op jit(solution)/shard_map/ppermute | solution.py:410
  51.1 3.0 %collective-permute-done.6.refs_2_.refs_3_ = f32[672,256]{1,0:T(8,128)S(1)} collective-permute-done((f32[672,256]{1,0:T(8,128)S(1)}, f32[672,256]{1,0:T(8,128)S(1)}, u32[]{:S(2)}, u32[]{:S(2)}) %collective-permute-start.6) | collective-permute-done | bytes 688160 | tf_op jit(solution)/shard_map/ppermute | solution.py:410
  54.1 0.4 collective-permute-start.8
  54.6 2.6 %collective-permute-done.7.refs_4_.refs_5_ = f32[672,256]{1,0:T(8,128)S(1)} collective-permute-done((f32[672,256]{1,0:T(8,128)S(1)}, f32[672,256]{1,0:T(8,128)S(1)}, u32[]{:S(2)}, u32[]{:S(2)}) %collective-permute-start.7) | collective-permute-done | bytes 688160 | tf_op jit(solution)/shard_map/ppermute | solution.py:410
  57.2 0.6 collective-permute-start.9
  57.8 0.0 collective-permute-done.14
  57.8 0.9 %collective-permute-done.15 = f32[136,128]{1,0:T(8,128)S(1)} collective-permute-done((f32[136,128]{1,0:T(8,128)S(1)}, f32[136,128]{1,0:T(8,128)S(1)}, u32[]{:S(2)}, u32[]{:S(2)}) %collective-permute-start.15) | collective-permute-done | bytes 69664 | tf_op jit(solution)/shard_map/ppermute | solution.py:410
  58.6 0.0 collective-permute-done.16
  58.6 3.7 %collective-permute-start.17 = (f32[136,128]{1,0:T(8,128)S(1)}, f32[136,128]{1,0:T(8,128)S(1)}, u32[]{:S(2)}, u32[]{:S(2)}) collective-permute-start(f32[136,128]{1,0:T(8,128)S(1)} %add_add_fusion.refs_3_), channel_id=1, source_target_pairs={{0,6},{1,7},{2,4},{3,5},{4,2},{5,3},{6,0},{7,1},{8,14},{9,15},{10,... | collective-permute-start | bytes 208904 | tf_op jit(solution)/shard_map/ppermute | solution.py:410
  62.3 0.0 collective-permute-start.18
  62.3 0.8 %collective-permute-start.19 = (f32[136,128]{1,0:T(8,128)S(1)}, f32[136,128]{1,0:T(8,128)S(1)}, u32[]{:S(2)}, u32[]{:S(2)}) collective-permute-start(f32[136,128]{1,0:T(8,128)S(1)} %add_add_fusion.refs_3_), channel_id=1, source_target_pairs={{0,2},{1,3},{2,0},{3,1},{4,6},{5,7},{6,4},{7,5},{8,10},{9,11},{10,... | collective-permute-start | bytes 208904 | tf_op jit(solution)/shard_map/ppermute | solution.py:410
  63.1 1.7 %collective-permute-done.17.refs_0_ = f32[136,128]{1,0:T(8,128)S(1)} collective-permute-done((f32[136,128]{1,0:T(8,128)S(1)}, f32[136,128]{1,0:T(8,128)S(1)}, u32[]{:S(2)}, u32[]{:S(2)}) %collective-permute-start.17) | collective-permute-done | bytes 69664 | tf_op jit(solution)/shard_map/ppermute | solution.py:410
  64.8 0.0 collective-permute-start.23
  64.8 2.7 %collective-permute-done.18.refs_1_ = f32[136,128]{1,0:T(8,128)S(1)} collective-permute-done((f32[136,128]{1,0:T(8,128)S(1)}, f32[136,128]{1,0:T(8,128)S(1)}, u32[]{:S(2)}, u32[]{:S(2)}) %collective-permute-start.18) | collective-permute-done | bytes 69664 | tf_op jit(solution)/shard_map/ppermute | solution.py:410
  67.6 0.0 collective-permute-start.20
  67.6 0.0 collective-permute-done.19.refs_2_
  67.6 0.5 collective-permute-start.21
  68.1 0.0 collective-permute-done.8.refs_6_
  68.1 0.1 collective-permute-start.22
  68.2 0.0 collective-permute-done.9.refs_7_
  68.2 1.7 %weight_order.1 = (f32[1296,512]{1,0:T(8,128)}, bf16[1296,512]{1,0:T(8,128)(2,1)S(1)}, bf16[1296,512]{1,0:T(8,128)(2,1)S(1)}) custom-call(f32[672,256]{1,0:T(8,128)S(1)} %momentum_update.1.refs_0_.refs_1_.m, f32[672,256]{1,0:T(8,128)S(1)} %momentum_update.1.refs_0_.refs_1_.m, f32[672,256]{1,0:T(8,128)S(1)} %collective-permute-done.6.refs_2_.refs_3_, ...), custom_call_target="tpu_custom_call" | custom-call | tf_op jit(solution)/shard_map/weight_order/pallas_call | solution.py:312
  69.9 0.0 collective-permute-done.23.refs_7_
  69.9 0.0 collective-permute-done.20.refs_4_
  69.9 0.0 collective-permute-done.21.refs_5_
  69.9 0.0 collective-permute-done.22.refs_6_
  69.9 8.1 %newton_schulz.1 = f32[1296,512]{1,0:T(8,128)} custom-call(bf16[1296,512]{1,0:T(8,128)(2,1)S(1)} %get-tuple-element.28.hi, bf16[1296,512]{1,0:T(8,128)(2,1)S(1)} %get-tuple-element.29.lo, f32[136,128]{1,0:T(8,128)S(1)} %collective-permute-done.17.refs_0_, f32[136,128]{1,0:T(8,128)S(1)} %collective-permute-done.18.refs_1_, ...), custom_call_target="tpu_custom_call" | custom-call | tf_op jit(solution)/shard_map/newton_schulz/pallas_call | solution.py:392
  (8 shorter events, 0.2 us)
Async XLA Ops:
  7.2 11.9 %collective-permute-start.4 = (f32[336,256]{1,0:T(8,128)S(1)}, f32[336,256]{1,0:T(8,128)S(1)}, u32[]{:S(2)}, u32[]{:S(2)}) collective-permute-start(f32[336,256]{1,0:T(8,128)S(1)} %get-tuple-element.26), channel_id=1, source_target_pairs={{0,16},{8,24},{16,0},{24,8},{1,17},{9,25},{17,1},{25,9},{2,18},{10... | collective-permute-start | bytes 1032200 | tf_op jit(solution)/shard_map/ppermute | solution.py:410
  10.2 11.0 %collective-permute-start.2 = (f32[336,256]{1,0:T(8,128)S(1)}, f32[336,256]{1,0:T(8,128)S(1)}, u32[]{:S(2)}, u32[]{:S(2)}) collective-permute-start(f32[336,256]{1,0:T(8,128)S(1)} %get-tuple-element.24), channel_id=1, source_target_pairs={{0,8},{8,0},{16,24},{24,16},{1,9},{9,1},{17,25},{25,17},{2,10},{10... | collective-permute-start | bytes 1032200 | tf_op jit(solution)/shard_map/ppermute | solution.py:410
  14.8 13.7 %collective-permute-start = (f32[336,256]{1,0:T(8,128)S(1)}, f32[336,256]{1,0:T(8,128)S(1)}, u32[]{:S(2)}, u32[]{:S(2)}) collective-permute-start(f32[336,256]{1,0:T(8,128)S(1)} %get-tuple-element.21), channel_id=1, source_target_pairs={{0,8},{8,0},{16,24},{24,16},{1,9},{9,1},{17,25},{25,17},{2,10},{10... | collective-permute-start | bytes 1032200 | tf_op jit(solution)/shard_map/ppermute | solution.py:410
  15.5 13.1 %collective-permute-start.1 = (f32[336,256]{1,0:T(8,128)S(1)}, f32[336,256]{1,0:T(8,128)S(1)}, u32[]{:S(2)}, u32[]{:S(2)}) collective-permute-start(f32[336,256]{1,0:T(8,128)S(1)} %get-tuple-element.22), channel_id=1, source_target_pairs={{0,16},{8,24},{16,0},{24,8},{1,17},{9,25},{17,1},{25,9},{2,18},{10... | collective-permute-start | bytes 1032200 | tf_op jit(solution)/shard_map/ppermute | solution.py:410
  19.1 15.3 %collective-permute-start.5 = (f32[336,256]{1,0:T(8,128)S(1)}, f32[336,256]{1,0:T(8,128)S(1)}, u32[]{:S(2)}, u32[]{:S(2)}) collective-permute-start(f32[336,256]{1,0:T(8,128)S(1)} %add.28), channel_id=1, source_target_pairs={{0,8},{8,0},{16,24},{24,16},{1,9},{9,1},{17,25},{25,17},{2,10},{10... | collective-permute-start | bytes 1032200 | tf_op jit(solution)/shard_map/ppermute | solution.py:410
  21.3 4.6 %copy-start = (f32[1296,512]{1,0:T(8,128)S(1)}, f32[1296,512]{1,0:T(8,128)}, u32[]{:S(2)}) copy-start(f32[1296,512]{1,0:T(8,128)} %m_ref.1) | copy-start | bytes 7962628
  21.3 13.2 %collective-permute-start.3 = (f32[336,256]{1,0:T(8,128)S(1)}, f32[336,256]{1,0:T(8,128)S(1)}, u32[]{:S(2)}, u32[]{:S(2)}) collective-permute-start(f32[336,256]{1,0:T(8,128)S(1)} %add.27), channel_id=1, source_target_pairs={{0,16},{8,24},{16,0},{24,8},{1,17},{9,25},{17,1},{25,9},{2,18},{10... | collective-permute-start | bytes 1032200 | tf_op jit(solution)/shard_map/ppermute | solution.py:410
  35.7 2.1 %collective-permute-start.10 = (f32[4,136,128]{2,1,0:T(8,128)S(1)}, f32[4,136,128]{2,1,0:T(8,128)S(1)}, u32[]{:S(2)}, u32[]{:S(2)}) collective-permute-start(f32[4,136,128]{2,1,0:T(8,128)S(1)} %get-tuple-element.31), channel_id=1, source_target_pairs={{0,1},{1,0},{2,3},{3,2},{4,5},{5,4},{6,7},{7,6},{8,9},{9,8},{10,11... | collective-permute-start | bytes 835592 | tf_op jit(solution)/shard_map/ppermute | solution.py:410
  35.8 18.3 %collective-permute-start.6 = (f32[672,256]{1,0:T(8,128)S(1)}, f32[672,256]{1,0:T(8,128)S(1)}, u32[]{:S(2)}, u32[]{:S(2)}) collective-permute-start(f32[672,256]{1,0:T(8,128)S(1)} %momentum_update.1.refs_0_.refs_1_.m), channel_id=1, source_target_pairs={{0,8},{8,0},{16,24},{24,16},{1,9},{9,1},{17,25},{25,17},{2,10},{10... | collective-permute-start | bytes 2064392 | tf_op jit(solution)/shard_map/ppermute | solution.py:410
  37.4 19.8 %collective-permute-start.7 = (f32[672,256]{1,0:T(8,128)S(1)}, f32[672,256]{1,0:T(8,128)S(1)}, u32[]{:S(2)}, u32[]{:S(2)}) collective-permute-start(f32[672,256]{1,0:T(8,128)S(1)} %momentum_update.1.refs_0_.refs_1_.m), channel_id=1, source_target_pairs={{0,16},{8,24},{16,0},{24,8},{1,17},{9,25},{17,1},{25,9},{2,18},{10... | collective-permute-start | bytes 2064392 | tf_op jit(solution)/shard_map/ppermute | solution.py:410
  37.9 6.6 %collective-permute-start.11 = (f32[136,128]{1,0:T(8,128)S(1)}, f32[136,128]{1,0:T(8,128)S(1)}, u32[]{:S(2)}, u32[]{:S(2)}) collective-permute-start(f32[136,128]{1,0:T(8,128)S(1)} %get-tuple-element.34), channel_id=1, source_target_pairs={{0,6},{1,7},{2,4},{3,5},{4,2},{5,3},{6,0},{7,1},{8,14},{9,15},{10,... | collective-permute-start | bytes 208904 | tf_op jit(solution)/shard_map/ppermute | solution.py:410
  41.6 6.0 %collective-permute-start.12 = (f32[136,128]{1,0:T(8,128)S(1)}, f32[136,128]{1,0:T(8,128)S(1)}, u32[]{:S(2)}, u32[]{:S(2)}) collective-permute-start(f32[136,128]{1,0:T(8,128)S(1)} %get-tuple-element.32), channel_id=1, source_target_pairs={{0,4},{1,5},{2,6},{3,7},{4,0},{5,1},{6,2},{7,3},{8,12},{9,13},{10,... | collective-permute-start | bytes 208904 | tf_op jit(solution)/shard_map/ppermute | solution.py:410
  41.6 6.0 %collective-permute-start.13 = (f32[136,128]{1,0:T(8,128)S(1)}, f32[136,128]{1,0:T(8,128)S(1)}, u32[]{:S(2)}, u32[]{:S(2)}) collective-permute-start(f32[136,128]{1,0:T(8,128)S(1)} %get-tuple-element.33), channel_id=1, source_target_pairs={{0,2},{1,3},{2,0},{3,1},{4,6},{5,7},{6,4},{7,5},{8,10},{9,11},{10,... | collective-permute-start | bytes 208904 | tf_op jit(solution)/shard_map/ppermute | solution.py:410
  47.6 10.2 %collective-permute-start.14 = (f32[136,128]{1,0:T(8,128)S(1)}, f32[136,128]{1,0:T(8,128)S(1)}, u32[]{:S(2)}, u32[]{:S(2)}) collective-permute-start(f32[136,128]{1,0:T(8,128)S(1)} %fusion.1), channel_id=1, source_target_pairs={{0,24},{8,16},{16,8},{24,0},{1,25},{9,17},{17,9},{25,1},{2,26},{10... | collective-permute-start | bytes 208904 | tf_op jit(solution)/shard_map/ppermute | solution.py:410
  49.1 9.5 %collective-permute-start.15 = (f32[136,128]{1,0:T(8,128)S(1)}, f32[136,128]{1,0:T(8,128)S(1)}, u32[]{:S(2)}, u32[]{:S(2)}) collective-permute-start(f32[136,128]{1,0:T(8,128)S(1)} %fusion.1), channel_id=1, source_target_pairs={{0,16},{8,24},{16,0},{24,8},{1,17},{9,25},{17,1},{25,9},{2,18},{10... | collective-permute-start | bytes 208904 | tf_op jit(solution)/shard_map/ppermute | solution.py:410
  50.3 8.3 %collective-permute-start.16 = (f32[136,128]{1,0:T(8,128)S(1)}, f32[136,128]{1,0:T(8,128)S(1)}, u32[]{:S(2)}, u32[]{:S(2)}) collective-permute-start(f32[136,128]{1,0:T(8,128)S(1)} %fusion.1), channel_id=1, source_target_pairs={{0,8},{8,0},{16,24},{24,16},{1,9},{9,1},{17,25},{25,17},{2,10},{10... | collective-permute-start | bytes 208904 | tf_op jit(solution)/shard_map/ppermute | solution.py:410
  54.1 13.9 %collective-permute-start.8 = (f32[336,256]{1,0:T(8,128)S(1)}, f32[336,256]{1,0:T(8,128)S(1)}, u32[]{:S(2)}, u32[]{:S(2)}) collective-permute-start(f32[336,256]{1,0:T(8,128)S(1)} %slice.24), channel_id=1, source_target_pairs={{0,16},{8,24},{16,0},{24,8},{1,17},{9,25},{17,1},{25,9},{2,18},{10... | collective-permute-start | bytes 1032200 | tf_op jit(solution)/shard_map/ppermute | solution.py:410
  57.2 11.0 %collective-permute-start.9 = (f32[336,256]{1,0:T(8,128)S(1)}, f32[336,256]{1,0:T(8,128)S(1)}, u32[]{:S(2)}, u32[]{:S(2)}) collective-permute-start(f32[336,256]{1,0:T(8,128)S(1)} %slice.25), channel_id=1, source_target_pairs={{0,8},{8,0},{16,24},{24,16},{1,9},{9,1},{17,25},{25,17},{2,10},{10... | collective-permute-start | bytes 1032200 | tf_op jit(solution)/shard_map/ppermute | solution.py:410
  58.6 6.2 %collective-permute-start.17 = (f32[136,128]{1,0:T(8,128)S(1)}, f32[136,128]{1,0:T(8,128)S(1)}, u32[]{:S(2)}, u32[]{:S(2)}) collective-permute-start(f32[136,128]{1,0:T(8,128)S(1)} %add_add_fusion.refs_3_), channel_id=1, source_target_pairs={{0,6},{1,7},{2,4},{3,5},{4,2},{5,3},{6,0},{7,1},{8,14},{9,15},{10,... | collective-permute-start | bytes 208904 | tf_op jit(solution)/shard_map/ppermute | solution.py:410
  62.3 5.3 %collective-permute-start.18 = (f32[136,128]{1,0:T(8,128)S(1)}, f32[136,128]{1,0:T(8,128)S(1)}, u32[]{:S(2)}, u32[]{:S(2)}) collective-permute-start(f32[136,128]{1,0:T(8,128)S(1)} %add_add_fusion.refs_3_), channel_id=1, source_target_pairs={{0,4},{1,5},{2,6},{3,7},{4,0},{5,1},{6,2},{7,3},{8,12},{9,13},{10,... | collective-permute-start | bytes 208904 | tf_op jit(solution)/shard_map/ppermute | solution.py:410
  62.3 5.3 %collective-permute-start.19 = (f32[136,128]{1,0:T(8,128)S(1)}, f32[136,128]{1,0:T(8,128)S(1)}, u32[]{:S(2)}, u32[]{:S(2)}) collective-permute-start(f32[136,128]{1,0:T(8,128)S(1)} %add_add_fusion.refs_3_), channel_id=1, source_target_pairs={{0,2},{1,3},{2,0},{3,1},{4,6},{5,7},{6,4},{7,5},{8,10},{9,11},{10,... | collective-permute-start | bytes 208904 | tf_op jit(solution)/shard_map/ppermute | solution.py:410
  64.8 5.1 %collective-permute-start.23 = (f32[136,128]{1,0:T(8,128)S(1)}, f32[136,128]{1,0:T(8,128)S(1)}, u32[]{:S(2)}, u32[]{:S(2)}) collective-permute-start(f32[136,128]{1,0:T(8,128)S(1)} %add_add_fusion.refs_3_), channel_id=1, source_target_pairs={{0,1},{1,0},{2,3},{3,2},{4,5},{5,4},{6,7},{7,6},{8,9},{9,8},{10,11... | collective-permute-start | bytes 208904 | tf_op jit(solution)/shard_map/ppermute | solution.py:410
  67.6 2.3 %collective-permute-start.20 = (f32[136,128]{1,0:T(8,128)S(1)}, f32[136,128]{1,0:T(8,128)S(1)}, u32[]{:S(2)}, u32[]{:S(2)}) collective-permute-start(f32[136,128]{1,0:T(8,128)S(1)} %collective-permute-done.17.refs_0_), channel_id=1, source_target_pairs={{0,1},{1,0},{2,3},{3,2},{4,5},{5,4},{6,7},{7,6},{8,9},{9,8},{10,11... | collective-permute-start | bytes 208904 | tf_op jit(solution)/shard_map/ppermute | solution.py:410
  67.6 2.3 %collective-permute-start.21 = (f32[136,128]{1,0:T(8,128)S(1)}, f32[136,128]{1,0:T(8,128)S(1)}, u32[]{:S(2)}, u32[]{:S(2)}) collective-permute-start(f32[136,128]{1,0:T(8,128)S(1)} %collective-permute-done.18.refs_1_), channel_id=1, source_target_pairs={{0,1},{1,0},{2,3},{3,2},{4,5},{5,4},{6,7},{7,6},{8,9},{9,8},{10,11... | collective-permute-start | bytes 208904 | tf_op jit(solution)/shard_map/ppermute | solution.py:410
  68.1 1.8 %collective-permute-start.22 = (f32[136,128]{1,0:T(8,128)S(1)}, f32[136,128]{1,0:T(8,128)S(1)}, u32[]{:S(2)}, u32[]{:S(2)}) collective-permute-start(f32[136,128]{1,0:T(8,128)S(1)} %collective-permute-done.19.refs_2_), channel_id=1, source_target_pairs={{0,1},{1,0},{2,3},{3,2},{4,5},{5,4},{6,7},{7,6},{8,9},{9,8},{10,11... | collective-permute-start | bytes 208904 | tf_op jit(solution)/shard_map/ppermute | solution.py:410

commit v5 on v4

--- a/solution.py
+++ b/solution.py
@@ -282,42 +282,23 @@
     )(near(m))
 
 
-def order_kernel(taps, cp, chans, known, stacked, *refs):
-    parts, (out, hi, lo, cols, sem) = refs[:-5], refs[-5:]
-    copies = []
-    for c in range(4):
-        for r in range(len(parts) // 2):
-            ref = parts[2 * r + c // 2]
-            base = ref.shape[0] // 2 * (c // 2) if stacked[r] else 0
-            for i in range(ref.shape[0] // cp // (2 if stacked[r] else 1)):
-                t = (lax.axis_index("dp") ^ r) * taps + i if known else i
-                if not known and i >= TAPS:
-                    continue
-                rows = ref[base + cp * i : base + cp * i + chans, LANE * (c % 2) : LANE * (c % 2) + LANE]
-
-                @pl.when(t < TAPS)
-                def _():
-                    cols.at[c][pl.ds(t, chans, stride=TAPS), :] = rows
-
-        copies.append(pltpu.make_async_copy(cols.at[c], out.at[:, pl.ds(LANE * c, LANE)], sem.at[c]))
-        copies[c].start()
-        hi[:, LANE * c : LANE * c + LANE], lo[:, LANE * c : LANE * c + LANE] = split(cols[c])
-    for copy in copies:
-        copy.wait()
-
-
-def order(parts, taps, cp, chans, known):
-    rows = chans * TAPS
-    stacked = [a is b for a, b in zip(parts[::2], parts[1::2])]
-    return pl.pallas_call(
-        functools.partial(order_kernel, taps, cp, chans, known, stacked),
-        out_shape=[jax.ShapeDtypeStruct((rows, 512), F32)] + [pltpu.VMEM((rows, 512), BF16)] * 2,
-        in_specs=[VMEM] * len(parts),
-        out_specs=[HBM, VMEM, VMEM],
-        scratch_shapes=[pltpu.VMEM((4, rows, LANE), F32), pltpu.SemaphoreType.DMA((4,))],
-        compiler_params=params(),
-        name="weight_order",
-    )(*map(near, parts))
+def second_kernel(more, m, mx, my, nx, ny):
+    rows = m.shape[0] // 2
+    nx[: rows - more, :] = m[rows + more :, :]
+    nx[rows - more :, :] = my[more:, :]
+    ny[: rows - more, :] = m[: rows - more, :]
+    ny[rows - more :, :] = mx[:rows, :]
+
+
+def second_step(m, mx, my, more):
+    return pl.pallas_call(
+        functools.partial(second_kernel, more),
+        out_shape=[pltpu.VMEM((m.shape[0] - more, 256), F32)] * 2,
+        in_specs=[VMEM] * 3,
+        out_specs=[VMEM] * 2,
+        compiler_params=params(),
+        name="second_step",
+    )(near(m), near(mx), near(my))
 
 
 def mm(a, b):
@@ -327,13 +308,8 @@
     return d(ah, bh) + (d(ah, bl) + d(al, bh))
 
 
-def row_cuts(rows):
-    cuts = [min(rows, -(-rows * k // 24) * 8) for k in range(4)]
-    return [(a, b) for a, b in zip(cuts, cuts[1:]) if b > a]
-
-
-def apply_kernel(hi, lo, *refs):
-    parts, (out, g_ref, p_ref, d_ref, acc, sem) = refs[:-6], refs[-6:]
+def poly_kernel(*refs):
+    parts, (qh, ql, g_ref, p_ref, d_ref) = refs[:-5], refs[-5:]
     if len(parts) == 1:
         g_ref[...] = parts[0][...]
     else:
@@ -378,32 +354,81 @@
     g2 = mm(split(mm(gs, p1s)), p1s)
     g2s = split(g2)
     p2 = jnp.where(diag, A1, 0.0) + B1 * g2 + C1 * mm(g2s, g2s)
-    qs = split(mm(p1s, split(p2)) * (scale * jnp.sqrt(F32(ROWS))))
-    copies = []
-    for k, (a, b) in enumerate(row_cuts(hi.shape[0])):
-        acc[a:b, :] = mm((hi[a:b, :], lo[a:b, :]), qs)
-        copies.append(pltpu.make_async_copy(acc.at[pl.ds(a, b - a)], out.at[pl.ds(a, b - a)], sem.at[k]))
-        copies[k].start()
-    for copy in copies:
-        copy.wait()
-
-
-def apply(hi, lo, parts):
-    return pl.pallas_call(
-        apply_kernel,
-        out_shape=jax.ShapeDtypeStruct(hi.shape, F32),
-        in_specs=[VMEM] * (2 + len(parts)),
-        out_specs=HBM,
+    qh[...], ql[...] = split(mm(p1s, split(p2)) * (scale * jnp.sqrt(F32(ROWS))))
+
+
+def newton_schulz(parts):
+    return pl.pallas_call(
+        poly_kernel,
+        out_shape=[pltpu.VMEM((512, 512), BF16)] * 2,
+        in_specs=[VMEM] * len(parts),
+        out_specs=[VMEM] * 2,
         scratch_shapes=[
             pltpu.VMEM((512, 512), F32),
             pltpu.VMEM((2, 128, 128), F32),
             pltpu.VMEM((2, 32, 128), F32),
-            pltpu.VMEM(hi.shape, F32),
+        ],
+        compiler_params=params(),
+        name="newton_schulz",
+    )(*map(near, parts))
+
+
+def finish_kernel(taps, cp, chans, known, places, qh, ql, *refs):
+    parts, (new, out, cols, hi, lo, acc, sem, osem) = refs[:-8], refs[-8:]
+    copies = []
+    for c in range(4):
+        for r in range(len(places) // 2):
+            i = 0
+            for n, base in places[2 * r + c // 2]:
+                ends = [b for m, b in sum(places, []) if m == n and b > base] + [parts[n].shape[0]]
+                for at in range(base, min(ends), cp):
+                    if i >= taps:
+                        break
+                    t = (lax.axis_index("dp") ^ r) * taps + i if known else r * taps + i
+                    i += 1
+                    if not known and t >= TAPS:
+                        continue
+                    rows = parts[n][at : at + chans, LANE * (c % 2) : LANE * (c % 2) + LANE]
+
+                    @pl.when(t < TAPS)
+                    def _():
+                        cols.at[c][pl.ds(t, chans, stride=TAPS), :] = rows
+
+            assert i == taps
+        copies.append(pltpu.make_async_copy(cols.at[c], new.at[:, pl.ds(LANE * c, LANE)], sem.at[c]))
+        copies[c].start()
+        hi[:, LANE * c : LANE * c + LANE], lo[:, LANE * c : LANE * c + LANE] = split(cols[c])
+    for k, (a, b) in enumerate(row_cuts(acc.shape[0])):
+        acc[a:b, :] = mm((hi[a:b, :], lo[a:b, :]), (qh[...], ql[...]))
+        copies.append(pltpu.make_async_copy(acc.at[pl.ds(a, b - a)], out.at[pl.ds(a, b - a)], osem.at[k]))
+        copies[-1].start()
+    for copy in copies:
+        copy.wait()
+
+
+def row_cuts(rows):
+    cuts = [min(rows, -(-rows * k // 24) * 8) for k in range(4)]
+    return [(a, b) for a, b in zip(cuts, cuts[1:]) if b > a]
+
+
+def finish(q, parts, places, taps, cp, chans, known):
+    rows = chans * TAPS
+    return pl.pallas_call(
+        functools.partial(finish_kernel, taps, cp, chans, known, list(places)),
+        out_shape=[jax.ShapeDtypeStruct((rows, 512), F32)] * 2,
+        in_specs=[VMEM] * (2 + len(parts)),
+        out_specs=[HBM] * 2,
+        scratch_shapes=[
+            pltpu.VMEM((4, rows, LANE), F32),
+            pltpu.VMEM((rows, 512), BF16),
+            pltpu.VMEM((rows, 512), BF16),
+            pltpu.VMEM((rows, 512), F32),
+            pltpu.SemaphoreType.DMA((4,)),
             pltpu.SemaphoreType.DMA((3,)),
         ],
         compiler_params=params(),
-        name="newton_schulz",
-    )(near(hi), near(lo), *map(near, parts))
+        name="finish",
+    )(*map(near, q), *map(near, parts))
 
 
 def swap(x, axis, size, bit):
@@ -447,7 +472,9 @@
     a0, b0 = conv_more(cot, v, chunk_pair(0, 0), 1, taps, cp)
     own = own_momentum(momentum, taps, cp)
     m = momentum_update(own, (a0, b0, a1, b1, a2, b2), taps, cp)
-    mx, my = over_x(m), over_y(m)
+    rows = taps * cp
+    more = 4 * cp
+    mx, my = over_x(m[: rows + more]), over_y(m[rows - more :])
     keep, send = own_gram(m)
     g = keep + over_core(send)
     z3, z2, z1 = [over_z(g[r], r) for r in (3, 2, 1)]
@@ -457,10 +484,16 @@
     z3, z2, z1 = [over_z(g, r) for r in (3, 2, 1)]
     g = [z3, z2, z1, g]
     g = g + [over_core(x) for x in g]
-    rows = taps * cp
-    ad, bd = over_y(mx[:rows]), over_x(my[rows:])
-    momentum_new, hi, lo = order((m, m, mx, mx, my, my, ad, bd), taps, cp, chans, True)
-    return momentum_new, apply(hi, lo, g)
+    nx, ny = second_step(m, mx, my, more)
+    nx, ny = over_x(nx), over_y(ny)
+    rest = rows - more
+    places = (
+        [(0, 0)], [(0, rows)],
+        [(1, 0)], [(1, rows), (3, 0)],
+        [(4, 0), (2, 0)], [(2, more)],
+        [(4, rest)], [(3, rest)],
+    )
+    return finish(newton_schulz(g), (m, mx, my, nx, ny), places, taps, cp, chans, True)
 
 
 def body_any(n_dp, layer_input, cotangent, momentum):
@@ -474,8 +507,8 @@
     gram = lax.psum(any_gram(m), ("dp", "shard"))
     rows = taps * cp
     full = [lax.all_gather(half, "dp", axis=0, tiled=True) for half in (m[:rows], m[rows:])]
-    momentum_new, hi, lo = order(full, taps, cp, chans, False)
-    return momentum_new, apply(hi, lo, [gram])
+    places = [[(half, r * rows)] for r in range(n_dp) for half in range(2)]
+    return finish(newton_schulz([gram]), full, places, taps, cp, chans, False)
 
 
 def solution(mesh):

time: 78.3 us -> 75.2 us (0.960)
  waiting for transfers between devices: 24.5 us -> 22.9 us
  starting transfers between devices: 25.1 us -> 24.1 us
    ppermute x24, waiting for transfers between devices: 24.5 us -> 22.9 us  [swap(): return lax.ppermute(x, axis, [(i, i ^ bit) for i in range(size)])]
    ppermute x24, starting transfers between devices: 25.1 us -> 24.1 us  [swap(): return lax.ppermute(x, axis, [(i, i ^ bit) for i in range(size)])]
    pallas_call x2 -> x3, Pallas kernels: 9.81 us -> 9.14 us  [the longest x1 5.06 us: newton_schulz(): pl.pallas_call(poly_kernel, out_shape=[pltpu.VMEM((512, 512), BF16)] * 2,...]
  transfers between devices with their start and end apart: 24 -> 24, of which waited for: 10 -> 13; matrix products, arithmetic and copies ran while one was open for 0% -> 0% of each run, Pallas kernels for 15% -> 20%
where the time goes in v5:
time: 75.2 us; the launch traced here: 75.1 us
  Pallas kernels  26.8 us (36%)
  starting transfers between devices  24.1 us (32%)
  waiting for transfers between devices  22.9 us (30%)
  between operations  0.96 us (1%)
    ppermute x24, starting transfers between devices, swap(): return lax.ppermute(x, axis, [(i, i ^ bit) for i in range(size)])  24.1 us
    ppermute x24, waiting for transfers between devices, swap(): return lax.ppermute(x, axis, [(i, i ^ bit) for i in range(size)])  22.9 us
    pallas_call x3, Pallas kernels, conv_more(): pl.pallas_call(functools.partial(more_kernel, depth, cp, taps, chunks), o...  9.3 us
    pallas_call x1, Pallas kernels, conv(): pl.pallas_call(functools.partial(conv_kernel, depth, cp, taps, chunks), o...  6.53 us
    pallas_call x1, Pallas kernels, newton_schulz(): pl.pallas_call(poly_kernel, out_shape=[pltpu.VMEM((512, 512), BF16)] * 2,...  5.06 us
    pallas_call x1, Pallas kernels, finish(): pl.pallas_call(functools.partial(finish_kernel, taps, cp, chans, known, l...  4.01 us
  transfers between devices with their start and end apart: 24, of which 13 were waited for; matrix products, arithmetic and copies ran while one was open for 0% of the time, Pallas kernels for 20%

profile of v5, /device:TPU:0, one launch (start us, length us, event | category | flops | bytes accessed | tf_op | source)
XLA Modules:
  0.0 75.1 jit_solution(8293188951637830005)
XLA Ops:
  0.6 6.5 %conv_first.1 = (f32[336,256]{1,0:T(8,128)S(1)}, f32[336,256]{1,0:T(8,128)S(1)}, bf16[8192,512]{1,0:T(8,128)(2,1)S(1)}, bf16[864,2304]{1,0:T(8,128)(2,1)S(1)}) custom-call(bf16[48,11560]{1,0:T(8,128)(2,1)} %x_hbm.1, bf16[8192,512]{1,0:T(8,128)(2,1)} %cot_hbm.1), custom_call_target="tpu_custom_call" | custom-call | tf_op jit(solution)/shard_map/conv_first/pallas_call | solution.py:129
  7.2 3.0 %collective-permute-start.4 = (f32[336,256]{1,0:T(8,128)S(1)}, f32[336,256]{1,0:T(8,128)S(1)}, u32[]{:S(2)}, u32[]{:S(2)}) collective-permute-start(f32[336,256]{1,0:T(8,128)S(1)} %get-tuple-element.27), channel_id=1, source_target_pairs={{0,16},{8,24},{16,0},{24,8},{1,17},{9,25},{17,1},{25,9},{2,18},{10... | collective-permute-start | bytes 1032200 | tf_op jit(solution)/shard_map/ppermute | solution.py:435
  10.2 1.5 %collective-permute-start.2 = (f32[336,256]{1,0:T(8,128)S(1)}, f32[336,256]{1,0:T(8,128)S(1)}, u32[]{:S(2)}, u32[]{:S(2)}) collective-permute-start(f32[336,256]{1,0:T(8,128)S(1)} %get-tuple-element.25), channel_id=1, source_target_pairs={{0,8},{8,0},{16,24},{24,16},{1,9},{9,1},{17,25},{25,17},{2,10},{10... | collective-permute-start | bytes 1032200 | tf_op jit(solution)/shard_map/ppermute | solution.py:435
  11.7 3.1 %conv_more.4 = (f32[336,256]{1,0:T(8,128)S(1)}, f32[336,256]{1,0:T(8,128)S(1)}) custom-call(bf16[8192,512]{1,0:T(8,128)(2,1)S(1)} %get-tuple-element.18.cot, bf16[864,2304]{1,0:T(8,128)(2,1)S(1)} %get-tuple-element.19.v), custom_call_target="tpu_custom_call" | custom-call | tf_op jit(solution)/shard_map/conv_more/pallas_call | solution.py:154
  14.8 0.7 collective-permute-start
  15.5 0.0 collective-permute-start.1
  15.5 3.1 %conv_more.5 = (f32[336,256]{1,0:T(8,128)S(1)}, f32[336,256]{1,0:T(8,128)S(1)}) custom-call(bf16[8192,512]{1,0:T(8,128)(2,1)S(1)} %get-tuple-element.18.cot, bf16[864,2304]{1,0:T(8,128)(2,1)S(1)} %get-tuple-element.19.v), custom_call_target="tpu_custom_call" | custom-call | tf_op jit(solution)/shard_map/conv_more/pallas_call | solution.py:154
  18.7 0.4 collective-permute-done.4
  19.1 2.1 %collective-permute-start.5 = (f32[336,256]{1,0:T(8,128)S(1)}, f32[336,256]{1,0:T(8,128)S(1)}, u32[]{:S(2)}, u32[]{:S(2)}) collective-permute-start(f32[336,256]{1,0:T(8,128)S(1)} %add.28), channel_id=1, source_target_pairs={{0,8},{8,0},{16,24},{24,16},{1,9},{9,1},{17,25},{25,17},{2,10},{10... | collective-permute-start | bytes 1032200 | tf_op jit(solution)/shard_map/ppermute | solution.py:435
  21.2 0.0 collective-permute-done.2
  21.3 0.0 copy-start
  21.3 1.6 %collective-permute-start.3 = (f32[336,256]{1,0:T(8,128)S(1)}, f32[336,256]{1,0:T(8,128)S(1)}, u32[]{:S(2)}, u32[]{:S(2)}) collective-permute-start(f32[336,256]{1,0:T(8,128)S(1)} %add.27), channel_id=1, source_target_pairs={{0,16},{8,24},{16,0},{24,8},{1,17},{9,25},{17,1},{25,9},{2,18},{10... | collective-permute-start | bytes 1032200 | tf_op jit(solution)/shard_map/ppermute | solution.py:435
  22.9 3.0 %conv_more.3 = (f32[336,256]{1,0:T(8,128)S(1)}, f32[336,256]{1,0:T(8,128)S(1)}) custom-call(bf16[8192,512]{1,0:T(8,128)(2,1)S(1)} %get-tuple-element.18.cot, bf16[864,2304]{1,0:T(8,128)(2,1)S(1)} %get-tuple-element.19.v), custom_call_target="tpu_custom_call" | custom-call | tf_op jit(solution)/shard_map/conv_more/pallas_call | solution.py:154
  25.9 0.0 copy-done
  25.9 0.6 own_momentum.1.m_ref
  26.5 2.1 %collective-permute-done.refs_2_ = f32[336,256]{1,0:T(8,128)S(1)} collective-permute-done((f32[336,256]{1,0:T(8,128)S(1)}, f32[336,256]{1,0:T(8,128)S(1)}, u32[]{:S(2)}, u32[]{:S(2)}) %collective-permute-start) | collective-permute-done | bytes 344096 | tf_op jit(solution)/shard_map/ppermute | solution.py:435
  28.6 0.0 collective-permute-done.1.refs_3_
  28.6 5.9 %collective-permute-done.5.refs_5_ = f32[336,256]{1,0:T(8,128)S(1)} collective-permute-done((f32[336,256]{1,0:T(8,128)S(1)}, f32[336,256]{1,0:T(8,128)S(1)}, u32[]{:S(2)}, u32[]{:S(2)}) %collective-permute-start.5) | collective-permute-done | bytes 344096 | tf_op jit(solution)/shard_map/ppermute | solution.py:435
  34.5 0.0 collective-permute-done.3.refs_4_
  34.5 0.2 momentum_update.1.m.refs_0_
  34.6 1.1 %own_gram.1 = (f32[4,136,128]{2,1,0:T(8,128)S(1)}, f32[4,136,128]{2,1,0:T(8,128)S(1)}) custom-call(f32[672,256]{1,0:T(8,128)S(1)} %momentum_update.1.m.refs_0_), custom_call_target="tpu_custom_call" | custom-call | tf_op jit(solution)/shard_map/own_gram/pallas_call | solution.py:257
  35.7 0.1 collective-permute-start.6
  35.8 0.1 fusion.2
  35.9 1.6 %collective-permute-start.20 = (f32[528,256]{1,0:T(8,128)S(1)}, f32[528,256]{1,0:T(8,128)S(1)}, u32[]{:S(2)}, u32[]{:S(2)}) collective-permute-start(f32[528,256]{1,0:T(8,128)S(1)} %get-tuple-element.35), channel_id=1, source_target_pairs={{0,8},{8,0},{16,24},{24,16},{1,9},{9,1},{17,25},{25,17},{2,10},{10... | collective-permute-start | bytes 1622024 | tf_op jit(solution)/shard_map/ppermute | solution.py:435
  37.5 0.5 collective-permute-start.21
  38.0 0.0 collective-permute-done.6
  38.0 3.7 %collective-permute-start.7 = (f32[136,128]{1,0:T(8,128)S(1)}, f32[136,128]{1,0:T(8,128)S(1)}, u32[]{:S(2)}, u32[]{:S(2)}) collective-permute-start(f32[136,128]{1,0:T(8,128)S(1)} %get-tuple-element.38), channel_id=1, source_target_pairs={{0,6},{1,7},{2,4},{3,5},{4,2},{5,3},{6,0},{7,1},{8,14},{9,15},{10,... | collective-permute-start | bytes 208904 | tf_op jit(solution)/shard_map/ppermute | solution.py:435
  41.7 0.0 collective-permute-start.8
  41.7 0.8 %collective-permute-start.9 = (f32[136,128]{1,0:T(8,128)S(1)}, f32[136,128]{1,0:T(8,128)S(1)}, u32[]{:S(2)}, u32[]{:S(2)}) collective-permute-start(f32[136,128]{1,0:T(8,128)S(1)} %get-tuple-element.37), channel_id=1, source_target_pairs={{0,2},{1,3},{2,0},{3,1},{4,6},{5,7},{6,4},{7,5},{8,10},{9,11},{10,... | collective-permute-start | bytes 208904 | tf_op jit(solution)/shard_map/ppermute | solution.py:435
  42.5 2.2 %collective-permute-done.7 = f32[136,128]{1,0:T(8,128)S(1)} collective-permute-done((f32[136,128]{1,0:T(8,128)S(1)}, f32[136,128]{1,0:T(8,128)S(1)}, u32[]{:S(2)}, u32[]{:S(2)}) %collective-permute-start.7) | collective-permute-done | bytes 69664 | tf_op jit(solution)/shard_map/ppermute | solution.py:435
  44.7 3.0 %collective-permute-done.8 = f32[136,128]{1,0:T(8,128)S(1)} collective-permute-done((f32[136,128]{1,0:T(8,128)S(1)}, f32[136,128]{1,0:T(8,128)S(1)}, u32[]{:S(2)}, u32[]{:S(2)}) %collective-permute-start.8) | collective-permute-done | bytes 69664 | tf_op jit(solution)/shard_map/ppermute | solution.py:435
  47.7 0.0 collective-permute-done.9
  47.7 1.6 %collective-permute-start.10 = (f32[136,128]{1,0:T(8,128)S(1)}, f32[136,128]{1,0:T(8,128)S(1)}, u32[]{:S(2)}, u32[]{:S(2)}) collective-permute-start(f32[136,128]{1,0:T(8,128)S(1)} %fusion.1), channel_id=1, source_target_pairs={{0,24},{8,16},{16,8},{24,0},{1,25},{9,17},{17,9},{25,1},{2,26},{10... | collective-permute-start | bytes 208904 | tf_op jit(solution)/shard_map/ppermute | solution.py:435
  49.3 1.0 %collective-permute-start.11 = (f32[136,128]{1,0:T(8,128)S(1)}, f32[136,128]{1,0:T(8,128)S(1)}, u32[]{:S(2)}, u32[]{:S(2)}) collective-permute-start(f32[136,128]{1,0:T(8,128)S(1)} %fusion.1), channel_id=1, source_target_pairs={{0,16},{8,24},{16,0},{24,8},{1,17},{9,25},{17,1},{25,9},{2,18},{10... | collective-permute-start | bytes 208904 | tf_op jit(solution)/shard_map/ppermute | solution.py:435
  50.3 1.0 %collective-permute-start.12 = (f32[136,128]{1,0:T(8,128)S(1)}, f32[136,128]{1,0:T(8,128)S(1)}, u32[]{:S(2)}, u32[]{:S(2)}) collective-permute-start(f32[136,128]{1,0:T(8,128)S(1)} %fusion.1), channel_id=1, source_target_pairs={{0,8},{8,0},{16,24},{24,16},{1,9},{9,1},{17,25},{25,17},{2,10},{10... | collective-permute-start | bytes 208904 | tf_op jit(solution)/shard_map/ppermute | solution.py:435
  51.3 0.0 collective-permute-done.20.mx.refs_1_
  51.3 2.8 %collective-permute-done.21.my.refs_2_ = f32[528,256]{1,0:T(8,128)S(1)} collective-permute-done((f32[528,256]{1,0:T(8,128)S(1)}, f32[528,256]{1,0:T(8,128)S(1)}, u32[]{:S(2)}, u32[]{:S(2)}) %collective-permute-start.21) | collective-permute-done | bytes 540704 | tf_op jit(solution)/shard_map/ppermute | solution.py:435
  54.1 0.1 second_step.1
  54.1 0.1 collective-permute-start.22
  54.2 0.1 collective-permute-start.23
  54.3 0.0 collective-permute-done.10
  54.3 0.5 collective-permute-done.11
  54.8 0.0 collective-permute-done.12
  54.9 3.7 %collective-permute-start.13 = (f32[136,128]{1,0:T(8,128)S(1)}, f32[136,128]{1,0:T(8,128)S(1)}, u32[]{:S(2)}, u32[]{:S(2)}) collective-permute-start(f32[136,128]{1,0:T(8,128)S(1)} %add_add_fusion.refs_3_), channel_id=1, source_target_pairs={{0,6},{1,7},{2,4},{3,5},{4,2},{5,3},{6,0},{7,1},{8,14},{9,15},{10,... | collective-permute-start | bytes 208904 | tf_op jit(solution)/shard_map/ppermute | solution.py:435
  58.5 0.0 collective-permute-start.14
  58.5 0.8 %collective-permute-start.15 = (f32[136,128]{1,0:T(8,128)S(1)}, f32[136,128]{1,0:T(8,128)S(1)}, u32[]{:S(2)}, u32[]{:S(2)}) collective-permute-start(f32[136,128]{1,0:T(8,128)S(1)} %add_add_fusion.refs_3_), channel_id=1, source_target_pairs={{0,2},{1,3},{2,0},{3,1},{4,6},{5,7},{6,4},{7,5},{8,10},{9,11},{10,... | collective-permute-start | bytes 208904 | tf_op jit(solution)/shard_map/ppermute | solution.py:435
  59.3 2.4 %collective-permute-done.13.refs_0_ = f32[136,128]{1,0:T(8,128)S(1)} collective-permute-done((f32[136,128]{1,0:T(8,128)S(1)}, f32[136,128]{1,0:T(8,128)S(1)}, u32[]{:S(2)}, u32[]{:S(2)}) %collective-permute-start.13) | collective-permute-done | bytes 69664 | tf_op jit(solution)/shard_map/ppermute | solution.py:435
  61.7 0.0 collective-permute-start.19
  61.7 2.3 %collective-permute-done.14.refs_1_ = f32[136,128]{1,0:T(8,128)S(1)} collective-permute-done((f32[136,128]{1,0:T(8,128)S(1)}, f32[136,128]{1,0:T(8,128)S(1)}, u32[]{:S(2)}, u32[]{:S(2)}) %collective-permute-start.14) | collective-permute-done | bytes 69664 | tf_op jit(solution)/shard_map/ppermute | solution.py:435
  64.1 0.0 collective-permute-start.16
  64.1 0.1 collective-permute-done.15.refs_2_
  64.1 0.5 collective-permute-start.17
  64.6 0.0 collective-permute-done.19.refs_7_
  64.6 0.1 collective-permute-start.18
  64.6 0.7 collective-permute-done.16.refs_4_
  65.3 0.2 collective-permute-done.17.refs_5_
  65.5 0.4 collective-permute-done.18.refs_6_
  65.8 5.1 %newton_schulz.1 = (bf16[512,512]{1,0:T(8,128)(2,1)S(1)}, bf16[512,512]{1,0:T(8,128)(2,1)S(1)}) custom-call(f32[136,128]{1,0:T(8,128)S(1)} %collective-permute-done.13.refs_0_, f32[136,128]{1,0:T(8,128)S(1)} %collective-permute-done.14.refs_1_, f32[136,128]{1,0:T(8,128)S(1)} %collective-permute-done.15.refs_2_, f32[136,128]{1,0:T(8,128)S(1)} %add_add_fusion.refs_3_, ...), custom_call_target="tpu_custom_call" | custom-call | tf_op jit(solution)/shard_map/newton_schulz/pallas_call | solution.py:361
  70.9 0.0 collective-permute-done.22.refs_3_
  70.9 0.0 collective-permute-done.23.refs_4_
  70.9 4.0 %finish.1 = (f32[1296,512]{1,0:T(8,128)}, f32[1296,512]{1,0:T(8,128)}) custom-call(bf16[512,512]{1,0:T(8,128)(2,1)S(1)} %get-tuple-element.30.qh, bf16[512,512]{1,0:T(8,128)(2,1)S(1)} %get-tuple-element.31.ql, f32[672,256]{1,0:T(8,128)S(1)} %momentum_update.1.m.refs_0_, f32[528,256]{1,0:T(8,128)S(1)} %collective-permute-done.20.mx.refs_1_, ...), custom_call_target="tpu_custom_call" | custom-call | tf_op jit(solution)/shard_map/finish/pallas_call | solution.py:416
  (6 shorter events, 0.2 us)
Async XLA Ops:
  7.2 11.9 %collective-permute-start.4 = (f32[336,256]{1,0:T(8,128)S(1)}, f32[336,256]{1,0:T(8,128)S(1)}, u32[]{:S(2)}, u32[]{:S(2)}) collective-permute-start(f32[336,256]{1,0:T(8,128)S(1)} %get-tuple-element.27), channel_id=1, source_target_pairs={{0,16},{8,24},{16,0},{24,8},{1,17},{9,25},{17,1},{25,9},{2,18},{10... | collective-permute-start | bytes 1032200 | tf_op jit(solution)/shard_map/ppermute | solution.py:435
  10.2 11.0 %collective-permute-start.2 = (f32[336,256]{1,0:T(8,128)S(1)}, f32[336,256]{1,0:T(8,128)S(1)}, u32[]{:S(2)}, u32[]{:S(2)}) collective-permute-start(f32[336,256]{1,0:T(8,128)S(1)} %get-tuple-element.25), channel_id=1, source_target_pairs={{0,8},{8,0},{16,24},{24,16},{1,9},{9,1},{17,25},{25,17},{2,10},{10... | collective-permute-start | bytes 1032200 | tf_op jit(solution)/shard_map/ppermute | solution.py:435
  14.8 13.7 %collective-permute-start = (f32[336,256]{1,0:T(8,128)S(1)}, f32[336,256]{1,0:T(8,128)S(1)}, u32[]{:S(2)}, u32[]{:S(2)}) collective-permute-start(f32[336,256]{1,0:T(8,128)S(1)} %get-tuple-element.22), channel_id=1, source_target_pairs={{0,8},{8,0},{16,24},{24,16},{1,9},{9,1},{17,25},{25,17},{2,10},{10... | collective-permute-start | bytes 1032200 | tf_op jit(solution)/shard_map/ppermute | solution.py:435
  15.5 13.1 %collective-permute-start.1 = (f32[336,256]{1,0:T(8,128)S(1)}, f32[336,256]{1,0:T(8,128)S(1)}, u32[]{:S(2)}, u32[]{:S(2)}) collective-permute-start(f32[336,256]{1,0:T(8,128)S(1)} %get-tuple-element.23), channel_id=1, source_target_pairs={{0,16},{8,24},{16,0},{24,8},{1,17},{9,25},{17,1},{25,9},{2,18},{10... | collective-permute-start | bytes 1032200 | tf_op jit(solution)/shard_map/ppermute | solution.py:435
  19.1 15.3 %collective-permute-start.5 = (f32[336,256]{1,0:T(8,128)S(1)}, f32[336,256]{1,0:T(8,128)S(1)}, u32[]{:S(2)}, u32[]{:S(2)}) collective-permute-start(f32[336,256]{1,0:T(8,128)S(1)} %add.28), channel_id=1, source_target_pairs={{0,8},{8,0},{16,24},{24,16},{1,9},{9,1},{17,25},{25,17},{2,10},{10... | collective-permute-start | bytes 1032200 | tf_op jit(solution)/shard_map/ppermute | solution.py:435
  21.3 4.6 %copy-start = (f32[1296,512]{1,0:T(8,128)S(1)}, f32[1296,512]{1,0:T(8,128)}, u32[]{:S(2)}) copy-start(f32[1296,512]{1,0:T(8,128)} %m_ref.1) | copy-start | bytes 7962628
  21.3 13.2 %collective-permute-start.3 = (f32[336,256]{1,0:T(8,128)S(1)}, f32[336,256]{1,0:T(8,128)S(1)}, u32[]{:S(2)}, u32[]{:S(2)}) collective-permute-start(f32[336,256]{1,0:T(8,128)S(1)} %add.27), channel_id=1, source_target_pairs={{0,16},{8,24},{16,0},{24,8},{1,17},{9,25},{17,1},{25,9},{2,18},{10... | collective-permute-start | bytes 1032200 | tf_op jit(solution)/shard_map/ppermute | solution.py:435
  35.7 2.2 %collective-permute-start.6 = (f32[4,136,128]{2,1,0:T(8,128)S(1)}, f32[4,136,128]{2,1,0:T(8,128)S(1)}, u32[]{:S(2)}, u32[]{:S(2)}) collective-permute-start(f32[4,136,128]{2,1,0:T(8,128)S(1)} %get-tuple-element.29), channel_id=1, source_target_pairs={{0,1},{1,0},{2,3},{3,2},{4,5},{5,4},{6,7},{7,6},{8,9},{9,8},{10,11... | collective-permute-start | bytes 835592 | tf_op jit(solution)/shard_map/ppermute | solution.py:435
  35.9 15.4 %collective-permute-start.20 = (f32[528,256]{1,0:T(8,128)S(1)}, f32[528,256]{1,0:T(8,128)S(1)}, u32[]{:S(2)}, u32[]{:S(2)}) collective-permute-start(f32[528,256]{1,0:T(8,128)S(1)} %get-tuple-element.35), channel_id=1, source_target_pairs={{0,8},{8,0},{16,24},{24,16},{1,9},{9,1},{17,25},{25,17},{2,10},{10... | collective-permute-start | bytes 1622024 | tf_op jit(solution)/shard_map/ppermute | solution.py:435
  37.5 16.6 %collective-permute-start.21 = (f32[528,256]{1,0:T(8,128)S(1)}, f32[528,256]{1,0:T(8,128)S(1)}, u32[]{:S(2)}, u32[]{:S(2)}) collective-permute-start(f32[528,256]{1,0:T(8,128)S(1)} %get-tuple-element.34), channel_id=1, source_target_pairs={{0,16},{8,24},{16,0},{24,8},{1,17},{9,25},{17,1},{25,9},{2,18},{10... | collective-permute-start | bytes 1622024 | tf_op jit(solution)/shard_map/ppermute | solution.py:435
  38.0 6.7 %collective-permute-start.7 = (f32[136,128]{1,0:T(8,128)S(1)}, f32[136,128]{1,0:T(8,128)S(1)}, u32[]{:S(2)}, u32[]{:S(2)}) collective-permute-start(f32[136,128]{1,0:T(8,128)S(1)} %get-tuple-element.38), channel_id=1, source_target_pairs={{0,6},{1,7},{2,4},{3,5},{4,2},{5,3},{6,0},{7,1},{8,14},{9,15},{10,... | collective-permute-start | bytes 208904 | tf_op jit(solution)/shard_map/ppermute | solution.py:435
  41.7 6.0 %collective-permute-start.8 = (f32[136,128]{1,0:T(8,128)S(1)}, f32[136,128]{1,0:T(8,128)S(1)}, u32[]{:S(2)}, u32[]{:S(2)}) collective-permute-start(f32[136,128]{1,0:T(8,128)S(1)} %get-tuple-element.36), channel_id=1, source_target_pairs={{0,4},{1,5},{2,6},{3,7},{4,0},{5,1},{6,2},{7,3},{8,12},{9,13},{10,... | collective-permute-start | bytes 208904 | tf_op jit(solution)/shard_map/ppermute | solution.py:435
  41.7 6.0 %collective-permute-start.9 = (f32[136,128]{1,0:T(8,128)S(1)}, f32[136,128]{1,0:T(8,128)S(1)}, u32[]{:S(2)}, u32[]{:S(2)}) collective-permute-start(f32[136,128]{1,0:T(8,128)S(1)} %get-tuple-element.37), channel_id=1, source_target_pairs={{0,2},{1,3},{2,0},{3,1},{4,6},{5,7},{6,4},{7,5},{8,10},{9,11},{10,... | collective-permute-start | bytes 208904 | tf_op jit(solution)/shard_map/ppermute | solution.py:435
  47.7 6.6 %collective-permute-start.10 = (f32[136,128]{1,0:T(8,128)S(1)}, f32[136,128]{1,0:T(8,128)S(1)}, u32[]{:S(2)}, u32[]{:S(2)}) collective-permute-start(f32[136,128]{1,0:T(8,128)S(1)} %fusion.1), channel_id=1, source_target_pairs={{0,24},{8,16},{16,8},{24,0},{1,25},{9,17},{17,9},{25,1},{2,26},{10... | collective-permute-start | bytes 208904 | tf_op jit(solution)/shard_map/ppermute | solution.py:435
  49.3 5.5 %collective-permute-start.11 = (f32[136,128]{1,0:T(8,128)S(1)}, f32[136,128]{1,0:T(8,128)S(1)}, u32[]{:S(2)}, u32[]{:S(2)}) collective-permute-start(f32[136,128]{1,0:T(8,128)S(1)} %fusion.1), channel_id=1, source_target_pairs={{0,16},{8,24},{16,0},{24,8},{1,17},{9,25},{17,1},{25,9},{2,18},{10... | collective-permute-start | bytes 208904 | tf_op jit(solution)/shard_map/ppermute | solution.py:435
  50.3 4.5 %collective-permute-start.12 = (f32[136,128]{1,0:T(8,128)S(1)}, f32[136,128]{1,0:T(8,128)S(1)}, u32[]{:S(2)}, u32[]{:S(2)}) collective-permute-start(f32[136,128]{1,0:T(8,128)S(1)} %fusion.1), channel_id=1, source_target_pairs={{0,8},{8,0},{16,24},{24,16},{1,9},{9,1},{17,25},{25,17},{2,10},{10... | collective-permute-start | bytes 208904 | tf_op jit(solution)/shard_map/ppermute | solution.py:435
  54.1 16.8 %collective-permute-start.22 = (f32[480,256]{1,0:T(8,128)S(1)}, f32[480,256]{1,0:T(8,128)S(1)}, u32[]{:S(2)}, u32[]{:S(2)}) collective-permute-start(f32[480,256]{1,0:T(8,128)S(1)} %get-tuple-element.32), channel_id=1, source_target_pairs={{0,8},{8,0},{16,24},{24,16},{1,9},{9,1},{17,25},{25,17},{2,10},{10... | collective-permute-start | bytes 1474568 | tf_op jit(solution)/shard_map/ppermute | solution.py:435
  54.2 16.7 %collective-permute-start.23 = (f32[480,256]{1,0:T(8,128)S(1)}, f32[480,256]{1,0:T(8,128)S(1)}, u32[]{:S(2)}, u32[]{:S(2)}) collective-permute-start(f32[480,256]{1,0:T(8,128)S(1)} %get-tuple-element.33), channel_id=1, source_target_pairs={{0,16},{8,24},{16,0},{24,8},{1,17},{9,25},{17,1},{25,9},{2,18},{10... | collective-permute-start | bytes 1474568 | tf_op jit(solution)/shard_map/ppermute | solution.py:435
  54.9 6.9 %collective-permute-start.13 = (f32[136,128]{1,0:T(8,128)S(1)}, f32[136,128]{1,0:T(8,128)S(1)}, u32[]{:S(2)}, u32[]{:S(2)}) collective-permute-start(f32[136,128]{1,0:T(8,128)S(1)} %add_add_fusion.refs_3_), channel_id=1, source_target_pairs={{0,6},{1,7},{2,4},{3,5},{4,2},{5,3},{6,0},{7,1},{8,14},{9,15},{10,... | collective-permute-start | bytes 208904 | tf_op jit(solution)/shard_map/ppermute | solution.py:435
  58.5 5.5 %collective-permute-start.14 = (f32[136,128]{1,0:T(8,128)S(1)}, f32[136,128]{1,0:T(8,128)S(1)}, u32[]{:S(2)}, u32[]{:S(2)}) collective-permute-start(f32[136,128]{1,0:T(8,128)S(1)} %add_add_fusion.refs_3_), channel_id=1, source_target_pairs={{0,4},{1,5},{2,6},{3,7},{4,0},{5,1},{6,2},{7,3},{8,12},{9,13},{10,... | collective-permute-start | bytes 208904 | tf_op jit(solution)/shard_map/ppermute | solution.py:435
  58.5 5.6 %collective-permute-start.15 = (f32[136,128]{1,0:T(8,128)S(1)}, f32[136,128]{1,0:T(8,128)S(1)}, u32[]{:S(2)}, u32[]{:S(2)}) collective-permute-start(f32[136,128]{1,0:T(8,128)S(1)} %add_add_fusion.refs_3_), channel_id=1, source_target_pairs={{0,2},{1,3},{2,0},{3,1},{4,6},{5,7},{6,4},{7,5},{8,10},{9,11},{10,... | collective-permute-start | bytes 208904 | tf_op jit(solution)/shard_map/ppermute | solution.py:435
  61.7 2.8 %collective-permute-start.19 = (f32[136,128]{1,0:T(8,128)S(1)}, f32[136,128]{1,0:T(8,128)S(1)}, u32[]{:S(2)}, u32[]{:S(2)}) collective-permute-start(f32[136,128]{1,0:T(8,128)S(1)} %add_add_fusion.refs_3_), channel_id=1, source_target_pairs={{0,1},{1,0},{2,3},{3,2},{4,5},{5,4},{6,7},{7,6},{8,9},{9,8},{10,11... | collective-permute-start | bytes 208904 | tf_op jit(solution)/shard_map/ppermute | solution.py:435
  64.1 1.3 %collective-permute-start.16 = (f32[136,128]{1,0:T(8,128)S(1)}, f32[136,128]{1,0:T(8,128)S(1)}, u32[]{:S(2)}, u32[]{:S(2)}) collective-permute-start(f32[136,128]{1,0:T(8,128)S(1)} %collective-permute-done.13.refs_0_), channel_id=1, source_target_pairs={{0,1},{1,0},{2,3},{3,2},{4,5},{5,4},{6,7},{7,6},{8,9},{9,8},{10,11... | collective-permute-start | bytes 208904 | tf_op jit(solution)/shard_map/ppermute | solution.py:435
  64.1 1.4 %collective-permute-start.17 = (f32[136,128]{1,0:T(8,128)S(1)}, f32[136,128]{1,0:T(8,128)S(1)}, u32[]{:S(2)}, u32[]{:S(2)}) collective-permute-start(f32[136,128]{1,0:T(8,128)S(1)} %collective-permute-done.14.refs_1_), channel_id=1, source_target_pairs={{0,1},{1,0},{2,3},{3,2},{4,5},{5,4},{6,7},{7,6},{8,9},{9,8},{10,11... | collective-permute-start | bytes 208904 | tf_op jit(solution)/shard_map/ppermute | solution.py:435
  64.6 1.3 %collective-permute-start.18 = (f32[136,128]{1,0:T(8,128)S(1)}, f32[136,128]{1,0:T(8,128)S(1)}, u32[]{:S(2)}, u32[]{:S(2)}) collective-permute-start(f32[136,128]{1,0:T(8,128)S(1)} %collective-permute-done.15.refs_2_), channel_id=1, source_target_pairs={{0,1},{1,0},{2,3},{3,2},{4,5},{5,4},{6,7},{7,6},{8,9},{9,8},{10,11... | collective-permute-start | bytes 208904 | tf_op jit(solution)/shard_map/ppermute | solution.py:435

commit v6 on v5

--- a/solution.py
+++ b/solution.py
@@ -308,8 +308,7 @@
     return d(ah, bh) + (d(ah, bl) + d(al, bh))
 
 
-def poly_kernel(*refs):
-    parts, (qh, ql, g_ref, p_ref, d_ref) = refs[:-5], refs[-5:]
+def assemble(parts, g_ref, p_ref, d_ref):
     if len(parts) == 1:
         g_ref[...] = parts[0][...]
     else:
@@ -342,6 +341,46 @@
             g_ref[128 * j : 128 * j + 128, 128 * i : 128 * i + 128] = g_ref[
                 128 * i : 128 * i + 128, 128 * j : 128 * j + 128
             ].T
+
+
+def tap_rows(places, parts, taps, cp, slot):
+    out = []
+    for n, base in places[slot]:
+        ends = [b for m, b in sum(places, []) if m == n and b > base] + [parts[n].shape[0]]
+        out += [(n, at) for at in range(base, min(ends), cp)]
+    return out[:taps]
+
+
+def row_cuts(rows):
+    cuts = [min(rows, -(-rows * k // 24) * 8) for k in range(4)]
+    return [(a, b) for a, b in zip(cuts, cuts[1:]) if b > a]
+
+
+def finish_kernel(taps, cp, chans, known, places, count, *refs):
+    parts, grams = refs[:count], refs[count:-11]
+    new, out, g_ref, p_ref, d_ref, cols, hi, lo, acc, sem, osem = refs[-11:]
+    copies = []
+
+    def reorder(c):
+        lanes = slice(LANE * (c % 2), LANE * (c % 2) + LANE)
+        for r in range(len(places) // 2):
+            rows = None
+            for i, (n, at) in enumerate(tap_rows(places, parts, taps, cp, 2 * r + c // 2)):
+                if not known and r * taps + i >= TAPS:
+                    continue
+                before, rows = rows, parts[n][at : at + chans, lanes]
+                t = r * taps + i
+                if known:
+                    t = (lax.axis_index("dp") ^ r) * taps + i
+                    if 3 * taps + i >= TAPS:
+                        rows = jnp.where(t < TAPS, rows, before)
+                        t = jnp.minimum(t, TAPS - 1)
+                cols.at[c][pl.ds(t, chans, stride=TAPS), :] = rows
+        hi[:, LANE * c : LANE * c + LANE], lo[:, LANE * c : LANE * c + LANE] = split(cols[c])
+        copies.append(pltpu.make_async_copy(cols.at[c], new.at[:, pl.ds(LANE * c, LANE)], sem.at[c]))
+        copies[-1].start()
+
+    assemble(grams, g_ref, p_ref, d_ref)
     gram = g_ref[...]
     n = gram.shape[0]
     diag = lax.broadcasted_iota(jnp.int32, (n, n), 0) == lax.broadcasted_iota(jnp.int32, (n, n), 1)
@@ -350,75 +389,35 @@
     g = gram * scale * scale
     gs = split(g)
     p1 = jnp.where(diag, A1, 0.0) + B1 * g + C1 * mm(gs, gs)
+    reorder(0)
     p1s = split(p1)
-    g2 = mm(split(mm(gs, p1s)), p1s)
+    h = mm(gs, p1s)
+    reorder(1)
+    g2 = mm(split(h), p1s)
+    reorder(2)
     g2s = split(g2)
     p2 = jnp.where(diag, A1, 0.0) + B1 * g2 + C1 * mm(g2s, g2s)
-    qh[...], ql[...] = split(mm(p1s, split(p2)) * (scale * jnp.sqrt(F32(ROWS))))
-
-
-def newton_schulz(parts):
-    return pl.pallas_call(
-        poly_kernel,
-        out_shape=[pltpu.VMEM((512, 512), BF16)] * 2,
-        in_specs=[VMEM] * len(parts),
-        out_specs=[VMEM] * 2,
+    reorder(3)
+    qs = split(mm(p1s, split(p2)) * (scale * jnp.sqrt(F32(ROWS))))
+    for k, (a, b) in enumerate(row_cuts(acc.shape[0])):
+        acc[a:b, :] = mm((hi[a:b, :], lo[a:b, :]), qs)
+        copies.append(pltpu.make_async_copy(acc.at[pl.ds(a, b - a)], out.at[pl.ds(a, b - a)], osem.at[k]))
+        copies[-1].start()
+    for copy in copies:
+        copy.wait()
+
+
+def finish(grams, parts, places, taps, cp, chans, known):
+    rows = chans * TAPS
+    return pl.pallas_call(
+        functools.partial(finish_kernel, taps, cp, chans, known, list(places), len(parts)),
+        out_shape=[jax.ShapeDtypeStruct((rows, 512), F32)] * 2,
+        in_specs=[VMEM] * (len(grams) + len(parts)),
+        out_specs=[HBM] * 2,
         scratch_shapes=[
             pltpu.VMEM((512, 512), F32),
             pltpu.VMEM((2, 128, 128), F32),
             pltpu.VMEM((2, 32, 128), F32),
-        ],
-        compiler_params=params(),
-        name="newton_schulz",
-    )(*map(near, parts))
-
-
-def finish_kernel(taps, cp, chans, known, places, qh, ql, *refs):
-    parts, (new, out, cols, hi, lo, acc, sem, osem) = refs[:-8], refs[-8:]
-    copies = []
-    for c in range(4):
-        for r in range(len(places) // 2):
-            i = 0
-            for n, base in places[2 * r + c // 2]:
-                ends = [b for m, b in sum(places, []) if m == n and b > base] + [parts[n].shape[0]]
-                for at in range(base, min(ends), cp):
-                    if i >= taps:
-                        break
-                    t = (lax.axis_index("dp") ^ r) * taps + i if known else r * taps + i
-                    i += 1
-                    if not known and t >= TAPS:
-                        continue
-                    rows = parts[n][at : at + chans, LANE * (c % 2) : LANE * (c % 2) + LANE]
-
-                    @pl.when(t < TAPS)
-                    def _():
-                        cols.at[c][pl.ds(t, chans, stride=TAPS), :] = rows
-
-            assert i == taps
-        copies.append(pltpu.make_async_copy(cols.at[c], new.at[:, pl.ds(LANE * c, LANE)], sem.at[c]))
-        copies[c].start()
-        hi[:, LANE * c : LANE * c + LANE], lo[:, LANE * c : LANE * c + LANE] = split(cols[c])
-    for k, (a, b) in enumerate(row_cuts(acc.shape[0])):
-        acc[a:b, :] = mm((hi[a:b, :], lo[a:b, :]), (qh[...], ql[...]))
-        copies.append(pltpu.make_async_copy(acc.at[pl.ds(a, b - a)], out.at[pl.ds(a, b - a)], osem.at[k]))
-        copies[-1].start()
-    for copy in copies:
-        copy.wait()
-
-
-def row_cuts(rows):
-    cuts = [min(rows, -(-rows * k // 24) * 8) for k in range(4)]
-    return [(a, b) for a, b in zip(cuts, cuts[1:]) if b > a]
-
-
-def finish(q, parts, places, taps, cp, chans, known):
-    rows = chans * TAPS
-    return pl.pallas_call(
-        functools.partial(finish_kernel, taps, cp, chans, known, list(places)),
-        out_shape=[jax.ShapeDtypeStruct((rows, 512), F32)] * 2,
-        in_specs=[VMEM] * (2 + len(parts)),
-        out_specs=[HBM] * 2,
-        scratch_shapes=[
             pltpu.VMEM((4, rows, LANE), F32),
             pltpu.VMEM((rows, 512), BF16),
             pltpu.VMEM((rows, 512), BF16),
@@ -428,7 +427,7 @@
         ],
         compiler_params=params(),
         name="finish",
-    )(*map(near, q), *map(near, parts))
+    )(*map(near, parts), *map(near, grams))
 
 
 def swap(x, axis, size, bit):
@@ -493,7 +492,7 @@
         [(4, 0), (2, 0)], [(2, more)],
         [(4, rest)], [(3, rest)],
     )
-    return finish(newton_schulz(g), (m, mx, my, nx, ny), places, taps, cp, chans, True)
+    return finish(g, (m, mx, my, nx, ny), places, taps, cp, chans, True)
 
 
 def body_any(n_dp, layer_input, cotangent, momentum):
@@ -508,7 +507,7 @@
     rows = taps * cp
     full = [lax.all_gather(half, "dp", axis=0, tiled=True) for half in (m[:rows], m[rows:])]
     places = [[(half, r * rows)] for r in range(n_dp) for half in range(2)]
-    return finish(newton_schulz([gram]), full, places, taps, cp, chans, False)
+    return finish([gram], full, places, taps, cp, chans, False)
 
 
 def solution(mesh):

time: 75.2 us -> 74.6 us (level)
    pallas_call x1 -> x0, Pallas kernels: 5.06 us -> none  [newton_schulz(): pl.pallas_call(poly_kernel, out_shape=[pltpu.VMEM((512, 512), BF16)] * 2,...]
    pallas_call x1, Pallas kernels: 4.01 us -> 8.46 us  [finish(): pl.pallas_call(functools.partial(finish_kernel, taps, cp, chans, known, l...]
  transfers between devices with their start and end apart: 24 -> 24, of which waited for: 13 -> 13; matrix products, arithmetic and copies ran while one was open for 0% -> 0% of each run, Pallas kernels for 20% -> 13%
where the time goes in v6:
time: 74.6 us; the launch traced here: 74.5 us
  Pallas kernels  26.2 us (35%)
  starting transfers between devices  24.1 us (32%)
  waiting for transfers between devices  22.9 us (31%)
  between operations  0.94 us (1%)
    ppermute x24, starting transfers between devices, swap(): return lax.ppermute(x, axis, [(i, i ^ bit) for i in range(size)])  24.1 us
    ppermute x24, waiting for transfers between devices, swap(): return lax.ppermute(x, axis, [(i, i ^ bit) for i in range(size)])  22.9 us
    pallas_call x3, Pallas kernels, conv_more(): pl.pallas_call(functools.partial(more_kernel, depth, cp, taps, chunks), o...  9.3 us
    pallas_call x1, Pallas kernels, finish(): pl.pallas_call(functools.partial(finish_kernel, taps, cp, chans, known, l...  8.46 us
    pallas_call x1, Pallas kernels, conv(): pl.pallas_call(functools.partial(conv_kernel, depth, cp, taps, chunks), o...  6.53 us
  transfers between devices with their start and end apart: 24, of which 13 were waited for; matrix products, arithmetic and copies ran while one was open for 0% of the time, Pallas kernels for 13%

profile of v6, /device:TPU:0, one launch (start us, length us, event | category | flops | bytes accessed | tf_op | source)
XLA Modules:
  0.0 74.5 jit_solution(17923685532892108546)
XLA Ops:
  0.6 6.5 %conv_first.1 = (f32[336,256]{1,0:T(8,128)S(1)}, f32[336,256]{1,0:T(8,128)S(1)}, bf16[8192,512]{1,0:T(8,128)(2,1)S(1)}, bf16[864,2304]{1,0:T(8,128)(2,1)S(1)}) custom-call(bf16[48,11560]{1,0:T(8,128)(2,1)} %x_hbm.1, bf16[8192,512]{1,0:T(8,128)(2,1)} %cot_hbm.1), custom_call_target="tpu_custom_call" | custom-call | tf_op jit(solution)/shard_map/conv_first/pallas_call | solution.py:129
  7.2 3.0 %collective-permute-start.4 = (f32[336,256]{1,0:T(8,128)S(1)}, f32[336,256]{1,0:T(8,128)S(1)}, u32[]{:S(2)}, u32[]{:S(2)}) collective-permute-start(f32[336,256]{1,0:T(8,128)S(1)} %get-tuple-element.25), channel_id=1, source_target_pairs={{0,16},{8,24},{16,0},{24,8},{1,17},{9,25},{17,1},{25,9},{2,18},{10... | collective-permute-start | bytes 1032200 | tf_op jit(solution)/shard_map/ppermute | solution.py:434
  10.2 1.5 %collective-permute-start.2 = (f32[336,256]{1,0:T(8,128)S(1)}, f32[336,256]{1,0:T(8,128)S(1)}, u32[]{:S(2)}, u32[]{:S(2)}) collective-permute-start(f32[336,256]{1,0:T(8,128)S(1)} %get-tuple-element.23), channel_id=1, source_target_pairs={{0,8},{8,0},{16,24},{24,16},{1,9},{9,1},{17,25},{25,17},{2,10},{10... | collective-permute-start | bytes 1032200 | tf_op jit(solution)/shard_map/ppermute | solution.py:434
  11.7 3.1 %conv_more.4 = (f32[336,256]{1,0:T(8,128)S(1)}, f32[336,256]{1,0:T(8,128)S(1)}) custom-call(bf16[8192,512]{1,0:T(8,128)(2,1)S(1)} %get-tuple-element.16.cot, bf16[864,2304]{1,0:T(8,128)(2,1)S(1)} %get-tuple-element.17.v), custom_call_target="tpu_custom_call" | custom-call | tf_op jit(solution)/shard_map/conv_more/pallas_call | solution.py:154
  14.8 0.7 collective-permute-start
  15.5 0.0 collective-permute-start.1
  15.5 3.1 %conv_more.5 = (f32[336,256]{1,0:T(8,128)S(1)}, f32[336,256]{1,0:T(8,128)S(1)}) custom-call(bf16[8192,512]{1,0:T(8,128)(2,1)S(1)} %get-tuple-element.16.cot, bf16[864,2304]{1,0:T(8,128)(2,1)S(1)} %get-tuple-element.17.v), custom_call_target="tpu_custom_call" | custom-call | tf_op jit(solution)/shard_map/conv_more/pallas_call | solution.py:154
  18.7 0.4 collective-permute-done.4
  19.1 2.1 %collective-permute-start.5 = (f32[336,256]{1,0:T(8,128)S(1)}, f32[336,256]{1,0:T(8,128)S(1)}, u32[]{:S(2)}, u32[]{:S(2)}) collective-permute-start(f32[336,256]{1,0:T(8,128)S(1)} %add.28), channel_id=1, source_target_pairs={{0,8},{8,0},{16,24},{24,16},{1,9},{9,1},{17,25},{25,17},{2,10},{10... | collective-permute-start | bytes 1032200 | tf_op jit(solution)/shard_map/ppermute | solution.py:434
  21.2 0.0 collective-permute-done.2
  21.3 0.0 copy-start
  21.3 1.6 %collective-permute-start.3 = (f32[336,256]{1,0:T(8,128)S(1)}, f32[336,256]{1,0:T(8,128)S(1)}, u32[]{:S(2)}, u32[]{:S(2)}) collective-permute-start(f32[336,256]{1,0:T(8,128)S(1)} %add.27), channel_id=1, source_target_pairs={{0,16},{8,24},{16,0},{24,8},{1,17},{9,25},{17,1},{25,9},{2,18},{10... | collective-permute-start | bytes 1032200 | tf_op jit(solution)/shard_map/ppermute | solution.py:434
  22.9 3.0 %conv_more.3 = (f32[336,256]{1,0:T(8,128)S(1)}, f32[336,256]{1,0:T(8,128)S(1)}) custom-call(bf16[8192,512]{1,0:T(8,128)(2,1)S(1)} %get-tuple-element.16.cot, bf16[864,2304]{1,0:T(8,128)(2,1)S(1)} %get-tuple-element.17.v), custom_call_target="tpu_custom_call" | custom-call | tf_op jit(solution)/shard_map/conv_more/pallas_call | solution.py:154
  25.9 0.0 copy-done
  25.9 0.6 own_momentum.1.m_ref
  26.5 2.1 %collective-permute-done.refs_2_ = f32[336,256]{1,0:T(8,128)S(1)} collective-permute-done((f32[336,256]{1,0:T(8,128)S(1)}, f32[336,256]{1,0:T(8,128)S(1)}, u32[]{:S(2)}, u32[]{:S(2)}) %collective-permute-start) | collective-permute-done | bytes 344096 | tf_op jit(solution)/shard_map/ppermute | solution.py:434
  28.6 0.0 collective-permute-done.1.refs_3_
  28.6 5.9 %collective-permute-done.5.refs_5_ = f32[336,256]{1,0:T(8,128)S(1)} collective-permute-done((f32[336,256]{1,0:T(8,128)S(1)}, f32[336,256]{1,0:T(8,128)S(1)}, u32[]{:S(2)}, u32[]{:S(2)}) %collective-permute-start.5) | collective-permute-done | bytes 344096 | tf_op jit(solution)/shard_map/ppermute | solution.py:434
  34.5 0.0 collective-permute-done.3.refs_4_
  34.5 0.2 momentum_update.1.m.refs_0_
  34.6 1.1 %own_gram.1 = (f32[4,136,128]{2,1,0:T(8,128)S(1)}, f32[4,136,128]{2,1,0:T(8,128)S(1)}) custom-call(f32[672,256]{1,0:T(8,128)S(1)} %momentum_update.1.m.refs_0_), custom_call_target="tpu_custom_call" | custom-call | tf_op jit(solution)/shard_map/own_gram/pallas_call | solution.py:257
  35.7 0.1 collective-permute-start.10
  35.8 0.1 fusion.2
  35.9 1.6 %collective-permute-start.6 = (f32[528,256]{1,0:T(8,128)S(1)}, f32[528,256]{1,0:T(8,128)S(1)}, u32[]{:S(2)}, u32[]{:S(2)}) collective-permute-start(f32[528,256]{1,0:T(8,128)S(1)} %get-tuple-element.31), channel_id=1, source_target_pairs={{0,8},{8,0},{16,24},{24,16},{1,9},{9,1},{17,25},{25,17},{2,10},{10... | collective-permute-start | bytes 1622024 | tf_op jit(solution)/shard_map/ppermute | solution.py:434
  37.5 0.5 collective-permute-start.7
  38.0 0.0 collective-permute-done.10
  38.0 3.7 %collective-permute-start.11 = (f32[136,128]{1,0:T(8,128)S(1)}, f32[136,128]{1,0:T(8,128)S(1)}, u32[]{:S(2)}, u32[]{:S(2)}) collective-permute-start(f32[136,128]{1,0:T(8,128)S(1)} %get-tuple-element.34), channel_id=1, source_target_pairs={{0,6},{1,7},{2,4},{3,5},{4,2},{5,3},{6,0},{7,1},{8,14},{9,15},{10,... | collective-permute-start | bytes 208904 | tf_op jit(solution)/shard_map/ppermute | solution.py:434
  41.7 0.0 collective-permute-start.12
  41.7 0.8 %collective-permute-start.13 = (f32[136,128]{1,0:T(8,128)S(1)}, f32[136,128]{1,0:T(8,128)S(1)}, u32[]{:S(2)}, u32[]{:S(2)}) collective-permute-start(f32[136,128]{1,0:T(8,128)S(1)} %get-tuple-element.33), channel_id=1, source_target_pairs={{0,2},{1,3},{2,0},{3,1},{4,6},{5,7},{6,4},{7,5},{8,10},{9,11},{10,... | collective-permute-start | bytes 208904 | tf_op jit(solution)/shard_map/ppermute | solution.py:434
  42.5 2.2 %collective-permute-done.11 = f32[136,128]{1,0:T(8,128)S(1)} collective-permute-done((f32[136,128]{1,0:T(8,128)S(1)}, f32[136,128]{1,0:T(8,128)S(1)}, u32[]{:S(2)}, u32[]{:S(2)}) %collective-permute-start.11) | collective-permute-done | bytes 69664 | tf_op jit(solution)/shard_map/ppermute | solution.py:434
  44.7 3.0 %collective-permute-done.12 = f32[136,128]{1,0:T(8,128)S(1)} collective-permute-done((f32[136,128]{1,0:T(8,128)S(1)}, f32[136,128]{1,0:T(8,128)S(1)}, u32[]{:S(2)}, u32[]{:S(2)}) %collective-permute-start.12) | collective-permute-done | bytes 69664 | tf_op jit(solution)/shard_map/ppermute | solution.py:434
  47.7 0.0 collective-permute-done.13
  47.7 1.6 %collective-permute-start.14 = (f32[136,128]{1,0:T(8,128)S(1)}, f32[136,128]{1,0:T(8,128)S(1)}, u32[]{:S(2)}, u32[]{:S(2)}) collective-permute-start(f32[136,128]{1,0:T(8,128)S(1)} %fusion.1), channel_id=1, source_target_pairs={{0,24},{8,16},{16,8},{24,0},{1,25},{9,17},{17,9},{25,1},{2,26},{10... | collective-permute-start | bytes 208904 | tf_op jit(solution)/shard_map/ppermute | solution.py:434
  49.3 1.0 %collective-permute-start.15 = (f32[136,128]{1,0:T(8,128)S(1)}, f32[136,128]{1,0:T(8,128)S(1)}, u32[]{:S(2)}, u32[]{:S(2)}) collective-permute-start(f32[136,128]{1,0:T(8,128)S(1)} %fusion.1), channel_id=1, source_target_pairs={{0,16},{8,24},{16,0},{24,8},{1,17},{9,25},{17,1},{25,9},{2,18},{10... | collective-permute-start | bytes 208904 | tf_op jit(solution)/shard_map/ppermute | solution.py:434
  50.3 1.0 %collective-permute-start.16 = (f32[136,128]{1,0:T(8,128)S(1)}, f32[136,128]{1,0:T(8,128)S(1)}, u32[]{:S(2)}, u32[]{:S(2)}) collective-permute-start(f32[136,128]{1,0:T(8,128)S(1)} %fusion.1), channel_id=1, source_target_pairs={{0,8},{8,0},{16,24},{24,16},{1,9},{9,1},{17,25},{25,17},{2,10},{10... | collective-permute-start | bytes 208904 | tf_op jit(solution)/shard_map/ppermute | solution.py:434
  51.3 0.0 collective-permute-done.6.mx.refs_1_
  51.3 2.8 %collective-permute-done.7.my.refs_2_ = f32[528,256]{1,0:T(8,128)S(1)} collective-permute-done((f32[528,256]{1,0:T(8,128)S(1)}, f32[528,256]{1,0:T(8,128)S(1)}, u32[]{:S(2)}, u32[]{:S(2)}) %collective-permute-start.7) | collective-permute-done | bytes 540704 | tf_op jit(solution)/shard_map/ppermute | solution.py:434
  54.1 0.1 second_step.1
  54.1 0.1 collective-permute-start.8
  54.2 0.1 collective-permute-start.9
  54.3 0.0 collective-permute-done.14
  54.3 0.5 collective-permute-done.15
  54.8 0.0 collective-permute-done.16
  54.9 3.7 %collective-permute-start.17 = (f32[136,128]{1,0:T(8,128)S(1)}, f32[136,128]{1,0:T(8,128)S(1)}, u32[]{:S(2)}, u32[]{:S(2)}) collective-permute-start(f32[136,128]{1,0:T(8,128)S(1)} %add_add_fusion.refs_8_), channel_id=1, source_target_pairs={{0,6},{1,7},{2,4},{3,5},{4,2},{5,3},{6,0},{7,1},{8,14},{9,15},{10,... | collective-permute-start | bytes 208904 | tf_op jit(solution)/shard_map/ppermute | solution.py:434
  58.5 0.0 collective-permute-start.18
  58.5 0.8 %collective-permute-start.19 = (f32[136,128]{1,0:T(8,128)S(1)}, f32[136,128]{1,0:T(8,128)S(1)}, u32[]{:S(2)}, u32[]{:S(2)}) collective-permute-start(f32[136,128]{1,0:T(8,128)S(1)} %add_add_fusion.refs_8_), channel_id=1, source_target_pairs={{0,2},{1,3},{2,0},{3,1},{4,6},{5,7},{6,4},{7,5},{8,10},{9,11},{10,... | collective-permute-start | bytes 208904 | tf_op jit(solution)/shard_map/ppermute | solution.py:434
  59.3 2.4 %collective-permute-done.17.refs_5_ = f32[136,128]{1,0:T(8,128)S(1)} collective-permute-done((f32[136,128]{1,0:T(8,128)S(1)}, f32[136,128]{1,0:T(8,128)S(1)}, u32[]{:S(2)}, u32[]{:S(2)}) %collective-permute-start.17) | collective-permute-done | bytes 69664 | tf_op jit(solution)/shard_map/ppermute | solution.py:434
  61.7 0.0 collective-permute-start.23
  61.7 2.3 %collective-permute-done.18.refs_6_ = f32[136,128]{1,0:T(8,128)S(1)} collective-permute-done((f32[136,128]{1,0:T(8,128)S(1)}, f32[136,128]{1,0:T(8,128)S(1)}, u32[]{:S(2)}, u32[]{:S(2)}) %collective-permute-start.18) | collective-permute-done | bytes 69664 | tf_op jit(solution)/shard_map/ppermute | solution.py:434
  64.1 0.0 collective-permute-start.20
  64.1 0.1 collective-permute-done.19.refs_7_
  64.1 0.5 collective-permute-start.21
  64.6 0.0 collective-permute-done.23.refs_12_
  64.6 0.1 collective-permute-start.22
  64.6 0.7 collective-permute-done.20.refs_9_
  65.3 0.2 collective-permute-done.21.refs_10_
  65.5 0.4 collective-permute-done.22.refs_11_
  65.8 0.0 collective-permute-done.8.refs_3_
  65.8 0.0 collective-permute-done.9.refs_4_
  65.8 8.5 %finish.1 = (f32[1296,512]{1,0:T(8,128)}, f32[1296,512]{1,0:T(8,128)}) custom-call(f32[672,256]{1,0:T(8,128)S(1)} %momentum_update.1.m.refs_0_, f32[528,256]{1,0:T(8,128)S(1)} %collective-permute-done.6.mx.refs_1_, f32[528,256]{1,0:T(8,128)S(1)} %collective-permute-done.7.my.refs_2_, f32[480,256]{1,0:T(8,128)S(1)} %collective-permute-done.8.refs_3_, ...), custom_call_target="tpu_custom_call" | custom-call | tf_op jit(solution)/shard_map/finish/pallas_call | solution.py:412
  (6 shorter events, 0.2 us)
Async XLA Ops:
  7.2 11.9 %collective-permute-start.4 = (f32[336,256]{1,0:T(8,128)S(1)}, f32[336,256]{1,0:T(8,128)S(1)}, u32[]{:S(2)}, u32[]{:S(2)}) collective-permute-start(f32[336,256]{1,0:T(8,128)S(1)} %get-tuple-element.25), channel_id=1, source_target_pairs={{0,16},{8,24},{16,0},{24,8},{1,17},{9,25},{17,1},{25,9},{2,18},{10... | collective-permute-start | bytes 1032200 | tf_op jit(solution)/shard_map/ppermute | solution.py:434
  10.2 11.0 %collective-permute-start.2 = (f32[336,256]{1,0:T(8,128)S(1)}, f32[336,256]{1,0:T(8,128)S(1)}, u32[]{:S(2)}, u32[]{:S(2)}) collective-permute-start(f32[336,256]{1,0:T(8,128)S(1)} %get-tuple-element.23), channel_id=1, source_target_pairs={{0,8},{8,0},{16,24},{24,16},{1,9},{9,1},{17,25},{25,17},{2,10},{10... | collective-permute-start | bytes 1032200 | tf_op jit(solution)/shard_map/ppermute | solution.py:434
  14.8 13.7 %collective-permute-start = (f32[336,256]{1,0:T(8,128)S(1)}, f32[336,256]{1,0:T(8,128)S(1)}, u32[]{:S(2)}, u32[]{:S(2)}) collective-permute-start(f32[336,256]{1,0:T(8,128)S(1)} %get-tuple-element.20), channel_id=1, source_target_pairs={{0,8},{8,0},{16,24},{24,16},{1,9},{9,1},{17,25},{25,17},{2,10},{10... | collective-permute-start | bytes 1032200 | tf_op jit(solution)/shard_map/ppermute | solution.py:434
  15.5 13.1 %collective-permute-start.1 = (f32[336,256]{1,0:T(8,128)S(1)}, f32[336,256]{1,0:T(8,128)S(1)}, u32[]{:S(2)}, u32[]{:S(2)}) collective-permute-start(f32[336,256]{1,0:T(8,128)S(1)} %get-tuple-element.21), channel_id=1, source_target_pairs={{0,16},{8,24},{16,0},{24,8},{1,17},{9,25},{17,1},{25,9},{2,18},{10... | collective-permute-start | bytes 1032200 | tf_op jit(solution)/shard_map/ppermute | solution.py:434
  19.1 15.3 %collective-permute-start.5 = (f32[336,256]{1,0:T(8,128)S(1)}, f32[336,256]{1,0:T(8,128)S(1)}, u32[]{:S(2)}, u32[]{:S(2)}) collective-permute-start(f32[336,256]{1,0:T(8,128)S(1)} %add.28), channel_id=1, source_target_pairs={{0,8},{8,0},{16,24},{24,16},{1,9},{9,1},{17,25},{25,17},{2,10},{10... | collective-permute-start | bytes 1032200 | tf_op jit(solution)/shard_map/ppermute | solution.py:434
  21.3 4.6 %copy-start = (f32[1296,512]{1,0:T(8,128)S(1)}, f32[1296,512]{1,0:T(8,128)}, u32[]{:S(2)}) copy-start(f32[1296,512]{1,0:T(8,128)} %m_ref.1) | copy-start | bytes 7962628
  21.3 13.2 %collective-permute-start.3 = (f32[336,256]{1,0:T(8,128)S(1)}, f32[336,256]{1,0:T(8,128)S(1)}, u32[]{:S(2)}, u32[]{:S(2)}) collective-permute-start(f32[336,256]{1,0:T(8,128)S(1)} %add.27), channel_id=1, source_target_pairs={{0,16},{8,24},{16,0},{24,8},{1,17},{9,25},{17,1},{25,9},{2,18},{10... | collective-permute-start | bytes 1032200 | tf_op jit(solution)/shard_map/ppermute | solution.py:434
  35.7 2.2 %collective-permute-start.10 = (f32[4,136,128]{2,1,0:T(8,128)S(1)}, f32[4,136,128]{2,1,0:T(8,128)S(1)}, u32[]{:S(2)}, u32[]{:S(2)}) collective-permute-start(f32[4,136,128]{2,1,0:T(8,128)S(1)} %get-tuple-element.29), channel_id=1, source_target_pairs={{0,1},{1,0},{2,3},{3,2},{4,5},{5,4},{6,7},{7,6},{8,9},{9,8},{10,11... | collective-permute-start | bytes 835592 | tf_op jit(solution)/shard_map/ppermute | solution.py:434
  35.9 15.4 %collective-permute-start.6 = (f32[528,256]{1,0:T(8,128)S(1)}, f32[528,256]{1,0:T(8,128)S(1)}, u32[]{:S(2)}, u32[]{:S(2)}) collective-permute-start(f32[528,256]{1,0:T(8,128)S(1)} %get-tuple-element.31), channel_id=1, source_target_pairs={{0,8},{8,0},{16,24},{24,16},{1,9},{9,1},{17,25},{25,17},{2,10},{10... | collective-permute-start | bytes 1622024 | tf_op jit(solution)/shard_map/ppermute | solution.py:434
  37.5 16.6 %collective-permute-start.7 = (f32[528,256]{1,0:T(8,128)S(1)}, f32[528,256]{1,0:T(8,128)S(1)}, u32[]{:S(2)}, u32[]{:S(2)}) collective-permute-start(f32[528,256]{1,0:T(8,128)S(1)} %get-tuple-element.30), channel_id=1, source_target_pairs={{0,16},{8,24},{16,0},{24,8},{1,17},{9,25},{17,1},{25,9},{2,18},{10... | collective-permute-start | bytes 1622024 | tf_op jit(solution)/shard_map/ppermute | solution.py:434
  38.0 6.7 %collective-permute-start.11 = (f32[136,128]{1,0:T(8,128)S(1)}, f32[136,128]{1,0:T(8,128)S(1)}, u32[]{:S(2)}, u32[]{:S(2)}) collective-permute-start(f32[136,128]{1,0:T(8,128)S(1)} %get-tuple-element.34), channel_id=1, source_target_pairs={{0,6},{1,7},{2,4},{3,5},{4,2},{5,3},{6,0},{7,1},{8,14},{9,15},{10,... | collective-permute-start | bytes 208904 | tf_op jit(solution)/shard_map/ppermute | solution.py:434
  41.7 6.0 %collective-permute-start.12 = (f32[136,128]{1,0:T(8,128)S(1)}, f32[136,128]{1,0:T(8,128)S(1)}, u32[]{:S(2)}, u32[]{:S(2)}) collective-permute-start(f32[136,128]{1,0:T(8,128)S(1)} %get-tuple-element.32), channel_id=1, source_target_pairs={{0,4},{1,5},{2,6},{3,7},{4,0},{5,1},{6,2},{7,3},{8,12},{9,13},{10,... | collective-permute-start | bytes 208904 | tf_op jit(solution)/shard_map/ppermute | solution.py:434
  41.7 6.0 %collective-permute-start.13 = (f32[136,128]{1,0:T(8,128)S(1)}, f32[136,128]{1,0:T(8,128)S(1)}, u32[]{:S(2)}, u32[]{:S(2)}) collective-permute-start(f32[136,128]{1,0:T(8,128)S(1)} %get-tuple-element.33), channel_id=1, source_target_pairs={{0,2},{1,3},{2,0},{3,1},{4,6},{5,7},{6,4},{7,5},{8,10},{9,11},{10,... | collective-permute-start | bytes 208904 | tf_op jit(solution)/shard_map/ppermute | solution.py:434
  47.7 6.6 %collective-permute-start.14 = (f32[136,128]{1,0:T(8,128)S(1)}, f32[136,128]{1,0:T(8,128)S(1)}, u32[]{:S(2)}, u32[]{:S(2)}) collective-permute-start(f32[136,128]{1,0:T(8,128)S(1)} %fusion.1), channel_id=1, source_target_pairs={{0,24},{8,16},{16,8},{24,0},{1,25},{9,17},{17,9},{25,1},{2,26},{10... | collective-permute-start | bytes 208904 | tf_op jit(solution)/shard_map/ppermute | solution.py:434
  49.3 5.5 %collective-permute-start.15 = (f32[136,128]{1,0:T(8,128)S(1)}, f32[136,128]{1,0:T(8,128)S(1)}, u32[]{:S(2)}, u32[]{:S(2)}) collective-permute-start(f32[136,128]{1,0:T(8,128)S(1)} %fusion.1), channel_id=1, source_target_pairs={{0,16},{8,24},{16,0},{24,8},{1,17},{9,25},{17,1},{25,9},{2,18},{10... | collective-permute-start | bytes 208904 | tf_op jit(solution)/shard_map/ppermute | solution.py:434
  50.3 4.5 %collective-permute-start.16 = (f32[136,128]{1,0:T(8,128)S(1)}, f32[136,128]{1,0:T(8,128)S(1)}, u32[]{:S(2)}, u32[]{:S(2)}) collective-permute-start(f32[136,128]{1,0:T(8,128)S(1)} %fusion.1), channel_id=1, source_target_pairs={{0,8},{8,0},{16,24},{24,16},{1,9},{9,1},{17,25},{25,17},{2,10},{10... | collective-permute-start | bytes 208904 | tf_op jit(solution)/shard_map/ppermute | solution.py:434
  54.1 11.7 %collective-permute-start.8 = (f32[480,256]{1,0:T(8,128)S(1)}, f32[480,256]{1,0:T(8,128)S(1)}, u32[]{:S(2)}, u32[]{:S(2)}) collective-permute-start(f32[480,256]{1,0:T(8,128)S(1)} %get-tuple-element.26), channel_id=1, source_target_pairs={{0,8},{8,0},{16,24},{24,16},{1,9},{9,1},{17,25},{25,17},{2,10},{10... | collective-permute-start | bytes 1474568 | tf_op jit(solution)/shard_map/ppermute | solution.py:434
  54.2 11.6 %collective-permute-start.9 = (f32[480,256]{1,0:T(8,128)S(1)}, f32[480,256]{1,0:T(8,128)S(1)}, u32[]{:S(2)}, u32[]{:S(2)}) collective-permute-start(f32[480,256]{1,0:T(8,128)S(1)} %get-tuple-element.27), channel_id=1, source_target_pairs={{0,16},{8,24},{16,0},{24,8},{1,17},{9,25},{17,1},{25,9},{2,18},{10... | collective-permute-start | bytes 1474568 | tf_op jit(solution)/shard_map/ppermute | solution.py:434
  54.9 6.9 %collective-permute-start.17 = (f32[136,128]{1,0:T(8,128)S(1)}, f32[136,128]{1,0:T(8,128)S(1)}, u32[]{:S(2)}, u32[]{:S(2)}) collective-permute-start(f32[136,128]{1,0:T(8,128)S(1)} %add_add_fusion.refs_8_), channel_id=1, source_target_pairs={{0,6},{1,7},{2,4},{3,5},{4,2},{5,3},{6,0},{7,1},{8,14},{9,15},{10,... | collective-permute-start | bytes 208904 | tf_op jit(solution)/shard_map/ppermute | solution.py:434
  58.5 5.5 %collective-permute-start.18 = (f32[136,128]{1,0:T(8,128)S(1)}, f32[136,128]{1,0:T(8,128)S(1)}, u32[]{:S(2)}, u32[]{:S(2)}) collective-permute-start(f32[136,128]{1,0:T(8,128)S(1)} %add_add_fusion.refs_8_), channel_id=1, source_target_pairs={{0,4},{1,5},{2,6},{3,7},{4,0},{5,1},{6,2},{7,3},{8,12},{9,13},{10,... | collective-permute-start | bytes 208904 | tf_op jit(solution)/shard_map/ppermute | solution.py:434
  58.5 5.6 %collective-permute-start.19 = (f32[136,128]{1,0:T(8,128)S(1)}, f32[136,128]{1,0:T(8,128)S(1)}, u32[]{:S(2)}, u32[]{:S(2)}) collective-permute-start(f32[136,128]{1,0:T(8,128)S(1)} %add_add_fusion.refs_8_), channel_id=1, source_target_pairs={{0,2},{1,3},{2,0},{3,1},{4,6},{5,7},{6,4},{7,5},{8,10},{9,11},{10,... | collective-permute-start | bytes 208904 | tf_op jit(solution)/shard_map/ppermute | solution.py:434
  61.7 2.8 %collective-permute-start.23 = (f32[136,128]{1,0:T(8,128)S(1)}, f32[136,128]{1,0:T(8,128)S(1)}, u32[]{:S(2)}, u32[]{:S(2)}) collective-permute-start(f32[136,128]{1,0:T(8,128)S(1)} %add_add_fusion.refs_8_), channel_id=1, source_target_pairs={{0,1},{1,0},{2,3},{3,2},{4,5},{5,4},{6,7},{7,6},{8,9},{9,8},{10,11... | collective-permute-start | bytes 208904 | tf_op jit(solution)/shard_map/ppermute | solution.py:434
  64.1 1.3 %collective-permute-start.20 = (f32[136,128]{1,0:T(8,128)S(1)}, f32[136,128]{1,0:T(8,128)S(1)}, u32[]{:S(2)}, u32[]{:S(2)}) collective-permute-start(f32[136,128]{1,0:T(8,128)S(1)} %collective-permute-done.17.refs_5_), channel_id=1, source_target_pairs={{0,1},{1,0},{2,3},{3,2},{4,5},{5,4},{6,7},{7,6},{8,9},{9,8},{10,11... | collective-permute-start | bytes 208904 | tf_op jit(solution)/shard_map/ppermute | solution.py:434
  64.1 1.4 %collective-permute-start.21 = (f32[136,128]{1,0:T(8,128)S(1)}, f32[136,128]{1,0:T(8,128)S(1)}, u32[]{:S(2)}, u32[]{:S(2)}) collective-permute-start(f32[136,128]{1,0:T(8,128)S(1)} %collective-permute-done.18.refs_6_), channel_id=1, source_target_pairs={{0,1},{1,0},{2,3},{3,2},{4,5},{5,4},{6,7},{7,6},{8,9},{9,8},{10,11... | collective-permute-start | bytes 208904 | tf_op jit(solution)/shard_map/ppermute | solution.py:434
  64.6 1.3 %collective-permute-start.22 = (f32[136,128]{1,0:T(8,128)S(1)}, f32[136,128]{1,0:T(8,128)S(1)}, u32[]{:S(2)}, u32[]{:S(2)}) collective-permute-start(f32[136,128]{1,0:T(8,128)S(1)} %collective-permute-done.19.refs_7_), channel_id=1, source_target_pairs={{0,1},{1,0},{2,3},{3,2},{4,5},{5,4},{6,7},{7,6},{8,9},{9,8},{10,11... | collective-permute-start | bytes 208904 | tf_op jit(solution)/shard_map/ppermute | solution.py:434

commit v7 on v6

--- a/solution.py
+++ b/solution.py
@@ -223,13 +223,19 @@
     out = []
     for i in range(4):
         a, b = slice(128 * i, 128 * i + 128), slice(128 * i, 512)
-        out.append(dot_t(hi[:, a], hi[:, b]) + (dot_t(hi[:, a], lo[:, b]) + dot_t(lo[:, a], hi[:, b])))
+        width = 512 - 128 * i
+        both = dot_t(hi[:, a], jnp.concatenate([hi[:, b], lo[:, b]], 1))
+        out.append(both[:, :width] + (both[:, width:] + dot_t(lo[:, a], hi[:, b])))
     return out
 
 
-def gram_kernel(m, keep, send):
+def step_kernel(taps, cp, more, m_ref, *refs):
+    m, fx, fy, keep, send = refs[-5:]
+    update_kernel(taps, cp, m_ref, *refs[:-5], m)
+    rows = taps * cp
+    fx[...] = m[: rows + more, :]
+    fy[...] = m[rows - more :, :]
     z, core = lax.axis_index("shard") // 2, lax.axis_index("shard") % 2
-    rows = m.shape[0] // 2
     gram = upper_gram(jnp.concatenate([m[:rows], m[rows:]], 1))
     row = lax.broadcasted_iota(jnp.int32, (128, 128), 0)
     col = lax.broadcasted_iota(jnp.int32, (128, 128), 1)
@@ -253,15 +259,18 @@
                 send[r ^ z] = piece
 
 
-def own_gram(m):
-    return pl.pallas_call(
-        gram_kernel,
-        out_shape=[pltpu.VMEM((4,) + PIECE, F32)] * 2,
-        in_specs=[VMEM],
-        out_specs=[VMEM] * 2,
-        compiler_params=params(),
-        name="own_gram",
-    )(near(m))
+def step(own, parts, taps, cp, more):
+    rows = taps * cp
+    return pl.pallas_call(
+        functools.partial(step_kernel, taps, cp, more),
+        out_shape=[pltpu.VMEM((2 * rows, 256), F32)]
+        + [pltpu.VMEM((rows + more, 256), F32)] * 2
+        + [pltpu.VMEM((4,) + PIECE, F32)] * 2,
+        in_specs=[VMEM] * (1 + len(parts)),
+        out_specs=[VMEM] * 5,
+        compiler_params=params(),
+        name="momentum_gram",
+    )(near(own), *map(near, parts))
 
 
 def any_gram_kernel(m, g_ref):
@@ -314,7 +323,7 @@
     else:
         z, core = lax.axis_index("shard") // 2, lax.axis_index("shard") % 2
         for n, part in enumerate(parts):
-            which, r = n // 4, 3 - n % 4
+            which, r = n // 4, (2, 3, 1, 0)[n % 4]
             q = z ^ r
             for half in range(2):
 
@@ -352,7 +361,7 @@
 
 
 def row_cuts(rows):
-    cuts = [min(rows, -(-rows * k // 24) * 8) for k in range(4)]
+    cuts = [min(rows, -(-rows * k // 128) * 8) for k in (0, 7, 13, 16)]
     return [(a, b) for a, b in zip(cuts, cuts[1:]) if b > a]
 
 
@@ -470,18 +479,16 @@
     a2, b2 = over_y(a2 + a3), over_x(b2 + b3)
     a0, b0 = conv_more(cot, v, chunk_pair(0, 0), 1, taps, cp)
     own = own_momentum(momentum, taps, cp)
-    m = momentum_update(own, (a0, b0, a1, b1, a2, b2), taps, cp)
     rows = taps * cp
     more = 4 * cp
-    mx, my = over_x(m[: rows + more]), over_y(m[rows - more :])
-    keep, send = own_gram(m)
+    m, fx, fy, keep, send = step(own, (a0, b0, a1, b1, a2, b2), taps, cp, more)
+    mx, my = over_x(fx), over_y(fy)
     g = keep + over_core(send)
-    z3, z2, z1 = [over_z(g[r], r) for r in (3, 2, 1)]
-    g = (z3 + z2) + (z1 + g[0])
+    za, zb, zc = [over_z(g[r], r) for r in (2, 3, 1)]
+    g = (za + zb) + (zc + g[0])
     d3, d1, d2 = [swap(g, "dp", 4, r) for r in (3, 1, 2)]
     g = (d3 + d2) + (d1 + g)
-    z3, z2, z1 = [over_z(g, r) for r in (3, 2, 1)]
-    g = [z3, z2, z1, g]
+    g = [over_z(g, r) for r in (2, 3, 1)] + [g]
     g = g + [over_core(x) for x in g]
     nx, ny = second_step(m, mx, my, more)
     nx, ny = over_x(nx), over_y(ny)

time: 74.6 us -> 74.1 us (level)
  transfers between devices with their start and end apart: 24 -> 24, of which waited for: 13 -> 15; matrix products, arithmetic and copies ran while one was open for 0% -> 0% of each run, Pallas kernels for 13% -> 13%
where the time goes in v7:
time: 74.1 us; the launch traced here: 73.9 us
  Pallas kernels  26 us (35%)
  starting transfers between devices  24.1 us (33%)
  waiting for transfers between devices  22.7 us (31%)
  between operations  0.9 us (1%)
    ppermute x24, starting transfers between devices, swap(): return lax.ppermute(x, axis, [(i, i ^ bit) for i in range(size)])  24.1 us
    ppermute x24, waiting for transfers between devices, swap(): return lax.ppermute(x, axis, [(i, i ^ bit) for i in range(size)])  22.7 us
    pallas_call x3, Pallas kernels, conv_more(): pl.pallas_call(functools.partial(more_kernel, depth, cp, taps, chunks), o...  9.3 us
    pallas_call x1, Pallas kernels, finish(): pl.pallas_call(functools.partial(finish_kernel, taps, cp, chans, known, l...  8.36 us
    pallas_call x1, Pallas kernels, conv(): pl.pallas_call(functools.partial(conv_kernel, depth, cp, taps, chunks), o...  6.53 us
  transfers between devices with their start and end apart: 24, of which 15 were waited for; matrix products, arithmetic and copies ran while one was open for 0% of the time, Pallas kernels for 13%

profile of v7, /device:TPU:0, one launch (start us, length us, event | category | flops | bytes accessed | tf_op | source)
XLA Modules:
  0.0 73.9 jit_solution(16754505243925094960)
XLA Ops:
  0.6 6.5 %conv_first.1 = (f32[336,256]{1,0:T(8,128)S(1)}, f32[336,256]{1,0:T(8,128)S(1)}, bf16[8192,512]{1,0:T(8,128)(2,1)S(1)}, bf16[864,2304]{1,0:T(8,128)(2,1)S(1)}) custom-call(bf16[48,11560]{1,0:T(8,128)(2,1)} %x_hbm.1, bf16[8192,512]{1,0:T(8,128)(2,1)} %cot_hbm.1), custom_call_target="tpu_custom_call" | custom-call | tf_op jit(solution)/shard_map/conv_first/pallas_call | solution.py:129
  7.2 3.0 %collective-permute-start.4 = (f32[336,256]{1,0:T(8,128)S(1)}, f32[336,256]{1,0:T(8,128)S(1)}, u32[]{:S(2)}, u32[]{:S(2)}) collective-permute-start(f32[336,256]{1,0:T(8,128)S(1)} %get-tuple-element.28), channel_id=1, source_target_pairs={{0,16},{8,24},{16,0},{24,8},{1,17},{9,25},{17,1},{25,9},{2,18},{10... | collective-permute-start | bytes 1032200 | tf_op jit(solution)/shard_map/ppermute | solution.py:443
  10.2 1.5 %collective-permute-start.2 = (f32[336,256]{1,0:T(8,128)S(1)}, f32[336,256]{1,0:T(8,128)S(1)}, u32[]{:S(2)}, u32[]{:S(2)}) collective-permute-start(f32[336,256]{1,0:T(8,128)S(1)} %get-tuple-element.26), channel_id=1, source_target_pairs={{0,8},{8,0},{16,24},{24,16},{1,9},{9,1},{17,25},{25,17},{2,10},{10... | collective-permute-start | bytes 1032200 | tf_op jit(solution)/shard_map/ppermute | solution.py:443
  11.7 3.1 %conv_more.4 = (f32[336,256]{1,0:T(8,128)S(1)}, f32[336,256]{1,0:T(8,128)S(1)}) custom-call(bf16[8192,512]{1,0:T(8,128)(2,1)S(1)} %get-tuple-element.19.cot, bf16[864,2304]{1,0:T(8,128)(2,1)S(1)} %get-tuple-element.20.v), custom_call_target="tpu_custom_call" | custom-call | tf_op jit(solution)/shard_map/conv_more/pallas_call | solution.py:154
  14.8 0.7 collective-permute-start
  15.5 0.0 collective-permute-start.1
  15.5 3.1 %conv_more.5 = (f32[336,256]{1,0:T(8,128)S(1)}, f32[336,256]{1,0:T(8,128)S(1)}) custom-call(bf16[8192,512]{1,0:T(8,128)(2,1)S(1)} %get-tuple-element.19.cot, bf16[864,2304]{1,0:T(8,128)(2,1)S(1)} %get-tuple-element.20.v), custom_call_target="tpu_custom_call" | custom-call | tf_op jit(solution)/shard_map/conv_more/pallas_call | solution.py:154
  18.7 0.4 collective-permute-done.4
  19.1 2.1 %collective-permute-start.5 = (f32[336,256]{1,0:T(8,128)S(1)}, f32[336,256]{1,0:T(8,128)S(1)}, u32[]{:S(2)}, u32[]{:S(2)}) collective-permute-start(f32[336,256]{1,0:T(8,128)S(1)} %add.28), channel_id=1, source_target_pairs={{0,8},{8,0},{16,24},{24,16},{1,9},{9,1},{17,25},{25,17},{2,10},{10... | collective-permute-start | bytes 1032200 | tf_op jit(solution)/shard_map/ppermute | solution.py:443
  21.2 0.0 collective-permute-done.2
  21.3 0.0 copy-start
  21.3 1.6 %collective-permute-start.3 = (f32[336,256]{1,0:T(8,128)S(1)}, f32[336,256]{1,0:T(8,128)S(1)}, u32[]{:S(2)}, u32[]{:S(2)}) collective-permute-start(f32[336,256]{1,0:T(8,128)S(1)} %add.27), channel_id=1, source_target_pairs={{0,16},{8,24},{16,0},{24,8},{1,17},{9,25},{17,1},{25,9},{2,18},{10... | collective-permute-start | bytes 1032200 | tf_op jit(solution)/shard_map/ppermute | solution.py:443
  22.9 3.0 %conv_more.3 = (f32[336,256]{1,0:T(8,128)S(1)}, f32[336,256]{1,0:T(8,128)S(1)}) custom-call(bf16[8192,512]{1,0:T(8,128)(2,1)S(1)} %get-tuple-element.19.cot, bf16[864,2304]{1,0:T(8,128)(2,1)S(1)} %get-tuple-element.20.v), custom_call_target="tpu_custom_call" | custom-call | tf_op jit(solution)/shard_map/conv_more/pallas_call | solution.py:154
  25.9 0.0 copy-done
  25.9 0.6 own_momentum.1.m_ref
  26.5 2.1 %collective-permute-done.refs_2_ = f32[336,256]{1,0:T(8,128)S(1)} collective-permute-done((f32[336,256]{1,0:T(8,128)S(1)}, f32[336,256]{1,0:T(8,128)S(1)}, u32[]{:S(2)}, u32[]{:S(2)}) %collective-permute-start) | collective-permute-done | bytes 344096 | tf_op jit(solution)/shard_map/ppermute | solution.py:443
  28.6 0.0 collective-permute-done.1.refs_3_
  28.6 5.9 %collective-permute-done.5.refs_5_ = f32[336,256]{1,0:T(8,128)S(1)} collective-permute-done((f32[336,256]{1,0:T(8,128)S(1)}, f32[336,256]{1,0:T(8,128)S(1)}, u32[]{:S(2)}, u32[]{:S(2)}) %collective-permute-start.5) | collective-permute-done | bytes 344096 | tf_op jit(solution)/shard_map/ppermute | solution.py:443
  34.5 0.0 collective-permute-done.3.refs_4_
  34.5 1.2 %momentum_gram.1 = (f32[672,256]{1,0:T(8,128)S(1)}, f32[528,256]{1,0:T(8,128)S(1)}, f32[528,256]{1,0:T(8,128)S(1)}, f32[4,136,128]{2,1,0:T(8,128)S(1)}, f32[4,136,128]{2,1,0:T(8,128)S(1)}) custom-call(f32[336,512]{1,0:T(8,128)S(1)} %own_momentum.1.m_ref, f32[336,256]{1,0:T(8,128)S(1)} %get-tuple-element.21.refs_0_, ...), custom_call_target="tpu_custom_call" | custom-call | tf_op jit(solution)/shard_map/momentum_gram/pallas_call | solution.py:264
  35.7 0.1 collective-permute-start.10
  35.8 1.5 %collective-permute-start.6 = (f32[528,256]{1,0:T(8,128)S(1)}, f32[528,256]{1,0:T(8,128)S(1)}, u32[]{:S(2)}, u32[]{:S(2)}) collective-permute-start(f32[528,256]{1,0:T(8,128)S(1)} %get-tuple-element.30), channel_id=1, source_target_pairs={{0,8},{8,0},{16,24},{24,16},{1,9},{9,1},{17,25},{25,17},{2,10},{10... | collective-permute-start | bytes 1622024 | tf_op jit(solution)/shard_map/ppermute | solution.py:443
  37.3 0.5 collective-permute-start.7
  37.8 0.0 collective-permute-done.10
  37.9 2.7 %collective-permute-start.11 = (f32[136,128]{1,0:T(8,128)S(1)}, f32[136,128]{1,0:T(8,128)S(1)}, u32[]{:S(2)}, u32[]{:S(2)}) collective-permute-start(f32[136,128]{1,0:T(8,128)S(1)} %get-tuple-element.38), channel_id=1, source_target_pairs={{0,4},{1,5},{2,6},{3,7},{4,0},{5,1},{6,2},{7,3},{8,12},{9,13},{10,... | collective-permute-start | bytes 208904 | tf_op jit(solution)/shard_map/ppermute | solution.py:443
  40.5 1.3 %collective-permute-start.12 = (f32[136,128]{1,0:T(8,128)S(1)}, f32[136,128]{1,0:T(8,128)S(1)}, u32[]{:S(2)}, u32[]{:S(2)}) collective-permute-start(f32[136,128]{1,0:T(8,128)S(1)} %get-tuple-element.36), channel_id=1, source_target_pairs={{0,6},{1,7},{2,4},{3,5},{4,2},{5,3},{6,0},{7,1},{8,14},{9,15},{10,... | collective-permute-start | bytes 208904 | tf_op jit(solution)/shard_map/ppermute | solution.py:443
  41.9 0.2 collective-permute-start.13
  42.1 3.6 %collective-permute-done.11 = f32[136,128]{1,0:T(8,128)S(1)} collective-permute-done((f32[136,128]{1,0:T(8,128)S(1)}, f32[136,128]{1,0:T(8,128)S(1)}, u32[]{:S(2)}, u32[]{:S(2)}) %collective-permute-start.11) | collective-permute-done | bytes 69664 | tf_op jit(solution)/shard_map/ppermute | solution.py:443
  45.7 1.2 %collective-permute-done.12 = f32[136,128]{1,0:T(8,128)S(1)} collective-permute-done((f32[136,128]{1,0:T(8,128)S(1)}, f32[136,128]{1,0:T(8,128)S(1)}, u32[]{:S(2)}, u32[]{:S(2)}) %collective-permute-start.12) | collective-permute-done | bytes 69664 | tf_op jit(solution)/shard_map/ppermute | solution.py:443
  46.9 0.3 collective-permute-done.13
  47.2 1.6 %collective-permute-start.14 = (f32[136,128]{1,0:T(8,128)S(1)}, f32[136,128]{1,0:T(8,128)S(1)}, u32[]{:S(2)}, u32[]{:S(2)}) collective-permute-start(f32[136,128]{1,0:T(8,128)S(1)} %fusion.1), channel_id=1, source_target_pairs={{0,24},{8,16},{16,8},{24,0},{1,25},{9,17},{17,9},{25,1},{2,26},{10... | collective-permute-start | bytes 208904 | tf_op jit(solution)/shard_map/ppermute | solution.py:443
  48.8 1.2 %collective-permute-start.15 = (f32[136,128]{1,0:T(8,128)S(1)}, f32[136,128]{1,0:T(8,128)S(1)}, u32[]{:S(2)}, u32[]{:S(2)}) collective-permute-start(f32[136,128]{1,0:T(8,128)S(1)} %fusion.1), channel_id=1, source_target_pairs={{0,16},{8,24},{16,0},{24,8},{1,17},{9,25},{17,1},{25,9},{2,18},{10... | collective-permute-start | bytes 208904 | tf_op jit(solution)/shard_map/ppermute | solution.py:443
  50.0 0.7 %collective-permute-start.16 = (f32[136,128]{1,0:T(8,128)S(1)}, f32[136,128]{1,0:T(8,128)S(1)}, u32[]{:S(2)}, u32[]{:S(2)}) collective-permute-start(f32[136,128]{1,0:T(8,128)S(1)} %fusion.1), channel_id=1, source_target_pairs={{0,8},{8,0},{16,24},{24,16},{1,9},{9,1},{17,25},{25,17},{2,10},{10... | collective-permute-start | bytes 208904 | tf_op jit(solution)/shard_map/ppermute | solution.py:443
  50.8 0.1 collective-permute-done.6.mx.refs_1_
  50.9 3.0 %collective-permute-done.7.my.refs_2_ = f32[528,256]{1,0:T(8,128)S(1)} collective-permute-done((f32[528,256]{1,0:T(8,128)S(1)}, f32[528,256]{1,0:T(8,128)S(1)}, u32[]{:S(2)}, u32[]{:S(2)}) %collective-permute-start.7) | collective-permute-done | bytes 540704 | tf_op jit(solution)/shard_map/ppermute | solution.py:443
  53.9 0.1 second_step.1
  54.0 0.6 collective-permute-start.8
  54.6 0.0 collective-permute-start.9
  54.6 0.0 collective-permute-done.14
  54.6 0.1 collective-permute-done.15
  54.7 0.0 collective-permute-done.16
  54.7 2.7 %collective-permute-start.17 = (f32[136,128]{1,0:T(8,128)S(1)}, f32[136,128]{1,0:T(8,128)S(1)}, u32[]{:S(2)}, u32[]{:S(2)}) collective-permute-start(f32[136,128]{1,0:T(8,128)S(1)} %add_add_fusion.refs_8_), channel_id=1, source_target_pairs={{0,4},{1,5},{2,6},{3,7},{4,0},{5,1},{6,2},{7,3},{8,12},{9,13},{10,... | collective-permute-start | bytes 208904 | tf_op jit(solution)/shard_map/ppermute | solution.py:443
  57.3 1.3 %collective-permute-start.18 = (f32[136,128]{1,0:T(8,128)S(1)}, f32[136,128]{1,0:T(8,128)S(1)}, u32[]{:S(2)}, u32[]{:S(2)}) collective-permute-start(f32[136,128]{1,0:T(8,128)S(1)} %add_add_fusion.refs_8_), channel_id=1, source_target_pairs={{0,6},{1,7},{2,4},{3,5},{4,2},{5,3},{6,0},{7,1},{8,14},{9,15},{10,... | collective-permute-start | bytes 208904 | tf_op jit(solution)/shard_map/ppermute | solution.py:443
  58.7 0.2 collective-permute-start.19
  58.9 1.3 %collective-permute-done.17.refs_5_ = f32[136,128]{1,0:T(8,128)S(1)} collective-permute-done((f32[136,128]{1,0:T(8,128)S(1)}, f32[136,128]{1,0:T(8,128)S(1)}, u32[]{:S(2)}, u32[]{:S(2)}) %collective-permute-start.17) | collective-permute-done | bytes 69664 | tf_op jit(solution)/shard_map/ppermute | solution.py:443
  60.2 0.0 collective-permute-start.23
  60.2 3.4 %collective-permute-done.18.refs_6_ = f32[136,128]{1,0:T(8,128)S(1)} collective-permute-done((f32[136,128]{1,0:T(8,128)S(1)}, f32[136,128]{1,0:T(8,128)S(1)}, u32[]{:S(2)}, u32[]{:S(2)}) %collective-permute-start.18) | collective-permute-done | bytes 69664 | tf_op jit(solution)/shard_map/ppermute | solution.py:443
  63.6 0.0 collective-permute-start.20
  63.6 0.1 collective-permute-done.19.refs_7_
  63.7 0.4 collective-permute-start.21
  64.1 0.0 collective-permute-done.23.refs_12_
  64.1 0.1 collective-permute-start.22
  64.2 0.6 collective-permute-done.20.refs_9_
  64.9 0.2 collective-permute-done.21.refs_10_
  65.0 0.4 collective-permute-done.22.refs_11_
  65.4 0.0 collective-permute-done.8.refs_3_
  65.4 0.0 collective-permute-done.9.refs_4_
  65.4 8.4 %finish.1 = (f32[1296,512]{1,0:T(8,128)}, f32[1296,512]{1,0:T(8,128)}) custom-call(f32[672,256]{1,0:T(8,128)S(1)} %get-tuple-element.29.m.refs_0_, f32[528,256]{1,0:T(8,128)S(1)} %collective-permute-done.6.mx.refs_1_, f32[528,256]{1,0:T(8,128)S(1)} %collective-permute-done.7.my.refs_2_, f32[480,256]{1,0:T(8,128)S(1)} %collective-permute-done.8.refs_3_, ...), custom_call_target="tpu_custom_call" | custom-call | tf_op jit(solution)/shard_map/finish/pallas_call | solution.py:421
  (6 shorter events, 0.2 us)
Async XLA Ops:
  7.2 11.9 %collective-permute-start.4 = (f32[336,256]{1,0:T(8,128)S(1)}, f32[336,256]{1,0:T(8,128)S(1)}, u32[]{:S(2)}, u32[]{:S(2)}) collective-permute-start(f32[336,256]{1,0:T(8,128)S(1)} %get-tuple-element.28), channel_id=1, source_target_pairs={{0,16},{8,24},{16,0},{24,8},{1,17},{9,25},{17,1},{25,9},{2,18},{10... | collective-permute-start | bytes 1032200 | tf_op jit(solution)/shard_map/ppermute | solution.py:443
  10.2 11.0 %collective-permute-start.2 = (f32[336,256]{1,0:T(8,128)S(1)}, f32[336,256]{1,0:T(8,128)S(1)}, u32[]{:S(2)}, u32[]{:S(2)}) collective-permute-start(f32[336,256]{1,0:T(8,128)S(1)} %get-tuple-element.26), channel_id=1, source_target_pairs={{0,8},{8,0},{16,24},{24,16},{1,9},{9,1},{17,25},{25,17},{2,10},{10... | collective-permute-start | bytes 1032200 | tf_op jit(solution)/shard_map/ppermute | solution.py:443
  14.8 13.7 %collective-permute-start = (f32[336,256]{1,0:T(8,128)S(1)}, f32[336,256]{1,0:T(8,128)S(1)}, u32[]{:S(2)}, u32[]{:S(2)}) collective-permute-start(f32[336,256]{1,0:T(8,128)S(1)} %get-tuple-element.23), channel_id=1, source_target_pairs={{0,8},{8,0},{16,24},{24,16},{1,9},{9,1},{17,25},{25,17},{2,10},{10... | collective-permute-start | bytes 1032200 | tf_op jit(solution)/shard_map/ppermute | solution.py:443
  15.5 13.1 %collective-permute-start.1 = (f32[336,256]{1,0:T(8,128)S(1)}, f32[336,256]{1,0:T(8,128)S(1)}, u32[]{:S(2)}, u32[]{:S(2)}) collective-permute-start(f32[336,256]{1,0:T(8,128)S(1)} %get-tuple-element.24), channel_id=1, source_target_pairs={{0,16},{8,24},{16,0},{24,8},{1,17},{9,25},{17,1},{25,9},{2,18},{10... | collective-permute-start | bytes 1032200 | tf_op jit(solution)/shard_map/ppermute | solution.py:443
  19.1 15.3 %collective-permute-start.5 = (f32[336,256]{1,0:T(8,128)S(1)}, f32[336,256]{1,0:T(8,128)S(1)}, u32[]{:S(2)}, u32[]{:S(2)}) collective-permute-start(f32[336,256]{1,0:T(8,128)S(1)} %add.28), channel_id=1, source_target_pairs={{0,8},{8,0},{16,24},{24,16},{1,9},{9,1},{17,25},{25,17},{2,10},{10... | collective-permute-start | bytes 1032200 | tf_op jit(solution)/shard_map/ppermute | solution.py:443
  21.3 4.6 %copy-start = (f32[1296,512]{1,0:T(8,128)S(1)}, f32[1296,512]{1,0:T(8,128)}, u32[]{:S(2)}) copy-start(f32[1296,512]{1,0:T(8,128)} %m_ref.1) | copy-start | bytes 7962628
  21.3 13.2 %collective-permute-start.3 = (f32[336,256]{1,0:T(8,128)S(1)}, f32[336,256]{1,0:T(8,128)S(1)}, u32[]{:S(2)}, u32[]{:S(2)}) collective-permute-start(f32[336,256]{1,0:T(8,128)S(1)} %add.27), channel_id=1, source_target_pairs={{0,16},{8,24},{16,0},{24,8},{1,17},{9,25},{17,1},{25,9},{2,18},{10... | collective-permute-start | bytes 1032200 | tf_op jit(solution)/shard_map/ppermute | solution.py:443
  35.7 2.1 %collective-permute-start.10 = (f32[4,136,128]{2,1,0:T(8,128)S(1)}, f32[4,136,128]{2,1,0:T(8,128)S(1)}, u32[]{:S(2)}, u32[]{:S(2)}) collective-permute-start(f32[4,136,128]{2,1,0:T(8,128)S(1)} %get-tuple-element.35), channel_id=1, source_target_pairs={{0,1},{1,0},{2,3},{3,2},{4,5},{5,4},{6,7},{7,6},{8,9},{9,8},{10,11... | collective-permute-start | bytes 835592 | tf_op jit(solution)/shard_map/ppermute | solution.py:443
  35.8 15.1 %collective-permute-start.6 = (f32[528,256]{1,0:T(8,128)S(1)}, f32[528,256]{1,0:T(8,128)S(1)}, u32[]{:S(2)}, u32[]{:S(2)}) collective-permute-start(f32[528,256]{1,0:T(8,128)S(1)} %get-tuple-element.30), channel_id=1, source_target_pairs={{0,8},{8,0},{16,24},{24,16},{1,9},{9,1},{17,25},{25,17},{2,10},{10... | collective-permute-start | bytes 1622024 | tf_op jit(solution)/shard_map/ppermute | solution.py:443
  37.3 16.6 %collective-permute-start.7 = (f32[528,256]{1,0:T(8,128)S(1)}, f32[528,256]{1,0:T(8,128)S(1)}, u32[]{:S(2)}, u32[]{:S(2)}) collective-permute-start(f32[528,256]{1,0:T(8,128)S(1)} %get-tuple-element.31), channel_id=1, source_target_pairs={{0,16},{8,24},{16,0},{24,8},{1,17},{9,25},{17,1},{25,9},{2,18},{10... | collective-permute-start | bytes 1622024 | tf_op jit(solution)/shard_map/ppermute | solution.py:443
  37.9 7.8 %collective-permute-start.11 = (f32[136,128]{1,0:T(8,128)S(1)}, f32[136,128]{1,0:T(8,128)S(1)}, u32[]{:S(2)}, u32[]{:S(2)}) collective-permute-start(f32[136,128]{1,0:T(8,128)S(1)} %get-tuple-element.38), channel_id=1, source_target_pairs={{0,4},{1,5},{2,6},{3,7},{4,0},{5,1},{6,2},{7,3},{8,12},{9,13},{10,... | collective-permute-start | bytes 208904 | tf_op jit(solution)/shard_map/ppermute | solution.py:443
  40.5 6.4 %collective-permute-start.12 = (f32[136,128]{1,0:T(8,128)S(1)}, f32[136,128]{1,0:T(8,128)S(1)}, u32[]{:S(2)}, u32[]{:S(2)}) collective-permute-start(f32[136,128]{1,0:T(8,128)S(1)} %get-tuple-element.36), channel_id=1, source_target_pairs={{0,6},{1,7},{2,4},{3,5},{4,2},{5,3},{6,0},{7,1},{8,14},{9,15},{10,... | collective-permute-start | bytes 208904 | tf_op jit(solution)/shard_map/ppermute | solution.py:443
  41.9 5.3 %collective-permute-start.13 = (f32[136,128]{1,0:T(8,128)S(1)}, f32[136,128]{1,0:T(8,128)S(1)}, u32[]{:S(2)}, u32[]{:S(2)}) collective-permute-start(f32[136,128]{1,0:T(8,128)S(1)} %get-tuple-element.37), channel_id=1, source_target_pairs={{0,2},{1,3},{2,0},{3,1},{4,6},{5,7},{6,4},{7,5},{8,10},{9,11},{10,... | collective-permute-start | bytes 208904 | tf_op jit(solution)/shard_map/ppermute | solution.py:443
  47.2 7.3 %collective-permute-start.14 = (f32[136,128]{1,0:T(8,128)S(1)}, f32[136,128]{1,0:T(8,128)S(1)}, u32[]{:S(2)}, u32[]{:S(2)}) collective-permute-start(f32[136,128]{1,0:T(8,128)S(1)} %fusion.1), channel_id=1, source_target_pairs={{0,24},{8,16},{16,8},{24,0},{1,25},{9,17},{17,9},{25,1},{2,26},{10... | collective-permute-start | bytes 208904 | tf_op jit(solution)/shard_map/ppermute | solution.py:443
  48.8 5.9 %collective-permute-start.15 = (f32[136,128]{1,0:T(8,128)S(1)}, f32[136,128]{1,0:T(8,128)S(1)}, u32[]{:S(2)}, u32[]{:S(2)}) collective-permute-start(f32[136,128]{1,0:T(8,128)S(1)} %fusion.1), channel_id=1, source_target_pairs={{0,16},{8,24},{16,0},{24,8},{1,17},{9,25},{17,1},{25,9},{2,18},{10... | collective-permute-start | bytes 208904 | tf_op jit(solution)/shard_map/ppermute | solution.py:443
  50.0 4.6 %collective-permute-start.16 = (f32[136,128]{1,0:T(8,128)S(1)}, f32[136,128]{1,0:T(8,128)S(1)}, u32[]{:S(2)}, u32[]{:S(2)}) collective-permute-start(f32[136,128]{1,0:T(8,128)S(1)} %fusion.1), channel_id=1, source_target_pairs={{0,8},{8,0},{16,24},{24,16},{1,9},{9,1},{17,25},{25,17},{2,10},{10... | collective-permute-start | bytes 208904 | tf_op jit(solution)/shard_map/ppermute | solution.py:443
  54.0 11.4 %collective-permute-start.8 = (f32[480,256]{1,0:T(8,128)S(1)}, f32[480,256]{1,0:T(8,128)S(1)}, u32[]{:S(2)}, u32[]{:S(2)}) collective-permute-start(f32[480,256]{1,0:T(8,128)S(1)} %get-tuple-element.32), channel_id=1, source_target_pairs={{0,8},{8,0},{16,24},{24,16},{1,9},{9,1},{17,25},{25,17},{2,10},{10... | collective-permute-start | bytes 1474568 | tf_op jit(solution)/shard_map/ppermute | solution.py:443
  54.6 10.8 %collective-permute-start.9 = (f32[480,256]{1,0:T(8,128)S(1)}, f32[480,256]{1,0:T(8,128)S(1)}, u32[]{:S(2)}, u32[]{:S(2)}) collective-permute-start(f32[480,256]{1,0:T(8,128)S(1)} %get-tuple-element.33), channel_id=1, source_target_pairs={{0,16},{8,24},{16,0},{24,8},{1,17},{9,25},{17,1},{25,9},{2,18},{10... | collective-permute-start | bytes 1474568 | tf_op jit(solution)/shard_map/ppermute | solution.py:443
  54.7 5.5 %collective-permute-start.17 = (f32[136,128]{1,0:T(8,128)S(1)}, f32[136,128]{1,0:T(8,128)S(1)}, u32[]{:S(2)}, u32[]{:S(2)}) collective-permute-start(f32[136,128]{1,0:T(8,128)S(1)} %add_add_fusion.refs_8_), channel_id=1, source_target_pairs={{0,4},{1,5},{2,6},{3,7},{4,0},{5,1},{6,2},{7,3},{8,12},{9,13},{10,... | collective-permute-start | bytes 208904 | tf_op jit(solution)/shard_map/ppermute | solution.py:443
  57.3 6.3 %collective-permute-start.18 = (f32[136,128]{1,0:T(8,128)S(1)}, f32[136,128]{1,0:T(8,128)S(1)}, u32[]{:S(2)}, u32[]{:S(2)}) collective-permute-start(f32[136,128]{1,0:T(8,128)S(1)} %add_add_fusion.refs_8_), channel_id=1, source_target_pairs={{0,6},{1,7},{2,4},{3,5},{4,2},{5,3},{6,0},{7,1},{8,14},{9,15},{10,... | collective-permute-start | bytes 208904 | tf_op jit(solution)/shard_map/ppermute | solution.py:443
  58.7 5.1 %collective-permute-start.19 = (f32[136,128]{1,0:T(8,128)S(1)}, f32[136,128]{1,0:T(8,128)S(1)}, u32[]{:S(2)}, u32[]{:S(2)}) collective-permute-start(f32[136,128]{1,0:T(8,128)S(1)} %add_add_fusion.refs_8_), channel_id=1, source_target_pairs={{0,2},{1,3},{2,0},{3,1},{4,6},{5,7},{6,4},{7,5},{8,10},{9,11},{10,... | collective-permute-start | bytes 208904 | tf_op jit(solution)/shard_map/ppermute | solution.py:443
  60.2 3.9 %collective-permute-start.23 = (f32[136,128]{1,0:T(8,128)S(1)}, f32[136,128]{1,0:T(8,128)S(1)}, u32[]{:S(2)}, u32[]{:S(2)}) collective-permute-start(f32[136,128]{1,0:T(8,128)S(1)} %add_add_fusion.refs_8_), channel_id=1, source_target_pairs={{0,1},{1,0},{2,3},{3,2},{4,5},{5,4},{6,7},{7,6},{8,9},{9,8},{10,11... | collective-permute-start | bytes 208904 | tf_op jit(solution)/shard_map/ppermute | solution.py:443
  63.6 1.3 %collective-permute-start.20 = (f32[136,128]{1,0:T(8,128)S(1)}, f32[136,128]{1,0:T(8,128)S(1)}, u32[]{:S(2)}, u32[]{:S(2)}) collective-permute-start(f32[136,128]{1,0:T(8,128)S(1)} %collective-permute-done.17.refs_5_), channel_id=1, source_target_pairs={{0,1},{1,0},{2,3},{3,2},{4,5},{5,4},{6,7},{7,6},{8,9},{9,8},{10,11... | collective-permute-start | bytes 208904 | tf_op jit(solution)/shard_map/ppermute | solution.py:443
  63.7 1.3 %collective-permute-start.21 = (f32[136,128]{1,0:T(8,128)S(1)}, f32[136,128]{1,0:T(8,128)S(1)}, u32[]{:S(2)}, u32[]{:S(2)}) collective-permute-start(f32[136,128]{1,0:T(8,128)S(1)} %collective-permute-done.18.refs_6_), channel_id=1, source_target_pairs={{0,1},{1,0},{2,3},{3,2},{4,5},{5,4},{6,7},{7,6},{8,9},{9,8},{10,11... | collective-permute-start | bytes 208904 | tf_op jit(solution)/shard_map/ppermute | solution.py:443
  64.1 1.3 %collective-permute-start.22 = (f32[136,128]{1,0:T(8,128)S(1)}, f32[136,128]{1,0:T(8,128)S(1)}, u32[]{:S(2)}, u32[]{:S(2)}) collective-permute-start(f32[136,128]{1,0:T(8,128)S(1)} %collective-permute-done.19.refs_7_), channel_id=1, source_target_pairs={{0,1},{1,0},{2,3},{3,2},{4,5},{5,4},{6,7},{7,6},{8,9},{9,8},{10,11... | collective-permute-start | bytes 208904 | tf_op jit(solution)/shard_map/ppermute | solution.py:443

commit v8 on v7

--- a/solution.py
+++ b/solution.py
@@ -68,24 +68,26 @@
             v[r0 : r0 + 16, LANE * j : LANE * j + LANE] = jnp.where(lane < 64, part[0], part[1])
 
 
-def conv_part(d, half, taps, cp, qs, cot, v, outs):
+def conv_part(steps, half, taps, cp, qs, cot, v, outs):
     vox = HW * HW
     for c in range(2):
-        lhs = []
-        for q in qs[c]:
-            for i in range(taps):
-                t = jnp.minimum(q * taps + i, TAPS - 1)
-                kd, kh, kw = t // 9, t // 3 % 3, t % 3
-                r0 = pl.multiple_of(((d + kd) * 3 + kw) * cp, 16)
-                lhs.append(v[pl.ds(r0, cp), pl.ds(pl.multiple_of(LANE * kh, LANE), 16 * LANE)])
-        rhs = []
-        for h in range(16):
-            for s1 in range(2):
-                for s0 in range(2):
-                    r0 = (d + half * s1) * vox + (h + 16 * s0) * HW
-                    rhs.append(cot[r0 : r0 + HW, 256 * c : 256 * c + 256])
-        part = jnp.dot(jnp.concatenate(lhs, 0), jnp.concatenate(rhs, 0), preferred_element_type=F32)
-        if d == 0:
+        lhs, rhs = [], []
+        for d in steps:
+            rows = []
+            for q in qs[c]:
+                for i in range(taps):
+                    t = jnp.minimum(q * taps + i, TAPS - 1)
+                    kd, kh, kw = t // 9, t // 3 % 3, t % 3
+                    r0 = pl.multiple_of(((d + kd) * 3 + kw) * cp, 16)
+                    rows.append(v[pl.ds(r0, cp), pl.ds(pl.multiple_of(LANE * kh, LANE), 16 * LANE)])
+            lhs.append(jnp.concatenate(rows, 0))
+            for h in range(16):
+                for s1 in range(2):
+                    for s0 in range(2):
+                        r0 = (d + half * s1) * vox + (h + 16 * s0) * HW
+                        rhs.append(cot[r0 : r0 + HW, 256 * c : 256 * c + 256])
+        part = jnp.dot(jnp.concatenate(lhs, 1), jnp.concatenate(rhs, 0), preferred_element_type=F32)
+        if steps[0] == 0:
             outs[c][...] = part
         else:
             outs[c][...] += part
@@ -117,10 +119,12 @@
         for d0 in range(half + 2):
             build_slab(d0, half, g, xs, tail, v, cp)
     qs = chunks()
-    for d in range(half):
-        for s1 in range(2):
-            copies[d + half * s1].wait()
-        conv_part(d, half, taps, cp, qs, cot, v, outs)
+    for d in range(0, half, 2):
+        steps = list(range(d, min(d + 2, half)))
+        for n in steps:
+            for s1 in range(2):
+                copies[n + half * s1].wait()
+        conv_part(steps, half, taps, cp, qs, cot, v, outs)
 
 
 def conv(x, cot, chunks, slots, taps):
@@ -145,8 +149,9 @@
 
 def more_kernel(depth, cp, taps, chunks, cot, v, *outs):
     qs = chunks()
-    for d in range(depth // 2):
-        conv_part(d, depth // 2, taps, cp, qs, cot, v, outs)
+    half = depth // 2
+    for d in range(0, half, 2):
+        conv_part(list(range(d, min(d + 2, half))), half, taps, cp, qs, cot, v, outs)
 
 
 def conv_more(cot, v, chunks, slots, taps, cp):

time: 74.1 us -> 74.5 us (level)
  no operation moved by 1% of the time
where the time goes in v8:
time: 74.5 us; the launch traced here: 74.4 us
  Pallas kernels  26.5 us (36%)
  starting transfers between devices  24.1 us (32%)
  waiting for transfers between devices  22.7 us (30%)
  between operations  0.9 us (1%)
    ppermute x24, starting transfers between devices, swap(): return lax.ppermute(x, axis, [(i, i ^ bit) for i in range(size)])  24.1 us
    ppermute x24, waiting for transfers between devices, swap(): return lax.ppermute(x, axis, [(i, i ^ bit) for i in range(size)])  22.7 us
    pallas_call x3, Pallas kernels, conv_more(): pl.pallas_call(functools.partial(more_kernel, depth, cp, taps, chunks), o...  9.3 us
    pallas_call x1, Pallas kernels, finish(): pl.pallas_call(functools.partial(finish_kernel, taps, cp, chans, known, l...  8.36 us
    pallas_call x1, Pallas kernels, conv(): pl.pallas_call(functools.partial(conv_kernel, depth, cp, taps, chunks), o...  7.01 us
  transfers between devices with their start and end apart: 24, of which 15 were waited for; matrix products, arithmetic and copies ran while one was open for 0% of the time, Pallas kernels for 13%

profile of v8, /device:TPU:0, one launch (start us, length us, event | category | flops | bytes accessed | tf_op | source)
XLA Modules:
  0.0 74.4 jit_solution(16408838783731523827)
XLA Ops:
  0.6 7.0 %conv_first.1 = (f32[336,256]{1,0:T(8,128)S(1)}, f32[336,256]{1,0:T(8,128)S(1)}, bf16[8192,512]{1,0:T(8,128)(2,1)S(1)}, bf16[864,2304]{1,0:T(8,128)(2,1)S(1)}) custom-call(bf16[48,11560]{1,0:T(8,128)(2,1)} %x_hbm.1, bf16[8192,512]{1,0:T(8,128)(2,1)} %cot_hbm.1), custom_call_target="tpu_custom_call" | custom-call | tf_op jit(solution)/shard_map/conv_first/pallas_call | solution.py:133
  7.6 3.0 %collective-permute-start.4 = (f32[336,256]{1,0:T(8,128)S(1)}, f32[336,256]{1,0:T(8,128)S(1)}, u32[]{:S(2)}, u32[]{:S(2)}) collective-permute-start(f32[336,256]{1,0:T(8,128)S(1)} %get-tuple-element.28), channel_id=1, source_target_pairs={{0,16},{8,24},{16,0},{24,8},{1,17},{9,25},{17,1},{25,9},{2,18},{10... | collective-permute-start | bytes 1032200 | tf_op jit(solution)/shard_map/ppermute | solution.py:448
  10.7 1.5 %collective-permute-start.2 = (f32[336,256]{1,0:T(8,128)S(1)}, f32[336,256]{1,0:T(8,128)S(1)}, u32[]{:S(2)}, u32[]{:S(2)}) collective-permute-start(f32[336,256]{1,0:T(8,128)S(1)} %get-tuple-element.26), channel_id=1, source_target_pairs={{0,8},{8,0},{16,24},{24,16},{1,9},{9,1},{17,25},{25,17},{2,10},{10... | collective-permute-start | bytes 1032200 | tf_op jit(solution)/shard_map/ppermute | solution.py:448
  12.2 3.1 %conv_more.4 = (f32[336,256]{1,0:T(8,128)S(1)}, f32[336,256]{1,0:T(8,128)S(1)}) custom-call(bf16[8192,512]{1,0:T(8,128)(2,1)S(1)} %get-tuple-element.19.cot, bf16[864,2304]{1,0:T(8,128)(2,1)S(1)} %get-tuple-element.20.v), custom_call_target="tpu_custom_call" | custom-call | tf_op jit(solution)/shard_map/conv_more/pallas_call | solution.py:159
  15.3 0.7 collective-permute-start
  16.0 0.0 collective-permute-start.1
  16.0 3.1 %conv_more.5 = (f32[336,256]{1,0:T(8,128)S(1)}, f32[336,256]{1,0:T(8,128)S(1)}) custom-call(bf16[8192,512]{1,0:T(8,128)(2,1)S(1)} %get-tuple-element.19.cot, bf16[864,2304]{1,0:T(8,128)(2,1)S(1)} %get-tuple-element.20.v), custom_call_target="tpu_custom_call" | custom-call | tf_op jit(solution)/shard_map/conv_more/pallas_call | solution.py:159
  19.1 0.4 collective-permute-done.4
  19.6 2.1 %collective-permute-start.5 = (f32[336,256]{1,0:T(8,128)S(1)}, f32[336,256]{1,0:T(8,128)S(1)}, u32[]{:S(2)}, u32[]{:S(2)}) collective-permute-start(f32[336,256]{1,0:T(8,128)S(1)} %add.28), channel_id=1, source_target_pairs={{0,8},{8,0},{16,24},{24,16},{1,9},{9,1},{17,25},{25,17},{2,10},{10... | collective-permute-start | bytes 1032200 | tf_op jit(solution)/shard_map/ppermute | solution.py:448
  21.7 0.0 collective-permute-done.2
  21.7 0.0 copy-start
  21.8 1.6 %collective-permute-start.3 = (f32[336,256]{1,0:T(8,128)S(1)}, f32[336,256]{1,0:T(8,128)S(1)}, u32[]{:S(2)}, u32[]{:S(2)}) collective-permute-start(f32[336,256]{1,0:T(8,128)S(1)} %add.27), channel_id=1, source_target_pairs={{0,16},{8,24},{16,0},{24,8},{1,17},{9,25},{17,1},{25,9},{2,18},{10... | collective-permute-start | bytes 1032200 | tf_op jit(solution)/shard_map/ppermute | solution.py:448
  23.3 3.0 %conv_more.3 = (f32[336,256]{1,0:T(8,128)S(1)}, f32[336,256]{1,0:T(8,128)S(1)}) custom-call(bf16[8192,512]{1,0:T(8,128)(2,1)S(1)} %get-tuple-element.19.cot, bf16[864,2304]{1,0:T(8,128)(2,1)S(1)} %get-tuple-element.20.v), custom_call_target="tpu_custom_call" | custom-call | tf_op jit(solution)/shard_map/conv_more/pallas_call | solution.py:159
  26.4 0.0 copy-done
  26.4 0.6 own_momentum.1.m_ref
  27.0 2.1 %collective-permute-done.refs_2_ = f32[336,256]{1,0:T(8,128)S(1)} collective-permute-done((f32[336,256]{1,0:T(8,128)S(1)}, f32[336,256]{1,0:T(8,128)S(1)}, u32[]{:S(2)}, u32[]{:S(2)}) %collective-permute-start) | collective-permute-done | bytes 344096 | tf_op jit(solution)/shard_map/ppermute | solution.py:448
  29.0 0.0 collective-permute-done.1.refs_3_
  29.0 5.9 %collective-permute-done.5.refs_5_ = f32[336,256]{1,0:T(8,128)S(1)} collective-permute-done((f32[336,256]{1,0:T(8,128)S(1)}, f32[336,256]{1,0:T(8,128)S(1)}, u32[]{:S(2)}, u32[]{:S(2)}) %collective-permute-start.5) | collective-permute-done | bytes 344096 | tf_op jit(solution)/shard_map/ppermute | solution.py:448
  34.9 0.0 collective-permute-done.3.refs_4_
  34.9 1.2 %momentum_gram.1 = (f32[672,256]{1,0:T(8,128)S(1)}, f32[528,256]{1,0:T(8,128)S(1)}, f32[528,256]{1,0:T(8,128)S(1)}, f32[4,136,128]{2,1,0:T(8,128)S(1)}, f32[4,136,128]{2,1,0:T(8,128)S(1)}) custom-call(f32[336,512]{1,0:T(8,128)S(1)} %own_momentum.1.m_ref, f32[336,256]{1,0:T(8,128)S(1)} %get-tuple-element.21.refs_0_, ...), custom_call_target="tpu_custom_call" | custom-call | tf_op jit(solution)/shard_map/momentum_gram/pallas_call | solution.py:269
  36.1 0.1 collective-permute-start.10
  36.2 1.6 %collective-permute-start.6 = (f32[528,256]{1,0:T(8,128)S(1)}, f32[528,256]{1,0:T(8,128)S(1)}, u32[]{:S(2)}, u32[]{:S(2)}) collective-permute-start(f32[528,256]{1,0:T(8,128)S(1)} %get-tuple-element.30), channel_id=1, source_target_pairs={{0,8},{8,0},{16,24},{24,16},{1,9},{9,1},{17,25},{25,17},{2,10},{10... | collective-permute-start | bytes 1622024 | tf_op jit(solution)/shard_map/ppermute | solution.py:448
  37.8 0.5 collective-permute-start.7
  38.3 0.0 collective-permute-done.10
  38.3 2.7 %collective-permute-start.11 = (f32[136,128]{1,0:T(8,128)S(1)}, f32[136,128]{1,0:T(8,128)S(1)}, u32[]{:S(2)}, u32[]{:S(2)}) collective-permute-start(f32[136,128]{1,0:T(8,128)S(1)} %get-tuple-element.38), channel_id=1, source_target_pairs={{0,4},{1,5},{2,6},{3,7},{4,0},{5,1},{6,2},{7,3},{8,12},{9,13},{10,... | collective-permute-start | bytes 208904 | tf_op jit(solution)/shard_map/ppermute | solution.py:448
  41.0 1.3 %collective-permute-start.12 = (f32[136,128]{1,0:T(8,128)S(1)}, f32[136,128]{1,0:T(8,128)S(1)}, u32[]{:S(2)}, u32[]{:S(2)}) collective-permute-start(f32[136,128]{1,0:T(8,128)S(1)} %get-tuple-element.36), channel_id=1, source_target_pairs={{0,6},{1,7},{2,4},{3,5},{4,2},{5,3},{6,0},{7,1},{8,14},{9,15},{10,... | collective-permute-start | bytes 208904 | tf_op jit(solution)/shard_map/ppermute | solution.py:448
  42.3 0.2 collective-permute-start.13
  42.6 3.6 %collective-permute-done.11 = f32[136,128]{1,0:T(8,128)S(1)} collective-permute-done((f32[136,128]{1,0:T(8,128)S(1)}, f32[136,128]{1,0:T(8,128)S(1)}, u32[]{:S(2)}, u32[]{:S(2)}) %collective-permute-start.11) | collective-permute-done | bytes 69664 | tf_op jit(solution)/shard_map/ppermute | solution.py:448
  46.2 1.2 %collective-permute-done.12 = f32[136,128]{1,0:T(8,128)S(1)} collective-permute-done((f32[136,128]{1,0:T(8,128)S(1)}, f32[136,128]{1,0:T(8,128)S(1)}, u32[]{:S(2)}, u32[]{:S(2)}) %collective-permute-start.12) | collective-permute-done | bytes 69664 | tf_op jit(solution)/shard_map/ppermute | solution.py:448
  47.4 0.3 collective-permute-done.13
  47.7 1.6 %collective-permute-start.14 = (f32[136,128]{1,0:T(8,128)S(1)}, f32[136,128]{1,0:T(8,128)S(1)}, u32[]{:S(2)}, u32[]{:S(2)}) collective-permute-start(f32[136,128]{1,0:T(8,128)S(1)} %fusion.1), channel_id=1, source_target_pairs={{0,24},{8,16},{16,8},{24,0},{1,25},{9,17},{17,9},{25,1},{2,26},{10... | collective-permute-start | bytes 208904 | tf_op jit(solution)/shard_map/ppermute | solution.py:448
  49.3 1.2 %collective-permute-start.15 = (f32[136,128]{1,0:T(8,128)S(1)}, f32[136,128]{1,0:T(8,128)S(1)}, u32[]{:S(2)}, u32[]{:S(2)}) collective-permute-start(f32[136,128]{1,0:T(8,128)S(1)} %fusion.1), channel_id=1, source_target_pairs={{0,16},{8,24},{16,0},{24,8},{1,17},{9,25},{17,1},{25,9},{2,18},{10... | collective-permute-start | bytes 208904 | tf_op jit(solution)/shard_map/ppermute | solution.py:448
  50.5 0.7 collective-permute-start.16
  51.3 0.1 collective-permute-done.6.mx.refs_1_
  51.4 3.0 %collective-permute-done.7.my.refs_2_ = f32[528,256]{1,0:T(8,128)S(1)} collective-permute-done((f32[528,256]{1,0:T(8,128)S(1)}, f32[528,256]{1,0:T(8,128)S(1)}, u32[]{:S(2)}, u32[]{:S(2)}) %collective-permute-start.7) | collective-permute-done | bytes 540704 | tf_op jit(solution)/shard_map/ppermute | solution.py:448
  54.4 0.1 second_step.1
  54.4 0.6 collective-permute-start.8
  55.0 0.0 collective-permute-start.9
  55.0 0.0 collective-permute-done.14
  55.0 0.1 collective-permute-done.15
  55.1 0.0 collective-permute-done.16
  55.2 2.7 %collective-permute-start.17 = (f32[136,128]{1,0:T(8,128)S(1)}, f32[136,128]{1,0:T(8,128)S(1)}, u32[]{:S(2)}, u32[]{:S(2)}) collective-permute-start(f32[136,128]{1,0:T(8,128)S(1)} %add_add_fusion.refs_8_), channel_id=1, source_target_pairs={{0,4},{1,5},{2,6},{3,7},{4,0},{5,1},{6,2},{7,3},{8,12},{9,13},{10,... | collective-permute-start | bytes 208904 | tf_op jit(solution)/shard_map/ppermute | solution.py:448
  57.8 1.3 %collective-permute-start.18 = (f32[136,128]{1,0:T(8,128)S(1)}, f32[136,128]{1,0:T(8,128)S(1)}, u32[]{:S(2)}, u32[]{:S(2)}) collective-permute-start(f32[136,128]{1,0:T(8,128)S(1)} %add_add_fusion.refs_8_), channel_id=1, source_target_pairs={{0,6},{1,7},{2,4},{3,5},{4,2},{5,3},{6,0},{7,1},{8,14},{9,15},{10,... | collective-permute-start | bytes 208904 | tf_op jit(solution)/shard_map/ppermute | solution.py:448
  59.1 0.2 collective-permute-start.19
  59.4 1.3 %collective-permute-done.17.refs_5_ = f32[136,128]{1,0:T(8,128)S(1)} collective-permute-done((f32[136,128]{1,0:T(8,128)S(1)}, f32[136,128]{1,0:T(8,128)S(1)}, u32[]{:S(2)}, u32[]{:S(2)}) %collective-permute-start.17) | collective-permute-done | bytes 69664 | tf_op jit(solution)/shard_map/ppermute | solution.py:448
  60.7 0.0 collective-permute-start.23
  60.7 3.4 %collective-permute-done.18.refs_6_ = f32[136,128]{1,0:T(8,128)S(1)} collective-permute-done((f32[136,128]{1,0:T(8,128)S(1)}, f32[136,128]{1,0:T(8,128)S(1)}, u32[]{:S(2)}, u32[]{:S(2)}) %collective-permute-start.18) | collective-permute-done | bytes 69664 | tf_op jit(solution)/shard_map/ppermute | solution.py:448
  64.1 0.0 collective-permute-start.20
  64.1 0.1 collective-permute-done.19.refs_7_
  64.2 0.4 collective-permute-start.21
  64.6 0.0 collective-permute-done.23.refs_12_
  64.6 0.1 collective-permute-start.22
  64.7 0.6 collective-permute-done.20.refs_9_
  65.3 0.2 collective-permute-done.21.refs_10_
  65.5 0.4 collective-permute-done.22.refs_11_
  65.9 0.0 collective-permute-done.8.refs_3_
  65.9 0.0 collective-permute-done.9.refs_4_
  65.9 8.4 %finish.1 = (f32[1296,512]{1,0:T(8,128)}, f32[1296,512]{1,0:T(8,128)}) custom-call(f32[672,256]{1,0:T(8,128)S(1)} %get-tuple-element.29.m.refs_0_, f32[528,256]{1,0:T(8,128)S(1)} %collective-permute-done.6.mx.refs_1_, f32[528,256]{1,0:T(8,128)S(1)} %collective-permute-done.7.my.refs_2_, f32[480,256]{1,0:T(8,128)S(1)} %collective-permute-done.8.refs_3_, ...), custom_call_target="tpu_custom_call" | custom-call | tf_op jit(solution)/shard_map/finish/pallas_call | solution.py:426
  (6 shorter events, 0.2 us)
Async XLA Ops:
  7.6 11.9 %collective-permute-start.4 = (f32[336,256]{1,0:T(8,128)S(1)}, f32[336,256]{1,0:T(8,128)S(1)}, u32[]{:S(2)}, u32[]{:S(2)}) collective-permute-start(f32[336,256]{1,0:T(8,128)S(1)} %get-tuple-element.28), channel_id=1, source_target_pairs={{0,16},{8,24},{16,0},{24,8},{1,17},{9,25},{17,1},{25,9},{2,18},{10... | collective-permute-start | bytes 1032200 | tf_op jit(solution)/shard_map/ppermute | solution.py:448
  10.7 11.0 %collective-permute-start.2 = (f32[336,256]{1,0:T(8,128)S(1)}, f32[336,256]{1,0:T(8,128)S(1)}, u32[]{:S(2)}, u32[]{:S(2)}) collective-permute-start(f32[336,256]{1,0:T(8,128)S(1)} %get-tuple-element.26), channel_id=1, source_target_pairs={{0,8},{8,0},{16,24},{24,16},{1,9},{9,1},{17,25},{25,17},{2,10},{10... | collective-permute-start | bytes 1032200 | tf_op jit(solution)/shard_map/ppermute | solution.py:448
  15.3 13.7 %collective-permute-start = (f32[336,256]{1,0:T(8,128)S(1)}, f32[336,256]{1,0:T(8,128)S(1)}, u32[]{:S(2)}, u32[]{:S(2)}) collective-permute-start(f32[336,256]{1,0:T(8,128)S(1)} %get-tuple-element.23), channel_id=1, source_target_pairs={{0,8},{8,0},{16,24},{24,16},{1,9},{9,1},{17,25},{25,17},{2,10},{10... | collective-permute-start | bytes 1032200 | tf_op jit(solution)/shard_map/ppermute | solution.py:448
  16.0 13.1 %collective-permute-start.1 = (f32[336,256]{1,0:T(8,128)S(1)}, f32[336,256]{1,0:T(8,128)S(1)}, u32[]{:S(2)}, u32[]{:S(2)}) collective-permute-start(f32[336,256]{1,0:T(8,128)S(1)} %get-tuple-element.24), channel_id=1, source_target_pairs={{0,16},{8,24},{16,0},{24,8},{1,17},{9,25},{17,1},{25,9},{2,18},{10... | collective-permute-start | bytes 1032200 | tf_op jit(solution)/shard_map/ppermute | solution.py:448
  19.6 15.3 %collective-permute-start.5 = (f32[336,256]{1,0:T(8,128)S(1)}, f32[336,256]{1,0:T(8,128)S(1)}, u32[]{:S(2)}, u32[]{:S(2)}) collective-permute-start(f32[336,256]{1,0:T(8,128)S(1)} %add.28), channel_id=1, source_target_pairs={{0,8},{8,0},{16,24},{24,16},{1,9},{9,1},{17,25},{25,17},{2,10},{10... | collective-permute-start | bytes 1032200 | tf_op jit(solution)/shard_map/ppermute | solution.py:448
  21.7 4.6 %copy-start = (f32[1296,512]{1,0:T(8,128)S(1)}, f32[1296,512]{1,0:T(8,128)}, u32[]{:S(2)}) copy-start(f32[1296,512]{1,0:T(8,128)} %m_ref.1) | copy-start | bytes 7962628
  21.8 13.2 %collective-permute-start.3 = (f32[336,256]{1,0:T(8,128)S(1)}, f32[336,256]{1,0:T(8,128)S(1)}, u32[]{:S(2)}, u32[]{:S(2)}) collective-permute-start(f32[336,256]{1,0:T(8,128)S(1)} %add.27), channel_id=1, source_target_pairs={{0,16},{8,24},{16,0},{24,8},{1,17},{9,25},{17,1},{25,9},{2,18},{10... | collective-permute-start | bytes 1032200 | tf_op jit(solution)/shard_map/ppermute | solution.py:448
  36.1 2.1 %collective-permute-start.10 = (f32[4,136,128]{2,1,0:T(8,128)S(1)}, f32[4,136,128]{2,1,0:T(8,128)S(1)}, u32[]{:S(2)}, u32[]{:S(2)}) collective-permute-start(f32[4,136,128]{2,1,0:T(8,128)S(1)} %get-tuple-element.35), channel_id=1, source_target_pairs={{0,1},{1,0},{2,3},{3,2},{4,5},{5,4},{6,7},{7,6},{8,9},{9,8},{10,11... | collective-permute-start | bytes 835592 | tf_op jit(solution)/shard_map/ppermute | solution.py:448
  36.2 15.1 %collective-permute-start.6 = (f32[528,256]{1,0:T(8,128)S(1)}, f32[528,256]{1,0:T(8,128)S(1)}, u32[]{:S(2)}, u32[]{:S(2)}) collective-permute-start(f32[528,256]{1,0:T(8,128)S(1)} %get-tuple-element.30), channel_id=1, source_target_pairs={{0,8},{8,0},{16,24},{24,16},{1,9},{9,1},{17,25},{25,17},{2,10},{10... | collective-permute-start | bytes 1622024 | tf_op jit(solution)/shard_map/ppermute | solution.py:448
  37.8 16.6 %collective-permute-start.7 = (f32[528,256]{1,0:T(8,128)S(1)}, f32[528,256]{1,0:T(8,128)S(1)}, u32[]{:S(2)}, u32[]{:S(2)}) collective-permute-start(f32[528,256]{1,0:T(8,128)S(1)} %get-tuple-element.31), channel_id=1, source_target_pairs={{0,16},{8,24},{16,0},{24,8},{1,17},{9,25},{17,1},{25,9},{2,18},{10... | collective-permute-start | bytes 1622024 | tf_op jit(solution)/shard_map/ppermute | solution.py:448
  38.3 7.8 %collective-permute-start.11 = (f32[136,128]{1,0:T(8,128)S(1)}, f32[136,128]{1,0:T(8,128)S(1)}, u32[]{:S(2)}, u32[]{:S(2)}) collective-permute-start(f32[136,128]{1,0:T(8,128)S(1)} %get-tuple-element.38), channel_id=1, source_target_pairs={{0,4},{1,5},{2,6},{3,7},{4,0},{5,1},{6,2},{7,3},{8,12},{9,13},{10,... | collective-permute-start | bytes 208904 | tf_op jit(solution)/shard_map/ppermute | solution.py:448
  41.0 6.4 %collective-permute-start.12 = (f32[136,128]{1,0:T(8,128)S(1)}, f32[136,128]{1,0:T(8,128)S(1)}, u32[]{:S(2)}, u32[]{:S(2)}) collective-permute-start(f32[136,128]{1,0:T(8,128)S(1)} %get-tuple-element.36), channel_id=1, source_target_pairs={{0,6},{1,7},{2,4},{3,5},{4,2},{5,3},{6,0},{7,1},{8,14},{9,15},{10,... | collective-permute-start | bytes 208904 | tf_op jit(solution)/shard_map/ppermute | solution.py:448
  42.3 5.3 %collective-permute-start.13 = (f32[136,128]{1,0:T(8,128)S(1)}, f32[136,128]{1,0:T(8,128)S(1)}, u32[]{:S(2)}, u32[]{:S(2)}) collective-permute-start(f32[136,128]{1,0:T(8,128)S(1)} %get-tuple-element.37), channel_id=1, source_target_pairs={{0,2},{1,3},{2,0},{3,1},{4,6},{5,7},{6,4},{7,5},{8,10},{9,11},{10,... | collective-permute-start | bytes 208904 | tf_op jit(solution)/shard_map/ppermute | solution.py:448
  47.7 7.3 %collective-permute-start.14 = (f32[136,128]{1,0:T(8,128)S(1)}, f32[136,128]{1,0:T(8,128)S(1)}, u32[]{:S(2)}, u32[]{:S(2)}) collective-permute-start(f32[136,128]{1,0:T(8,128)S(1)} %fusion.1), channel_id=1, source_target_pairs={{0,24},{8,16},{16,8},{24,0},{1,25},{9,17},{17,9},{25,1},{2,26},{10... | collective-permute-start | bytes 208904 | tf_op jit(solution)/shard_map/ppermute | solution.py:448
  49.3 5.9 %collective-permute-start.15 = (f32[136,128]{1,0:T(8,128)S(1)}, f32[136,128]{1,0:T(8,128)S(1)}, u32[]{:S(2)}, u32[]{:S(2)}) collective-permute-start(f32[136,128]{1,0:T(8,128)S(1)} %fusion.1), channel_id=1, source_target_pairs={{0,16},{8,24},{16,0},{24,8},{1,17},{9,25},{17,1},{25,9},{2,18},{10... | collective-permute-start | bytes 208904 | tf_op jit(solution)/shard_map/ppermute | solution.py:448
  50.5 4.6 %collective-permute-start.16 = (f32[136,128]{1,0:T(8,128)S(1)}, f32[136,128]{1,0:T(8,128)S(1)}, u32[]{:S(2)}, u32[]{:S(2)}) collective-permute-start(f32[136,128]{1,0:T(8,128)S(1)} %fusion.1), channel_id=1, source_target_pairs={{0,8},{8,0},{16,24},{24,16},{1,9},{9,1},{17,25},{25,17},{2,10},{10... | collective-permute-start | bytes 208904 | tf_op jit(solution)/shard_map/ppermute | solution.py:448
  54.4 11.4 %collective-permute-start.8 = (f32[480,256]{1,0:T(8,128)S(1)}, f32[480,256]{1,0:T(8,128)S(1)}, u32[]{:S(2)}, u32[]{:S(2)}) collective-permute-start(f32[480,256]{1,0:T(8,128)S(1)} %get-tuple-element.32), channel_id=1, source_target_pairs={{0,8},{8,0},{16,24},{24,16},{1,9},{9,1},{17,25},{25,17},{2,10},{10... | collective-permute-start | bytes 1474568 | tf_op jit(solution)/shard_map/ppermute | solution.py:448
  55.0 10.8 %collective-permute-start.9 = (f32[480,256]{1,0:T(8,128)S(1)}, f32[480,256]{1,0:T(8,128)S(1)}, u32[]{:S(2)}, u32[]{:S(2)}) collective-permute-start(f32[480,256]{1,0:T(8,128)S(1)} %get-tuple-element.33), channel_id=1, source_target_pairs={{0,16},{8,24},{16,0},{24,8},{1,17},{9,25},{17,1},{25,9},{2,18},{10... | collective-permute-start | bytes 1474568 | tf_op jit(solution)/shard_map/ppermute | solution.py:448
  55.2 5.5 %collective-permute-start.17 = (f32[136,128]{1,0:T(8,128)S(1)}, f32[136,128]{1,0:T(8,128)S(1)}, u32[]{:S(2)}, u32[]{:S(2)}) collective-permute-start(f32[136,128]{1,0:T(8,128)S(1)} %add_add_fusion.refs_8_), channel_id=1, source_target_pairs={{0,4},{1,5},{2,6},{3,7},{4,0},{5,1},{6,2},{7,3},{8,12},{9,13},{10,... | collective-permute-start | bytes 208904 | tf_op jit(solution)/shard_map/ppermute | solution.py:448
  57.8 6.3 %collective-permute-start.18 = (f32[136,128]{1,0:T(8,128)S(1)}, f32[136,128]{1,0:T(8,128)S(1)}, u32[]{:S(2)}, u32[]{:S(2)}) collective-permute-start(f32[136,128]{1,0:T(8,128)S(1)} %add_add_fusion.refs_8_), channel_id=1, source_target_pairs={{0,6},{1,7},{2,4},{3,5},{4,2},{5,3},{6,0},{7,1},{8,14},{9,15},{10,... | collective-permute-start | bytes 208904 | tf_op jit(solution)/shard_map/ppermute | solution.py:448
  59.1 5.1 %collective-permute-start.19 = (f32[136,128]{1,0:T(8,128)S(1)}, f32[136,128]{1,0:T(8,128)S(1)}, u32[]{:S(2)}, u32[]{:S(2)}) collective-permute-start(f32[136,128]{1,0:T(8,128)S(1)} %add_add_fusion.refs_8_), channel_id=1, source_target_pairs={{0,2},{1,3},{2,0},{3,1},{4,6},{5,7},{6,4},{7,5},{8,10},{9,11},{10,... | collective-permute-start | bytes 208904 | tf_op jit(solution)/shard_map/ppermute | solution.py:448
  60.7 3.9 %collective-permute-start.23 = (f32[136,128]{1,0:T(8,128)S(1)}, f32[136,128]{1,0:T(8,128)S(1)}, u32[]{:S(2)}, u32[]{:S(2)}) collective-permute-start(f32[136,128]{1,0:T(8,128)S(1)} %add_add_fusion.refs_8_), channel_id=1, source_target_pairs={{0,1},{1,0},{2,3},{3,2},{4,5},{5,4},{6,7},{7,6},{8,9},{9,8},{10,11... | collective-permute-start | bytes 208904 | tf_op jit(solution)/shard_map/ppermute | solution.py:448
  64.1 1.3 %collective-permute-start.20 = (f32[136,128]{1,0:T(8,128)S(1)}, f32[136,128]{1,0:T(8,128)S(1)}, u32[]{:S(2)}, u32[]{:S(2)}) collective-permute-start(f32[136,128]{1,0:T(8,128)S(1)} %collective-permute-done.17.refs_5_), channel_id=1, source_target_pairs={{0,1},{1,0},{2,3},{3,2},{4,5},{5,4},{6,7},{7,6},{8,9},{9,8},{10,11... | collective-permute-start | bytes 208904 | tf_op jit(solution)/shard_map/ppermute | solution.py:448
  64.2 1.3 %collective-permute-start.21 = (f32[136,128]{1,0:T(8,128)S(1)}, f32[136,128]{1,0:T(8,128)S(1)}, u32[]{:S(2)}, u32[]{:S(2)}) collective-permute-start(f32[136,128]{1,0:T(8,128)S(1)} %collective-permute-done.18.refs_6_), channel_id=1, source_target_pairs={{0,1},{1,0},{2,3},{3,2},{4,5},{5,4},{6,7},{7,6},{8,9},{9,8},{10,11... | collective-permute-start | bytes 208904 | tf_op jit(solution)/shard_map/ppermute | solution.py:448
  64.6 1.3 %collective-permute-start.22 = (f32[136,128]{1,0:T(8,128)S(1)}, f32[136,128]{1,0:T(8,128)S(1)}, u32[]{:S(2)}, u32[]{:S(2)}) collective-permute-start(f32[136,128]{1,0:T(8,128)S(1)} %collective-permute-done.19.refs_7_), channel_id=1, source_target_pairs={{0,1},{1,0},{2,3},{3,2},{4,5},{5,4},{6,7},{7,6},{8,9},{9,8},{10,11... | collective-permute-start | bytes 208904 | tf_op jit(solution)/shard_map/ppermute | solution.py:448
